TPU v7x, 32 devices: a whole 2x2x4 slice. The times are simulated.
32 devices in a mesh: dp: 8 (over y, x, core), seq: 4 (over z).
Axes of the slice: x: 2, y: 2, z: 4, core: 2. Of those that a mesh axis runs over, the one named last changes fastest.
Arguments:
- inputs: bfloat16 [8, 1024, 1024], P('dp', 'seq'), may hold values from -6 to 6
- cotangent: bfloat16 [8, 1024, 1024], P('dp', 'seq'), may hold values from -6 to 6
- query_proj: bfloat16 [1024, 1024], P(('dp', 'seq')), may hold values from -0.1875 to 0.1875
- key_proj: bfloat16 [1024, 1024], P(('dp', 'seq')), may hold values from -0.1875 to 0.1875
- value_proj: bfloat16 [1024, 2048], P(('dp', 'seq')), may hold values from -0.1875 to 0.1875
- gate_proj: bfloat16 [1024, 2048], P(('dp', 'seq')), may hold values from -0.1875 to 0.1875
- rate_proj: bfloat16 [1024, 16], P(('dp', 'seq')), may hold values from -0.1875 to 0.1875
- output_proj: bfloat16 [2048, 1024], P(('dp', 'seq')), may hold values from -0.125 to 0.125
- ffn_gate: bfloat16 [1024, 2816], P(('dp', 'seq')), may hold values from -0.1875 to 0.1875
- ffn_up: bfloat16 [1024, 2816], P(('dp', 'seq')), may hold values from -0.1875 to 0.1875
- ffn_down: bfloat16 [2816, 1024], P(('dp', 'seq')), may hold values from -0.109375 to 0.109375
- mixer_gain: float32 [1024], replicated, may hold values from 0.5 to 1.5
- ffn_gain: float32 [1024], replicated, may hold values from 0.5 to 1.5
- query_filter: float32 [4, 1024], replicated, may hold values from -3 to 3
- key_filter: float32 [4, 1024], replicated, may hold values from -3 to 3
- value_filter: float32 [4, 2048], replicated, may hold values from -3 to 3
- decay_log: float32 [8], replicated, may hold values from 0 to 2.7
- step_bias: float32 [8], replicated, may hold values from -6 to -3
- head_gain: float32 [256], replicated, may hold values from 0.5 to 1.5
Outputs:
- block_out: bfloat16 [8, 1024, 1024], P('dp', 'seq')
- grad_inputs: bfloat16 [8, 1024, 1024], P('dp', 'seq')
- grad_query: bfloat16 [1024, 1024], P(('dp', 'seq'))
- grad_key: bfloat16 [1024, 1024], P(('dp', 'seq'))
- grad_value: bfloat16 [1024, 2048], P(('dp', 'seq'))
- grad_gate: bfloat16 [1024, 2048], P(('dp', 'seq'))
- grad_rate: bfloat16 [1024, 16], P(('dp', 'seq'))
- grad_output: bfloat16 [2048, 1024], P(('dp', 'seq'))
- grad_ffngate: bfloat16 [1024, 2816], P(('dp', 'seq'))
- grad_ffnup: bfloat16 [1024, 2816], P(('dp', 'seq'))
- grad_ffndown: bfloat16 [2816, 1024], P(('dp', 'seq'))
- grad_mixgain: bfloat16 [1024], replicated
- grad_ffngain: bfloat16 [1024], replicated
- grad_qfilter: bfloat16 [4, 1024], replicated
- grad_kfilter: bfloat16 [4, 1024], replicated
- grad_vfilter: bfloat16 [4, 2048], replicated
- grad_decay: bfloat16 [8], replicated
- grad_stepbias: bfloat16 [8], replicated
- grad_headgain: bfloat16 [256], replicated
All inputs are finite; a program needn't handle non-finite values.
Results may differ from a plain program's by a relative error of at most 0.019.
Values may be sent and summed in bfloat16 or wider, within the bound.
No kernel may reach another device: no remote copies, remote signals or barrier semaphores. Data moves between devices by JAX's collectives and lax.ppermute only.
A program may use at most 112 MiB of HBM per device.

v0:
```python
import jax
import jax.numpy as jnp
from jax import lax
from jax.sharding import PartitionSpec as P

H = 8
DK = 128
DV = 256
BLOCK = 64


precise = lax.Precision.HIGHEST


def rms_scale(values, gain):
    return values * lax.rsqrt(jnp.mean(values * values, axis=-1, keepdims=True) + 1e-05) * gain


def swiglu(hidden_gate, hidden_up):
    return jax.nn.silu(hidden_gate) * hidden_up


def causal_conv(series, filters):
    taps_count = filters.shape[0]
    length_here = series.shape[1]
    padded = jnp.pad(series, ((0, 0), (taps_count - 1, 0), (0, 0), (0, 0)))
    summed = padded[:, 0:length_here] * filters[0]
    for offset in range(1, taps_count):
        summed = summed + padded[:, offset : offset + length_here] * filters[offset]
    return jax.nn.silu(summed)


def to_blocks(series):
    shaped = series.reshape(
        (series.shape[0], series.shape[1] // BLOCK, BLOCK, series.shape[2]) + series.shape[3:]
    )
    return jnp.swapaxes(jnp.moveaxis(shaped, 1, 0), 2, 3)


def from_blocks(blocked):
    moved = jnp.moveaxis(jnp.swapaxes(blocked, 2, 3), 0, 1)
    return moved.reshape((moved.shape[0], moved.shape[1] * BLOCK, moved.shape[3], moved.shape[4]))


def block_step(memory, blocks_in):
    query_part, key_part, value_part, strength_part, decay_part = blocks_in
    running = jnp.cumsum(decay_part, axis=-1)
    row_ids = lax.broadcasted_iota(jnp.int32, (BLOCK, BLOCK), 0)
    col_ids = lax.broadcasted_iota(jnp.int32, (BLOCK, BLOCK), 1)
    lower = row_ids >= col_ids
    strict = row_ids > col_ids
    spread = jnp.where(lower, running[..., :, None] - running[..., None, :], 0.0)
    decays = jnp.where(lower, jnp.exp(spread), 0.0)
    inner = jnp.einsum("bhid,bhjd->bhij", key_part, key_part, precision=precise)
    coupling = jnp.where(strict, strength_part[..., :, None] * inner * decays, 0.0)
    identity = jnp.eye(BLOCK, dtype=coupling.dtype)
    inverse = identity - coupling
    power = coupling
    reach = 2
    while reach < BLOCK:
        power = jnp.einsum("bhij,bhjk->bhik", power, power, precision=precise)
        inverse = jnp.einsum("bhij,bhjk->bhik", inverse, identity + power, precision=precise)
        reach = reach * 2
    scaling = jnp.exp(running)
    carried = jnp.einsum("bhid,bhdv->bhiv", key_part, memory, precision=precise)
    target = strength_part[..., None] * (value_part - scaling[..., None] * carried)
    update = jnp.einsum("bhij,bhjv->bhiv", inverse, target, precision=precise)
    scores = jnp.einsum("bhid,bhjd->bhij", query_part, key_part, precision=precise) * decays
    output = scaling[..., None] * jnp.einsum(
        "bhid,bhdv->bhiv", query_part, memory, precision=precise
    )
    output = output + jnp.einsum("bhij,bhjv->bhiv", scores, update, precision=precise)
    tail_decay = jnp.exp(running[..., -1:] - running)
    memory = jnp.exp(running[..., -1])[..., None, None] * memory
    memory = memory + jnp.einsum(
        "bhid,bhiv->bhdv", key_part * tail_decay[..., None], update, precision=precise
    )
    return (memory, output)


def mixer(
    query_in,
    key_in,
    value_in,
    gate_in,
    rate_in,
    query_taps,
    key_taps,
    value_taps,
    decay_log,
    step_bias,
    head_gain,
):
    queries = causal_conv(query_in, query_taps)
    keys = causal_conv(key_in, key_taps)
    values = causal_conv(value_in, value_taps)
    queries = (
        queries
        * lax.rsqrt(jnp.sum(queries * queries, axis=-1, keepdims=True) + 1e-06)
        * queries.shape[-1] ** (-0.5)
    )
    keys = keys * lax.rsqrt(jnp.sum(keys * keys, axis=-1, keepdims=True) + 1e-06)
    strength = jax.nn.sigmoid(rate_in[..., 0])
    log_decay = -jnp.exp(decay_log) * jax.nn.softplus(rate_in[..., 1] + step_bias)
    start_state = jnp.zeros(
        (queries.shape[0], queries.shape[2], keys.shape[-1], values.shape[-1]), queries.dtype
    )
    final_state, blocked = lax.scan(
        jax.checkpoint(block_step),
        start_state,
        (
            to_blocks(queries),
            to_blocks(keys),
            to_blocks(values),
            to_blocks(strength),
            to_blocks(log_decay),
        ),
    )
    raw = from_blocks(blocked)
    normal = raw * lax.rsqrt(jnp.mean(raw * raw, axis=-1, keepdims=True) + 1e-05)
    return normal * head_gain * jax.nn.silu(gate_in)


def head_slice(table, first_head, local_heads, channels):
    picked = lax.dynamic_slice_in_dim(table, first_head * channels, local_heads * channels, 1)
    return picked.reshape((table.shape[0], local_heads, channels))


def place_heads(gradient, table, first_head, channels):
    flat = gradient.reshape((table.shape[0], gradient.shape[1] * channels))
    return lax.dynamic_update_slice_in_dim(
        jnp.zeros(table.shape, jnp.float32), flat, first_head * channels, 1
    )


def flat_rows(gradient, device_total):
    return gradient.reshape((device_total * 8, gradient.size // (device_total * 8)))


def shards(
    inputs,
    cotangent,
    query_proj,
    key_proj,
    value_proj,
    gate_proj,
    rate_proj,
    output_proj,
    ffn_gate,
    ffn_up,
    ffn_down,
    mixer_gain,
    ffn_gain,
    query_filter,
    key_filter,
    value_filter,
    decay_log,
    step_bias,
    head_gain,
):
    seq_count, piece_len, model_width = inputs.shape
    token_count = seq_count * piece_len
    local_heads = H // lax.axis_size("seq")
    first_head = lax.axis_index("seq") * local_heads
    device_total = lax.axis_size("dp") * lax.axis_size("seq")
    residual = inputs.astype(jnp.float32)
    normed, first_norm_back = jax.vjp(rms_scale, residual, mixer_gain)
    normed_low = normed.astype(jnp.bfloat16).reshape(token_count, model_width)
    kept_in = (
        lax.all_gather(query_proj, ("dp", "seq"), axis=0, tiled=True),
        lax.all_gather(key_proj, ("dp", "seq"), axis=0, tiled=True),
        lax.all_gather(value_proj, ("dp", "seq"), axis=0, tiled=True),
        lax.all_gather(gate_proj, ("dp", "seq"), axis=0, tiled=True),
        lax.all_gather(rate_proj, ("dp", "seq"), axis=0, tiled=True),
    )
    projected = tuple(
        (jnp.dot(normed_low, weight, preferred_element_type=jnp.float32) for weight in kept_in)
    )
    query_low = projected[0].astype(jnp.bfloat16).reshape(seq_count, piece_len, H, DK)
    key_low = projected[1].astype(jnp.bfloat16).reshape(seq_count, piece_len, H, DK)
    value_low = projected[2].astype(jnp.bfloat16).reshape(seq_count, piece_len, H, DV)
    gate_low = projected[3].astype(jnp.bfloat16).reshape(seq_count, piece_len, H, DV)
    rate_low = projected[4].astype(jnp.bfloat16).reshape(seq_count, piece_len, H, 2)
    query_heads, key_heads, value_heads, gate_heads, rate_heads = (
        lax.all_to_all(query_low, "seq", split_axis=2, concat_axis=1, tiled=True),
        lax.all_to_all(key_low, "seq", split_axis=2, concat_axis=1, tiled=True),
        lax.all_to_all(value_low, "seq", split_axis=2, concat_axis=1, tiled=True),
        lax.all_to_all(gate_low, "seq", split_axis=2, concat_axis=1, tiled=True),
        lax.all_to_all(rate_low, "seq", split_axis=2, concat_axis=1, tiled=True),
    )
    mixed, mixer_back = jax.vjp(
        mixer,
        query_heads.astype(jnp.float32),
        key_heads.astype(jnp.float32),
        value_heads.astype(jnp.float32),
        gate_heads.astype(jnp.float32),
        rate_heads.astype(jnp.float32),
        head_slice(query_filter, first_head, local_heads, DK),
        head_slice(key_filter, first_head, local_heads, DK),
        head_slice(value_filter, first_head, local_heads, DV),
        lax.dynamic_slice_in_dim(decay_log, first_head, local_heads, 0),
        lax.dynamic_slice_in_dim(step_bias, first_head, local_heads, 0),
        head_gain,
    )
    mixed_low = lax.all_to_all(
        mixed.astype(jnp.bfloat16), "seq", split_axis=1, concat_axis=2, tiled=True
    ).reshape(token_count, H * DV)
    out_weight, gate_weight, up_weight, down_weight = (
        lax.all_gather(output_proj, ("dp", "seq"), axis=0, tiled=True),
        lax.all_gather(ffn_gate, ("dp", "seq"), axis=0, tiled=True),
        lax.all_gather(ffn_up, ("dp", "seq"), axis=0, tiled=True),
        lax.all_gather(ffn_down, ("dp", "seq"), axis=0, tiled=True),
    )
    middle = residual.reshape(token_count, model_width) + jnp.dot(
        mixed_low, out_weight, preferred_element_type=jnp.float32
    )
    normed_two, second_norm_back = jax.vjp(rms_scale, middle, ffn_gain)
    second_low = normed_two.astype(jnp.bfloat16)
    hidden_gate = jnp.dot(second_low, gate_weight, preferred_element_type=jnp.float32)
    hidden_up = jnp.dot(second_low, up_weight, preferred_element_type=jnp.float32)
    activated, swiglu_back = jax.vjp(swiglu, hidden_gate, hidden_up)
    active_low = activated.astype(jnp.bfloat16)
    block_out = (
        (middle + jnp.dot(active_low, down_weight, preferred_element_type=jnp.float32))
        .astype(jnp.bfloat16)
        .reshape(inputs.shape)
    )
    cot_low = cotangent.reshape(token_count, model_width)
    back_out, back_gate, back_up, back_down = (
        lax.all_gather(output_proj, ("dp", "seq"), axis=0, tiled=True),
        lax.all_gather(ffn_gate, ("dp", "seq"), axis=0, tiled=True),
        lax.all_gather(ffn_up, ("dp", "seq"), axis=0, tiled=True),
        lax.all_gather(ffn_down, ("dp", "seq"), axis=0, tiled=True),
    )
    adj_act = jnp.einsum("td,fd->tf", cot_low, back_down, preferred_element_type=jnp.float32)
    grad_down = jnp.einsum("tf,td->fd", active_low, cot_low, preferred_element_type=jnp.float32)
    adj_hgate, adj_hup = swiglu_back(adj_act)
    hgate_low = adj_hgate.astype(jnp.bfloat16)
    hup_low = adj_hup.astype(jnp.bfloat16)
    adj_second = jnp.einsum("tf,df->td", hgate_low, back_gate, preferred_element_type=jnp.float32)
    adj_second = adj_second + jnp.einsum(
        "tf,df->td", hup_low, back_up, preferred_element_type=jnp.float32
    )
    grad_ffngate = jnp.einsum(
        "td,tf->df", second_low, hgate_low, preferred_element_type=jnp.float32
    )
    grad_ffnup = jnp.einsum("td,tf->df", second_low, hup_low, preferred_element_type=jnp.float32)
    adj_norm_two, gain_two = second_norm_back(adj_second)
    adj_middle = cot_low.astype(jnp.float32) + adj_norm_two
    attn_low = adj_middle.astype(jnp.bfloat16)
    adj_mixed = (
        jnp.einsum("td,hd->th", attn_low, back_out, preferred_element_type=jnp.float32)
        .astype(jnp.bfloat16)
        .reshape(seq_count, piece_len, H, DV)
    )
    grad_output = jnp.einsum("th,td->hd", mixed_low, attn_low, preferred_element_type=jnp.float32)
    rest_part = (
        lax.psum_scatter(
            flat_rows(grad_output, device_total).astype(jnp.bfloat16),
            "dp",
            scatter_dimension=0,
            tiled=True,
        ).astype(jnp.float32),
        lax.psum_scatter(
            flat_rows(grad_ffngate, device_total).astype(jnp.bfloat16),
            "dp",
            scatter_dimension=0,
            tiled=True,
        ).astype(jnp.float32),
        lax.psum_scatter(
            flat_rows(grad_ffnup, device_total).astype(jnp.bfloat16),
            "dp",
            scatter_dimension=0,
            tiled=True,
        ).astype(jnp.float32),
        lax.psum_scatter(
            flat_rows(grad_down, device_total).astype(jnp.bfloat16),
            "dp",
            scatter_dimension=0,
            tiled=True,
        ).astype(jnp.float32),
    )
    rest_sums = (
        lax.psum_scatter(
            rest_part[0].astype(jnp.bfloat16), "seq", scatter_dimension=0, tiled=True
        ).astype(jnp.float32),
        lax.psum_scatter(
            rest_part[1].astype(jnp.bfloat16), "seq", scatter_dimension=0, tiled=True
        ).astype(jnp.float32),
        lax.psum_scatter(
            rest_part[2].astype(jnp.bfloat16), "seq", scatter_dimension=0, tiled=True
        ).astype(jnp.float32),
        lax.psum_scatter(
            rest_part[3].astype(jnp.bfloat16), "seq", scatter_dimension=0, tiled=True
        ).astype(jnp.float32),
    )
    mixer_grads = mixer_back(
        lax.all_to_all(adj_mixed, "seq", split_axis=2, concat_axis=1, tiled=True).astype(
            jnp.float32
        )
    )
    query_back, key_back, value_back, gate_back, rate_back = (
        lax.all_to_all(
            mixer_grads[0].astype(jnp.bfloat16), "seq", split_axis=1, concat_axis=2, tiled=True
        ),
        lax.all_to_all(
            mixer_grads[1].astype(jnp.bfloat16), "seq", split_axis=1, concat_axis=2, tiled=True
        ),
        lax.all_to_all(
            mixer_grads[2].astype(jnp.bfloat16), "seq", split_axis=1, concat_axis=2, tiled=True
        ),
        lax.all_to_all(
            mixer_grads[3].astype(jnp.bfloat16), "seq", split_axis=1, concat_axis=2, tiled=True
        ),
        lax.all_to_all(
            mixer_grads[4].astype(jnp.bfloat16), "seq", split_axis=1, concat_axis=2, tiled=True
        ),
    )
    rows_back = (
        query_back.reshape(token_count, H * DK),
        key_back.reshape(token_count, H * DK),
        value_back.reshape(token_count, H * DV),
        gate_back.reshape(token_count, H * DV),
        rate_back.reshape(token_count, H * 2),
    )
    pieces = lax.all_gather(
        (query_proj, key_proj, value_proj, gate_proj, rate_proj), ("dp", "seq"), axis=0, tiled=True
    )
    grad_summed = jnp.einsum(
        "tc,dc->td", rows_back[0], pieces[0], preferred_element_type=jnp.float32
    )
    for member in range(1, 5):
        grad_summed = grad_summed + jnp.einsum(
            "tc,dc->td", rows_back[member], pieces[member], preferred_element_type=jnp.float32
        )
    in_grads = tuple(
        (
            flat_rows(
                jnp.einsum("td,tc->dc", normed_low, rows, preferred_element_type=jnp.float32),
                device_total,
            )
            for rows in rows_back
        )
    )
    mixer_part = (
        lax.psum_scatter(
            in_grads[0].astype(jnp.bfloat16), "dp", scatter_dimension=0, tiled=True
        ).astype(jnp.float32),
        lax.psum_scatter(
            in_grads[1].astype(jnp.bfloat16), "dp", scatter_dimension=0, tiled=True
        ).astype(jnp.float32),
        lax.psum_scatter(
            in_grads[2].astype(jnp.bfloat16), "dp", scatter_dimension=0, tiled=True
        ).astype(jnp.float32),
        lax.psum_scatter(
            in_grads[3].astype(jnp.bfloat16), "dp", scatter_dimension=0, tiled=True
        ).astype(jnp.float32),
        lax.psum_scatter(
            in_grads[4].astype(jnp.bfloat16), "dp", scatter_dimension=0, tiled=True
        ).astype(jnp.float32),
    )
    mixer_sums = (
        lax.psum_scatter(
            mixer_part[0].astype(jnp.bfloat16), "seq", scatter_dimension=0, tiled=True
        ).astype(jnp.float32),
        lax.psum_scatter(
            mixer_part[1].astype(jnp.bfloat16), "seq", scatter_dimension=0, tiled=True
        ).astype(jnp.float32),
        lax.psum_scatter(
            mixer_part[2].astype(jnp.bfloat16), "seq", scatter_dimension=0, tiled=True
        ).astype(jnp.float32),
        lax.psum_scatter(
            mixer_part[3].astype(jnp.bfloat16), "seq", scatter_dimension=0, tiled=True
        ).astype(jnp.float32),
        lax.psum_scatter(
            mixer_part[4].astype(jnp.bfloat16), "seq", scatter_dimension=0, tiled=True
        ).astype(jnp.float32),
    )
    adj_first, gain_one = first_norm_back(grad_summed.reshape(inputs.shape))
    grad_inputs = (adj_middle.reshape(inputs.shape) + adj_first).astype(jnp.bfloat16)
    decay_full = lax.dynamic_update_slice_in_dim(
        jnp.zeros(decay_log.shape, jnp.float32), mixer_grads[8], first_head, 0
    )
    step_full = lax.dynamic_update_slice_in_dim(
        jnp.zeros(step_bias.shape, jnp.float32), mixer_grads[9], first_head, 0
    )
    small_sums = lax.psum(
        (
            gain_one,
            gain_two,
            place_heads(mixer_grads[5], query_filter, first_head, DK),
            place_heads(mixer_grads[6], key_filter, first_head, DK),
            place_heads(mixer_grads[7], value_filter, first_head, DV),
            decay_full,
            step_full,
            mixer_grads[10],
        ),
        ("dp", "seq"),
    )
    mixer_shapes = (
        query_proj.shape,
        key_proj.shape,
        value_proj.shape,
        gate_proj.shape,
        rate_proj.shape,
    )
    rest_shapes = (output_proj.shape, ffn_gate.shape, ffn_up.shape, ffn_down.shape)
    mixer_out = tuple(
        (
            summed.reshape(shape).astype(jnp.bfloat16)
            for summed, shape in zip(mixer_sums, mixer_shapes)
        )
    )
    rest_out = tuple(
        (
            summed.reshape(shape).astype(jnp.bfloat16)
            for summed, shape in zip(rest_sums, rest_shapes)
        )
    )
    return (
        block_out,
        grad_inputs,
        mixer_out[0],
        mixer_out[1],
        mixer_out[2],
        mixer_out[3],
        mixer_out[4],
        rest_out[0],
        rest_out[1],
        rest_out[2],
        rest_out[3],
        small_sums[0].astype(jnp.bfloat16),
        small_sums[1].astype(jnp.bfloat16),
        small_sums[2].astype(jnp.bfloat16),
        small_sums[3].astype(jnp.bfloat16),
        small_sums[4].astype(jnp.bfloat16),
        small_sums[5].astype(jnp.bfloat16),
        small_sums[6].astype(jnp.bfloat16),
        small_sums[7].astype(jnp.bfloat16),
    )


def solution(mesh):
    in_specs = (
        P("dp", "seq", None),
        P("dp", "seq", None),
        P(("dp", "seq"), None),
        P(("dp", "seq"), None),
        P(("dp", "seq"), None),
        P(("dp", "seq"), None),
        P(("dp", "seq"), None),
        P(("dp", "seq"), None),
        P(("dp", "seq"), None),
        P(("dp", "seq"), None),
        P(("dp", "seq"), None),
        P(),
        P(),
        P(),
        P(),
        P(),
        P(),
        P(),
        P(),
    )
    out_specs = (
        P("dp", "seq", None),
        P("dp", "seq", None),
        P(("dp", "seq"), None),
        P(("dp", "seq"), None),
        P(("dp", "seq"), None),
        P(("dp", "seq"), None),
        P(("dp", "seq"), None),
        P(("dp", "seq"), None),
        P(("dp", "seq"), None),
        P(("dp", "seq"), None),
        P(("dp", "seq"), None),
        P(),
        P(),
        P(),
        P(),
        P(),
        P(),
        P(),
        P(),
    )
    return jax.shard_map(shards, mesh=mesh, in_specs=in_specs, out_specs=out_specs, check_vma=False)
```

profile of v0, /device:TPU:0, one launch (start us, length us, event | category | flops | bytes accessed | tf_op | source)
XLA Modules:
  0.0 1998.3 jit_solution(5110075347907635718)
XLA Ops:
  11.9 71.4 %all-gather = bf16[32,32,16]{1,2,0:T(8,128)(2,1)S(1)} all-gather(bf16[1,32,16]{1,2,0:T(8,128)(2,1)} %bitcast.1172), channel_id=1, replica_groups=mesh['dp'=8,'seq'=4] {'dp','seq'}, dimensions={0}, use_global_device_ids=true | all-gather | bytes 33792 | tf_op jit(solution)/shard_map/all_gather | solution.py:174
  96.5 5.0 all-to-all-start.1
  103.7 26.5 %all-gather.14.cloned.1.call-done = bf16[1024,1024]{1,0:T(8,128)(2,1)} async-done(((bf16[32,1024]{1,0:T(8,128)(2,1)}), bf16[1024,1024]{1,0:T(8,128)(2,1)}) %all-gather.14.cloned.1.call-update) | async-done | bytes 2097168 | tf_op jit(solution)/shard_map/all_gather | solution.py:170
  138.6 60.0 %all-gather.12.cloned.1.call-done = bf16[1024,2048]{1,0:T(8,128)(2,1)} async-done(((bf16[32,2048]{1,0:T(8,128)(2,1)}), bf16[1024,2048]{1,0:T(8,128)(2,1)}) %all-gather.12.cloned.1.call-update) | async-done | bytes 4194320 | tf_op jit(solution)/shard_map/all_gather | solution.py:172
  211.9 61.9 %all-gather.16.cloned.1.call-done = bf16[1024,2048]{1,0:T(8,128)(2,1)} async-done(((bf16[32,2048]{1,0:T(8,128)(2,1)}), bf16[1024,2048]{1,0:T(8,128)(2,1)}) %all-gather.16.cloned.1.call-update) | async-done | bytes 4194320 | tf_op jit(solution)/shard_map/all_gather | solution.py:173
  278.9 4.4 all-to-all-start.4
  288.0 178.7 %while.44 = (s32[]{:T(128)}, f32[1,2,128,256]{3,2,1,0:T(8,128)S(1)}, f32[16,1,2,64,256]{4,3,0,2,1:T(8,128)S(1)}, f32[16,1,2,128,256]{4,3,2,1,0:T(8,128)}, f32[16...) while((s32[]{:T(128)}, ...), condition=%wide.region_5.6_spmd.clone.clone, body=%wide.region_3.5_spmd.clone.clone.sunk | while | flops 290127872 | bytes 4267730 | solution.py:108
  471.6 36.4 %all_to_all.144 = bf16[1,1024,2,256]{3,2,0,1:T(2,128)(2,1)S(1)} all-to-all(bf16[1,1024,2,256]{3,2,0,1:T(2,128)(2,1)S(1)} %copy.335), channel_id=1, replica_groups=mesh['dp'=8,'seq'=4] {'seq'}, dimensions={1} | all-to-all | bytes 2097152 | tf_op jit(solution)/shard_map/all_to_all | solution.py:205
  516.5 6.0 fusion.297
  522.5 5.9 fusion.298
  528.4 34.5 %all-gather.24.cloned.1.call-done = bf16[2816,1024]{1,0:T(8,128)(2,1)} async-done(((bf16[88,1024]{1,0:T(8,128)(2,1)}), bf16[2816,1024]{1,0:T(8,128)(2,1)}) %all-gather.24.cloned.1.call-update) | async-done | bytes 5767184 | tf_op jit(solution)/shard_map/all_gather | solution.py:212
  562.9 8.3 multiply_convert_fusion
  571.2 5.4 fusion.299
  586.9 26.4 %all-to-all-done.6 = bf16[1,256,8,256]{3,1,0,2:T(8,128)(2,1)} async-done(((bf16[1,256,8,256]{3,1,0,2:T(8,128)(2,1)}), bf16[1,256,8,256]{3,1,0,2:T(8,128)(2,1)}, u32[]{:S(2)}, u32[]{:S(2)}) %all-to-all-start.6) | async-done | bytes 1048608 | tf_op jit(solution)/shard_map/all_to_all | solution.py:298
  626.1 676.8 %while.43 = (s32[]{:T(128)}, f32[1,2,128,256]{2,3,1,0:T(8,128)}, f32[16,1,2,64,128]{4,3,0,2,1:T(8,128)}, f32[16,1,2,64,128]{4,3,0,2,1:T(8,128)}, f32[16,1,2,64,2...) while((s32[]{:T(128)}, f32[1,2,128,256]{2,3,1,0:T(8,128)}, ...), condition=%wide.region_22.23_spmd.clone, body=%wide.region_10.22_spmd.clone.sunk | while | flops 794755840 | bytes 14484511 | solution.py:108
  1309.4 17.2 all_to_all.145
  1341.0 16.6 all_to_all.146
  1361.9 4.4 convert_element_type.500
  1366.3 4.8 convolution_convert_fusion.3
  1371.1 7.4 convert_element_type.515
  1379.6 5.5 convolution_convert_fusion.2
  1385.1 10.8 convert_element_type.518
  1396.4 5.6 convolution_convert_fusion.1
  1402.0 10.7 convert_element_type.521
  1413.7 5.5 convolution_convert_fusion
  1419.2 12.5 convert_element_type.524
  1437.8 6.4 multiply_reduce_fusion.6
  1447.9 5.0 all-to-all-start.9
  1455.9 21.4 %all-to-all-done.9 = bf16[1,1024,2,256]{3,2,0,1:T(2,128)(2,1)} async-done(((bf16[1,1024,2,256]{3,2,0,1:T(2,128)(2,1)}), bf16[1,1024,2,256]{3,2,0,1:T(2,128)(2,1)}, u32[]{:S(2)}, u32[]{:S(2)}) %all-to-all-start.9) | async-done | bytes 1048608 | tf_op jit(solution)/shard_map/all_to_all | solution.py:309
  1481.9 4.8 convolution_convert_fusion.5
  1486.7 8.1 convert_element_type.506
  1499.3 27.7 %all_to_all.147 = bf16[1,1024,2,256]{3,2,0,1:T(2,128)(2,1)S(1)} all-to-all(bf16[1,1024,2,256]{3,2,0,1:T(2,128)(2,1)S(1)} %copy.362), channel_id=1, replica_groups=mesh['dp'=8,'seq'=4] {'seq'}, dimensions={1} | all-to-all | bytes 2097152 | tf_op jit(solution)/shard_map/all_to_all | solution.py:312
  1531.1 8.0 convert_element_type.509
  1541.8 57.8 %reduce-scatter.44.cloned.1.call-done = bf16[32,11264]{1,0:T(8,128)(2,1)} async-done(((bf16[256,11264]{1,0:T(8,128)(2,1)}), bf16[32,11264]{1,0:T(8,128)(2,1)}) %reduce-scatter.44.cloned.1.call-update) | async-done | bytes 720912 | tf_op jit(solution)/shard_map/reduce_scatter | solution.py:270
  1600.9 61.4 %reduce-scatter.48.cloned.1.call-done = bf16[32,11264]{1,0:T(8,128)(2,1)} async-done(((bf16[256,11264]{1,0:T(8,128)(2,1)}), bf16[32,11264]{1,0:T(8,128)(2,1)}) %reduce-scatter.48.cloned.1.call-update) | async-done | bytes 720912 | tf_op jit(solution)/shard_map/reduce_scatter | solution.py:276
  1662.5 5.6 fusion.231
  1668.8 30.2 %reduce-scatter.34.cloned.1.call-done = bf16[32,64]{1,0:T(8,128)(2,1)} async-done(((bf16[256,64]{1,0:T(8,128)(2,1)}), bf16[32,64]{1,0:T(8,128)(2,1)}) %reduce-scatter.34.cloned.1.call-update) | async-done | bytes 4112 | tf_op jit(solution)/shard_map/reduce_scatter | solution.py:358
  1699.0 11.9 all-reduce.31
  1711.7 42.2 %reduce-scatter.26.cloned.1.call-done = bf16[32,8192]{1,0:T(8,128)(2,1)} async-done(((bf16[256,8192]{1,0:T(8,128)(2,1)}), bf16[32,8192]{1,0:T(8,128)(2,1)}) %reduce-scatter.26.cloned.1.call-update) | async-done | bytes 524304 | tf_op jit(solution)/shard_map/reduce_scatter | solution.py:352
  1757.6 4.6 fusion.301
  1764.6 43.9 %reduce-scatter.30.cloned.1.call-done = bf16[32,8192]{1,0:T(8,128)(2,1)} async-done(((bf16[256,8192]{1,0:T(8,128)(2,1)}), bf16[32,8192]{1,0:T(8,128)(2,1)}) %reduce-scatter.30.cloned.1.call-update) | async-done | bytes 524304 | tf_op jit(solution)/shard_map/reduce_scatter | solution.py:355
  1812.2 41.4 %all-reduce.32 = (bf16[1024]{0:T(1024)(128)(2,1)}, bf16[1024]{0:T(1024)(128)(2,1)}, bf16[4,1024]{1,0:T(4,128)(2,1)}, bf16[4,1024]{1,0:T(4,128)(2,1)}, bf16[4,204...) all-reduce(f32[1024]{0:T(1024)S(1)} %get-tuple-element.831, ...), channel_id=1, replica_groups=mesh['dp'=8,'seq'=4] {'dp','seq'}, use_global_device_ids=true, to_apply=%region_45.46 | all-reduce | flops 18704 | bytes 112224 | tf_op jit(solution)/shard_map/psum | solution.py:387
  1857.8 15.0 reduce-scatter.38.cloned.1.call-done
  1874.4 21.8 %reduce-scatter.42.cloned.1.call-done = bf16[8,11264]{1,0:T(8,128)(2,1)} async-done(((bf16[32,11264]{1,0:T(8,128)(2,1)}), bf16[8,11264]{1,0:T(8,128)(2,1)}) %reduce-scatter.42.cloned.1.call-update) | async-done | bytes 180240 | tf_op jit(solution)/shard_map/reduce_scatter | solution.py:287
  1898.0 22.4 %reduce-scatter.46.cloned.1.call-done = bf16[8,11264]{1,0:T(8,128)(2,1)} async-done(((bf16[32,11264]{1,0:T(8,128)(2,1)}), bf16[8,11264]{1,0:T(8,128)(2,1)}) %reduce-scatter.46.cloned.1.call-update) | async-done | bytes 180240 | tf_op jit(solution)/shard_map/reduce_scatter | solution.py:290
  1922.1 22.5 %reduce-scatter.50.cloned.1.call-done = bf16[8,11264]{1,0:T(8,128)(2,1)} async-done(((bf16[32,11264]{1,0:T(8,128)(2,1)}), bf16[8,11264]{1,0:T(8,128)(2,1)}) %reduce-scatter.50.cloned.1.call-update) | async-done | bytes 180240 | tf_op jit(solution)/shard_map/reduce_scatter | solution.py:293
  1946.4 21.1 %reduce-scatter.28.cloned.1.call-done = bf16[8,8192]{1,0:T(8,128)(2,1)} async-done(((bf16[32,8192]{1,0:T(8,128)(2,1)}), bf16[8,8192]{1,0:T(8,128)(2,1)}) %reduce-scatter.28.cloned.1.call-update) | async-done | bytes 131088 | tf_op jit(solution)/shard_map/reduce_scatter | solution.py:369
  1969.2 20.7 %reduce-scatter.32.cloned.1.call-done = bf16[8,8192]{1,0:T(8,128)(2,1)} async-done(((bf16[32,8192]{1,0:T(8,128)(2,1)}), bf16[8,8192]{1,0:T(8,128)(2,1)}) %reduce-scatter.32.cloned.1.call-update) | async-done | bytes 131088 | tf_op jit(solution)/shard_map/reduce_scatter | solution.py:372
  (2126 shorter events, 1016.1 us)
Async XLA Ops:
  7.2 85.9 %copy-start.2 = (bf16[1,256,1024]{2,1,0:T(8,128)(2,1)S(1)}, bf16[1,256,1024]{2,1,0:T(8,128)(2,1)}, u32[]{:S(2)}) copy-start(bf16[1,256,1024]{2,1,0:T(8,128)(2,1)} %param.23) | copy-start | bytes 1572868
  7.2 85.9 %copy-start.32 = (f32[1024]{0:T(1024)S(1)}, f32[1024]{0:T(1024)}, u32[]{:S(2)}) copy-start(f32[1024]{0:T(1024)} %param.34) | copy-start | bytes 12292
  7.2 84.7 %copy-start.95 = (f32[8]{0:T(128)S(1)}, f32[8]{0:T(128)}, u32[]{:S(2)}) copy-start(f32[8]{0:T(128)} %param.40) | copy-start | bytes 100
  7.2 84.8 %copy-start.90 = (f32[8]{0:T(128)S(1)}, f32[8]{0:T(128)}, u32[]{:S(2)}) copy-start(f32[8]{0:T(128)} %param.39) | copy-start | bytes 100
  7.2 85.9 %all-gather.10.cloned.1.call-start = ((), (), s32[]{:S(2)}) async-start(), calls=%async_computation.29 | async-start | bytes 2162688 | tf_op jit(solution)/shard_map/all_gather | solution.py:171
  8.0 122.2 %all-gather.14.cloned.1.call-start = ((), (), s32[]{:S(2)}) async-start(), calls=%async_computation.31 | async-start | bytes 2162688 | tf_op jit(solution)/shard_map/all_gather | solution.py:170
  8.7 189.9 %all-gather.12.cloned.1.call-start = ((), (), s32[]{:S(2)}) async-start(), calls=%async_computation.30 | async-start | bytes 4325376 | tf_op jit(solution)/shard_map/all_gather | solution.py:172
  9.5 264.4 %all-gather.16.cloned.1.call-start = ((), (), s32[]{:S(2)}) async-start(), calls=%async_computation.32 | async-start | bytes 4325376 | tf_op jit(solution)/shard_map/all_gather | solution.py:173
  10.0 501.4 %all-gather.18.cloned.1.call-start = ((), (), s32[]{:S(2)}) async-start(), calls=%async_computation.33 | async-start | bytes 4325376 | tf_op jit(solution)/shard_map/all_gather | solution.py:209
  10.6 505.9 %all-gather.20.cloned.1.call-start = ((), (), s32[]{:S(2)}) async-start(), calls=%async_computation.34 | async-start | bytes 5947392 | tf_op jit(solution)/shard_map/all_gather | solution.py:210
  11.2 511.3 %all-gather.22.cloned.1.call-start = ((), (), s32[]{:S(2)}) async-start(), calls=%async_computation.35 | async-start | bytes 5947392 | tf_op jit(solution)/shard_map/all_gather | solution.py:211
  84.8 189.1 %copy-start.44 = (f32[256]{0:T(256)}, f32[256]{0:T(256)S(1)}, u32[]{:S(2)}) copy-start(f32[256]{0:T(256)S(1)} %fusion.266) | copy-start | bytes 3076
  86.8 9.7 all-to-all-start
  90.0 472.8 %all-gather.24.cloned.1.call-start = ((), (), s32[]{:S(2)}) async-start(), calls=%async_computation.36 | async-start | bytes 5947392 | tf_op jit(solution)/shard_map/all_gather | solution.py:212
  91.8 191.9 %copy-start.55 = (f32[2,256]{1,0:T(2,128)}, f32[2,256]{1,0:T(2,128)S(1)}, u32[]{:S(2)}) copy-start(f32[2,256]{1,0:T(2,128)S(1)} %mul.1374) | copy-start | bytes 6148
  91.8 191.9 %copy-start.57 = (f32[2,256]{1,0:T(2,128)}, f32[2,256]{1,0:T(2,128)S(1)}, u32[]{:S(2)}) copy-start(f32[2,256]{1,0:T(2,128)S(1)} %mul.1377) | copy-start | bytes 6148
  91.9 191.8 %copy-start.59 = (f32[2,256]{1,0:T(2,128)}, f32[2,256]{1,0:T(2,128)S(1)}, u32[]{:S(2)}) copy-start(f32[2,256]{1,0:T(2,128)S(1)} %mul.1380) | copy-start | bytes 6148
  91.9 191.8 %copy-start.61 = (f32[2,256]{1,0:T(2,128)}, f32[2,256]{1,0:T(2,128)S(1)}, u32[]{:S(2)}) copy-start(f32[2,256]{1,0:T(2,128)S(1)} %mul.1383) | copy-start | bytes 6148
  93.0 115.7 %copy-start.66 = (f32[1,256]{1,0:T(1,128)}, f32[1,256]{1,0:T(1,128)S(1)}, u32[]{:S(2)}) copy-start(f32[1,256]{1,0:T(1,128)S(1)} %get-tuple-element.961) | copy-start | bytes 3076
  93.0 115.7 %copy-start.68 = (f32[1,256]{1,0:T(1,128)}, f32[1,256]{1,0:T(1,128)S(1)}, u32[]{:S(2)}) copy-start(f32[1,256]{1,0:T(1,128)S(1)} %get-tuple-element.962) | copy-start | bytes 3076
  93.0 115.7 %copy-start.70 = (f32[1,256]{1,0:T(1,128)}, f32[1,256]{1,0:T(1,128)S(1)}, u32[]{:S(2)}) copy-start(f32[1,256]{1,0:T(1,128)S(1)} %get-tuple-element.963) | copy-start | bytes 3076
  93.1 115.7 %copy-start.72 = (f32[1,256]{1,0:T(1,128)}, f32[1,256]{1,0:T(1,128)S(1)}, u32[]{:S(2)}) copy-start(f32[1,256]{1,0:T(1,128)S(1)} %get-tuple-element.964) | copy-start | bytes 3076
  96.5 37.1 %all-to-all-start.1 = ((bf16[1,256,8,128]{3,1,0,2:T(8,128)(2,1)}), bf16[1,256,8,128]{3,1,0,2:T(8,128)(2,1)S(1)}, u32[]{:S(2)}, u32[]{:S(2)}) async-start(bf16[1,256,8,128]{3,1,0,2:T(8,128)(2,1)} %copy.317), calls=%async_computation.1 | async-start | bytes 1048576 | tf_op jit(solution)/shard_map/all_to_all | solution.py:186
  133.5 70.1 %all-to-all-start.3 = ((bf16[1,256,8,128]{3,1,0,2:T(8,128)(2,1)}), bf16[1,256,8,128]{3,1,0,2:T(8,128)(2,1)S(1)}, u32[]{:S(2)}, u32[]{:S(2)}) async-start(bf16[1,256,8,128]{3,1,0,2:T(8,128)(2,1)} %copy.323), calls=%async_computation.3 | async-start | bytes 1048576 | tf_op jit(solution)/shard_map/all_to_all | solution.py:185
  203.6 75.2 %all-to-all-start.2 = ((bf16[1,256,8,256]{3,1,0,2:T(8,128)(2,1)}), bf16[1,256,8,256]{3,1,0,2:T(8,128)(2,1)S(1)}, u32[]{:S(2)}, u32[]{:S(2)}) async-start(bf16[1,256,8,256]{3,1,0,2:T(8,128)(2,1)} %copy.320), calls=%async_computation.2 | async-start | bytes 2097152 | tf_op jit(solution)/shard_map/all_to_all | solution.py:187
  278.9 188.3 %all-to-all-start.4 = ((bf16[1,256,8,256]{3,1,0,2:T(8,128)(2,1)}), bf16[1,256,8,256]{3,1,0,2:T(8,128)(2,1)}, u32[]{:S(2)}, u32[]{:S(2)}) async-start(bf16[1,256,8,256]{3,1,0,2:T(8,128)(2,1)} %copy.332), calls=%async_computation.4 | async-start | bytes 2097152 | tf_op jit(solution)/shard_map/all_to_all | solution.py:188
  582.6 30.8 %all-to-all-start.6 = ((bf16[1,256,8,256]{3,1,0,2:T(8,128)(2,1)}), bf16[1,256,8,256]{3,1,0,2:T(8,128)(2,1)}, u32[]{:S(2)}, u32[]{:S(2)}) async-start(bf16[1,256,8,256]{3,1,0,2:T(8,128)(2,1)} %copy.338), calls=%async_computation.6 | async-start | bytes 2097152 | tf_op jit(solution)/shard_map/all_to_all | solution.py:298
  586.9 952.3 %reduce-scatter.22.cloned.1.call-start = ((), (), s32[]{:S(2)}) async-start(), calls=%async_computation.39 | async-start | bytes 2359296 | tf_op jit(solution)/shard_map/reduce_scatter | solution.py:349
  1335.3 204.5 %reduce-scatter.18.cloned.1.call-start = ((), (), s32[]{:S(2)}) async-start(), calls=%async_computation.37 | async-start | bytes 2359296 | tf_op jit(solution)/shard_map/reduce_scatter | solution.py:346
  1366.3 174.2 %reduce-scatter.36.cloned.1.call-start = ((), (), s32[]{:S(2)}) async-start(), calls=%async_computation.46 | async-start | bytes 4718592 | tf_op jit(solution)/shard_map/reduce_scatter | solution.py:258
  1378.6 162.5 %reduce-scatter.40.cloned.1.call-start = ((), (), s32[]{:S(2)}) async-start(), calls=%async_computation.48 | async-start | bytes 6488064 | tf_op jit(solution)/shard_map/reduce_scatter | solution.py:264
  1395.9 203.7 %reduce-scatter.44.cloned.1.call-start = ((), (), s32[]{:S(2)}) async-start(), calls=%async_computation.50 | async-start | bytes 6488064 | tf_op jit(solution)/shard_map/reduce_scatter | solution.py:270
  1412.7 249.7 %reduce-scatter.48.cloned.1.call-start = ((), (), s32[]{:S(2)}) async-start(), calls=%async_computation.52 | async-start | bytes 6488064 | tf_op jit(solution)/shard_map/reduce_scatter | solution.py:276
  1434.5 13.3 all-to-all-start.11
  1447.9 29.4 %all-to-all-start.9 = ((bf16[1,1024,2,256]{3,2,0,1:T(2,128)(2,1)}), bf16[1,1024,2,256]{3,2,0,1:T(2,128)(2,1)}, u32[]{:S(2)}, u32[]{:S(2)}) async-start(bf16[1,1024,2,256]{3,2,0,1:T(2,128)(2,1)} %copy.358), calls=%async_computation.9 | async-start | bytes 2097152 | tf_op jit(solution)/shard_map/all_to_all | solution.py:309
  1452.9 246.1 %reduce-scatter.34.cloned.1.call-start = ((), (), s32[]{:S(2)}) async-start(), calls=%async_computation.45 | async-start | bytes 73728 | tf_op jit(solution)/shard_map/reduce_scatter | solution.py:358
  1455.7 298.3 %reduce-scatter.26.cloned.1.call-start = ((), (), s32[]{:S(2)}) async-start(), calls=%async_computation.41 | async-start | bytes 4718592 | tf_op jit(solution)/shard_map/reduce_scatter | solution.py:352
  1494.9 313.6 %reduce-scatter.30.cloned.1.call-start = ((), (), s32[]{:S(2)}) async-start(), calls=%async_computation.43 | async-start | bytes 4718592 | tf_op jit(solution)/shard_map/reduce_scatter | solution.py:355
  1539.1 123.4 %copy-start.26 = (f32[256,1024]{1,0:T(8,128)S(1)}, f32[256,1024]{1,0:T(8,128)}, u32[]{:S(2)}) copy-start(f32[256,1024]{1,0:T(8,128)} %copy-done.24) | copy-start | bytes 3145732
  1539.1 315.6 %reduce-scatter.24.cloned.1.call-start = ((), (), s32[]{:S(2)}) async-start(), calls=%async_computation.40 | async-start | bytes 327680 | tf_op jit(solution)/shard_map/reduce_scatter | solution.py:366
  1539.7 316.6 %reduce-scatter.20.cloned.1.call-start = ((), (), s32[]{:S(2)}) async-start(), calls=%async_computation.38 | async-start | bytes 327680 | tf_op jit(solution)/shard_map/reduce_scatter | solution.py:363
  1540.5 332.4 %reduce-scatter.38.cloned.1.call-start = ((), (), s32[]{:S(2)}) async-start(), calls=%async_computation.47 | async-start | bytes 655360 | tf_op jit(solution)/shard_map/reduce_scatter | solution.py:284
  1541.0 355.2 %reduce-scatter.42.cloned.1.call-start = ((), (), s32[]{:S(2)}) async-start(), calls=%async_computation.49 | async-start | bytes 901120 | tf_op jit(solution)/shard_map/reduce_scatter | solution.py:287
  1541.8 378.6 %reduce-scatter.46.cloned.1.call-start = ((), (), s32[]{:S(2)}) async-start(), calls=%async_computation.51 | async-start | bytes 901120 | tf_op jit(solution)/shard_map/reduce_scatter | solution.py:290
  1599.6 344.9 %reduce-scatter.50.cloned.1.call-start = ((), (), s32[]{:S(2)}) async-start(), calls=%async_computation.53 | async-start | bytes 901120 | tf_op jit(solution)/shard_map/reduce_scatter | solution.py:293
  1662.4 91.8 %copy-start.19 = (bf16[1,256,4,2,128]{1,4,3,2,0:T(8,128)(2,1)S(1)}, bf16[1,256,4,2,128]{1,4,3,2,0:T(8,128)(2,1)}, u32[]{:S(2)}) copy-start(bf16[1,256,4,2,128]{1,4,3,2,0:T(8,128)(2,1)} %copy-done.18) | copy-start | bytes 1572868
  1662.4 305.1 %reduce-scatter.28.cloned.1.call-start = ((), (), s32[]{:S(2)}) async-start(), calls=%async_computation.42 | async-start | bytes 655360 | tf_op jit(solution)/shard_map/reduce_scatter | solution.py:369
  1754.0 235.9 %reduce-scatter.32.cloned.1.call-start = ((), (), s32[]{:S(2)}) async-start(), calls=%async_computation.44 | async-start | bytes 655360 | tf_op jit(solution)/shard_map/reduce_scatter | solution.py:372
  (157 other events, 998.1 us)
Sparse Core Ops, SparseCore 0:
  11.0 59.3 all-gather.9
  73.3 56.8 all-gather.13
  133.2 65.3 all-gather.11
  201.5 72.3 all-gather.15
  276.7 71.3 all-gather.17
  350.7 66.4 all-gather.19
  420.0 73.8 all-gather.21
  496.8 66.0 all-gather.23
  1335.4 39.3 reduce-scatter.21
  1378.3 41.2 reduce-scatter.17
  1422.9 51.3 reduce-scatter.35
  1478.0 59.0 reduce-scatter.39
  1540.5 59.0 reduce-scatter.43
  1603.3 59.0 reduce-scatter.47
  1665.8 33.1 reduce-scatter.33
  1702.6 51.3 reduce-scatter.25
  1757.2 51.2 reduce-scatter.29
  1810.7 19.6 reduce-scatter.23
  1832.7 18.0 reduce-scatter.19
  1853.0 19.8 reduce-scatter.37
  1875.2 20.9 reduce-scatter.41
  1898.7 21.6 reduce-scatter.45
  1922.8 21.7 reduce-scatter.49
  1946.8 20.7 reduce-scatter.27
  1969.9 19.9 reduce-scatter.31
where the time goes:
time: 2020 us; the launch traced here: 2000 us
  matrix products  633 us (31%)
  waiting for transfers between devices  597 us (30%)
  local copies, waits for them, and re-layouts  294 us (15%)
  blocking collectives  223 us (11%)
  other arithmetic  192 us (10%)
  starting transfers between devices  34 us (2%)
    dot_general x320, matrix products, block_step(): power = jnp.einsum('bhij,bhjk->bhik', power, power, precision=precise)  87.9 us
    dot_general x64, matrix products, block_step(): jnp.einsum('bhid,bhdv->bhiv', query_part, memory, precision=precise)  81.9 us
    dot_general x320, matrix products, block_step(): jnp.einsum('bhij,bhjk->bhik', inverse, identity + power, precision=precise)  74.6 us
    dot_general x64, matrix products, block_step(): carried = jnp.einsum('bhid,bhdv->bhiv', key_part, memory, precision=precise)  71.6 us
    all_gather x1, blocking collectives, shards(): lax.all_gather(rate_proj, ('dp', 'seq'), axis=0, tiled=True)  71.4 us
    dot_general x64, matrix products, block_step(): jnp.einsum('bhid,bhjd->bhij', query_part, key_part, precision=precise)  69 us
    squeeze x80, local copies, waits for them, and re-layouts, mixer(): lax.scan(jax.checkpoint(block_step), start_state, (to_blocks(queries), to...  65.8 us
    all_gather x1, waiting for transfers between devices, shards(): lax.all_gather(gate_proj, ('dp', 'seq'), axis=0, tiled=True)  61.9 us
  transfers between devices with their start and end apart: 33, of which 17 were waited for; matrix products, arithmetic and copies ran while one was open for 20% of the time, Pallas kernels for 0%

commit v1 on v0

v1 whole, which is shorter than its diff:
```python
import functools

import jax
import jax.numpy as jnp
from jax import lax
from jax.experimental import pallas as pl
from jax.experimental.pallas import tpu as pltpu
from jax.sharding import PartitionSpec as P

H = 8
DK = 128
DV = 256


CHUNK = 256
LANES = 128
F32 = jnp.float32
BF16 = jnp.bfloat16


def mm(left, right, left_dim=1, right_dim=0):
    return lax.dot_general(
        left.astype(BF16),
        right.astype(BF16),
        (((left_dim,), (right_dim,)), ((), ())),
        preferred_element_type=F32,
    )


def mm_nt(left, right):
    return mm(left, right, 1, 1)


def mm_tn(left, right):
    return mm(left, right, 0, 0)


def iota(shape, axis):
    return lax.broadcasted_iota(jnp.int32, shape, axis)


def exact_mm(ones, values):
    first = values.astype(BF16)
    rest = values - first.astype(F32)
    second = rest.astype(BF16)
    third = (rest - second.astype(F32)).astype(BF16)
    return mm(ones, first) + mm(ones, second) + mm(ones, third)


def small_inverse(coupling):
    size = coupling.shape[0]
    rows = iota(coupling.shape, 0)
    cols = iota(coupling.shape, 1)
    solved = jnp.where((rows // 2 == cols // 2), -coupling, 0.0)
    width = 2
    while width < size:
        band = (rows // (2 * width) == cols // (2 * width)) & (rows // width != cols // width)
        part = jnp.where(band, coupling, 0.0)
        step = part + mm(part, solved)
        solved = solved - step - mm(solved, step)
        width = 2 * width
    return solved


def lower_inverse(coupling):
    size = coupling.shape[0]
    if size <= LANES:
        return small_inverse(coupling)
    half = size // 2
    head = lower_inverse(coupling[:half, :half])
    tail = lower_inverse(coupling[half:, half:])
    part = coupling[half:, :half]
    step = part + mm(part, head)
    corner = -step - mm(tail, step)
    top = jnp.concatenate([head, jnp.zeros((half, half), F32)], axis=1)
    return jnp.concatenate([top, jnp.concatenate([corner, tail], axis=1)], axis=0)


def silu_slope(values, gate):
    return gate * (1.0 + values * (1.0 - gate))


def softplus(values):
    return jnp.maximum(values, 0.0) + jnp.log1p(jnp.exp(-jnp.abs(values)))


def conv_taps(current, before, first_chunk):
    before = jnp.where(first_chunk, 0.0, before.astype(F32))
    joined = jnp.concatenate([before, current.astype(F32)], axis=0)
    top = before.shape[0]
    rows = current.shape[0]
    return [joined[top - 3 + tap : top - 3 + tap + rows] for tap in range(4)]


def decay_parts(rate, decay_scale, decay_bias):
    rows = rate.shape[0]
    shifted = rate + decay_bias
    log_decay = -decay_scale * softplus(shifted)
    lower = jnp.where(iota((rows, rows), 0) >= iota((rows, rows), 1), 1.0, 0.0)
    running = exact_mm(lower, log_decay)
    return shifted, log_decay, running


def head_parts(summed, running, running_rows, head, heads):
    rows = summed.shape[0]
    gates = jax.nn.sigmoid(summed)
    conv = summed * gates
    q_at, k_at, v_at = head * DK, (heads + head) * DK, 2 * heads * DK + head * DV
    q_conv, k_conv = conv[:, q_at : q_at + DK], conv[:, k_at : k_at + DK]
    value = conv[:, v_at : v_at + DV]
    q_scale = lax.rsqrt(jnp.sum(q_conv * q_conv, axis=1, keepdims=True) + 1e-06)
    k_scale = lax.rsqrt(jnp.sum(k_conv * k_conv, axis=1, keepdims=True) + 1e-06)
    query = q_conv * (q_scale * DK**-0.5)
    key = k_conv * k_scale
    lane = 2 * head + 1
    total = running[:, lane : lane + 1]
    across = running_rows[lane : lane + 1, :]
    lower = iota((rows, rows), 0) >= iota((rows, rows), 1)
    decays = jnp.where(lower, jnp.exp(jnp.minimum(total - across, 0.0)), 0.0)
    last = total[rows - 1 : rows, :]
    return q_conv, k_conv, q_scale, k_scale, query, key, value, total, decays, last


def mixer_forward_kernel(
    current_ref, before_ref, filter_ref, side_ref, gain_ref,
    mixed_ref, solved_ref, update_ref, start_ref, raw_ref, memory_ref, *, heads
):
    chunk = pl.program_id(1)

    @pl.when(chunk == 0)
    def _():
        memory_ref[...] = jnp.zeros(memory_ref.shape, F32)

    conv_width = 2 * heads * DK + heads * DV
    gate_at = conv_width
    rate_at = conv_width + heads * DV
    taps = conv_taps(
        current_ref[0, :, :conv_width], before_ref[0, :, :conv_width], chunk == 0
    )
    rows = taps[0].shape[0]
    summed = taps[0] * filter_ref[0:1, :]
    for tap in range(1, 4):
        summed = summed + taps[tap] * filter_ref[tap : tap + 1, :]
    rate = current_ref[0, :, rate_at : rate_at + LANES].astype(F32)
    strengths = jax.nn.sigmoid(rate)
    shifted, log_decay, running = decay_parts(rate, side_ref[0:1, :], side_ref[1:2, :])
    running_rows = running.T
    strict = iota((rows, rows), 0) > iota((rows, rows), 1)
    for head in range(heads):
        _, _, _, _, query, key, value, total, decays, last = head_parts(
            summed, running, running_rows, head, heads
        )
        strength = strengths[:, 2 * head : 2 * head + 1]
        scaling = jnp.exp(total)
        inner = mm_nt(key, key)
        coupling = jnp.where(strict, strength * inner * decays, 0.0)
        solved = lower_inverse(coupling)
        start = memory_ref[head]
        target = strength * (value - scaling * mm(key, start))
        update = target + mm(solved, target)
        scores = mm_nt(query, key) * decays
        raw = scaling * mm(query, start) + mm(scores, update)
        tail = key * jnp.exp(last - total)
        memory_ref[head] = jnp.exp(last) * start + mm_tn(tail, update)
        start_ref[0, 0, head] = start
        solved_ref[0, 0, head] = solved.astype(BF16)
        at = head * DV
        update_ref[0, :, at : at + DV] = update.astype(BF16)
        raw_ref[0, :, at : at + DV] = raw
        gate = current_ref[0, :, gate_at + at : gate_at + at + DV].astype(F32)
        normal = raw * lax.rsqrt(jnp.mean(raw * raw, axis=1, keepdims=True) + 1e-05)
        mixed_ref[0, :, at : at + DV] = (
            normal * gain_ref[...] * (gate * jax.nn.sigmoid(gate))
        ).astype(BF16)


def mixer_backward_kernel(
    current_ref, before_ref, filter_ref, side_ref, gain_ref,
    adjoint_ref, solved_ref, update_ref, start_ref, raw_ref,
    grad_ref, filter_sum_ref, side_sum_ref, gain_sum_ref, memory_ref, after_ref, *, heads, chunks
):
    step = pl.program_id(1)

    @pl.when(step == 0)
    def _():
        memory_ref[...] = jnp.zeros(memory_ref.shape, F32)
        after_ref[...] = jnp.zeros(after_ref.shape, F32)

    @pl.when((step == 0) & (pl.program_id(0) == 0))
    def _():
        filter_sum_ref[...] = jnp.zeros(filter_sum_ref.shape, F32)
        side_sum_ref[...] = jnp.zeros(side_sum_ref.shape, F32)
        gain_sum_ref[...] = jnp.zeros(gain_sum_ref.shape, F32)

    conv_width = 2 * heads * DK + heads * DV
    gate_at = conv_width
    rate_at = conv_width + heads * DV
    taps = conv_taps(
        current_ref[0, :, :conv_width], before_ref[0, :, :conv_width], step == chunks - 1
    )
    rows = taps[0].shape[0]
    summed = taps[0] * filter_ref[0:1, :]
    for tap in range(1, 4):
        summed = summed + taps[tap] * filter_ref[tap : tap + 1, :]
    rate = current_ref[0, :, rate_at : rate_at + LANES].astype(F32)
    strengths = jax.nn.sigmoid(rate)
    decay_scale = side_ref[0:1, :]
    shifted, log_decay, running = decay_parts(rate, decay_scale, side_ref[1:2, :])
    running_rows = running.T
    strict = iota((rows, rows), 0) > iota((rows, rows), 1)
    lane_ids = iota((rows, LANES), 1)
    row_ids = iota((LANES, rows), 0)
    last_lanes = iota((1, LANES), 1)
    sum_across = jnp.zeros((rows, LANES), F32)
    sum_down = jnp.zeros((LANES, rows), F32)
    sum_last = jnp.zeros((1, LANES), F32)
    adj_strength = jnp.zeros((rows, LANES), F32)
    q_adjoints, k_adjoints, v_adjoints = [], [], []
    for head in range(heads):
        q_conv, k_conv, q_scale, k_scale, query, key, value, total, decays, last = head_parts(
            summed, running, running_rows, head, heads
        )
        strength = strengths[:, 2 * head : 2 * head + 1]
        scaling = jnp.exp(total)
        at = head * DV
        raw = raw_ref[0, :, at : at + DV]
        gate = current_ref[0, :, gate_at + at : gate_at + at + DV].astype(F32)
        gate_sig = jax.nn.sigmoid(gate)
        gate_silu = gate * gate_sig
        adj_mixed = adjoint_ref[0, :, at : at + DV].astype(F32)
        inv = lax.rsqrt(jnp.mean(raw * raw, axis=1, keepdims=True) + 1e-05)
        normal = raw * inv
        upstream = adj_mixed * gain_ref[...] * gate_silu
        adj_raw = inv * (
            upstream - normal * jnp.mean(upstream * normal, axis=1, keepdims=True)
        )
        adj_gate = adj_mixed * normal * gain_ref[...] * silu_slope(gate, gate_sig)
        grad_ref[0, :, gate_at + at : gate_at + at + DV] = adj_gate.astype(BF16)
        gain_sum_ref[...] += jnp.sum(adj_mixed * normal * gate_silu, axis=0, keepdims=True)

        start = start_ref[0, 0, head]
        solved = solved_ref[0, 0, head]
        update = update_ref[0, :, at : at + DV]
        adj_memory = memory_ref[head]
        tail_decay = jnp.exp(last - total)
        last_decay = jnp.exp(last)
        inner = mm_nt(key, key)
        scores = mm_nt(query, key) * decays
        spread = mm(key * tail_decay, adj_memory)
        adj_update = mm_tn(scores, adj_raw) + spread
        adj_target = adj_update + mm_tn(solved, adj_update)
        adj_scores = mm_nt(adj_raw, update)
        adj_coupling = jnp.where(strict, -mm_nt(adj_target, update), 0.0) * decays
        adj_inner = strength * adj_coupling
        from_inner = adj_coupling * inner
        adj_qk = adj_scores * decays
        key_start = mm(key, start)
        query_start = mm(query, start)
        adj_query = scaling * mm_nt(adj_raw, start) + mm(adj_qk, key)
        adj_key = (
            mm_tn(adj_qk, query)
            + tail_decay * mm_nt(update, adj_memory)
            - scaling * strength * mm_nt(adj_target, start)
            + mm(adj_inner, key)
            + mm_tn(adj_inner, key)
        )
        adj_value = strength * adj_target
        strength_sum = jnp.sum(
            adj_target * (value - scaling * key_start), axis=1, keepdims=True
        ) + jnp.sum(from_inner, axis=1, keepdims=True)
        pairs = adj_scores * scores + strength * from_inner
        tail_sum = jnp.sum(spread * update.astype(F32), axis=1, keepdims=True)
        decay_sum = (
            jnp.sum(pairs, axis=1, keepdims=True)
            + scaling * jnp.sum(query_start * adj_raw, axis=1, keepdims=True)
            - scaling * strength * jnp.sum(key_start * adj_target, axis=1, keepdims=True)
            - tail_sum
        )
        at_end = jnp.sum(tail_sum, axis=0, keepdims=True) + last_decay * jnp.sum(
            jnp.sum(start * adj_memory, axis=1, keepdims=True), axis=0, keepdims=True
        )
        lane = 2 * head + 1
        sum_across = sum_across + jnp.where(lane_ids == lane, decay_sum, 0.0)
        sum_down = sum_down + jnp.where(
            row_ids == lane, jnp.sum(pairs, axis=0, keepdims=True), 0.0
        )
        sum_last = sum_last + jnp.where(last_lanes == lane, at_end, 0.0)
        adj_strength = adj_strength + jnp.where(lane_ids == lane - 1, strength_sum, 0.0)
        memory_ref[head] = (
            last_decay * adj_memory
            + mm_tn(query * scaling, adj_raw)
            - mm_tn(key * (scaling * strength), adj_target)
        )
        adj_query = adj_query * DK**-0.5
        q_adjoints.append(
            q_scale * adj_query
            - q_conv
            * (q_scale * q_scale * q_scale * jnp.sum(q_conv * adj_query, axis=1, keepdims=True))
        )
        k_adjoints.append(
            k_scale * adj_key
            - k_conv
            * (k_scale * k_scale * k_scale * jnp.sum(k_conv * adj_key, axis=1, keepdims=True))
        )
        v_adjoints.append(adj_value)

    upper = jnp.where(iota((rows, rows), 0) <= iota((rows, rows), 1), 1.0, 0.0)
    adj_log_decay = exact_mm(upper, sum_across - sum_down.T) + sum_last
    adj_shifted = -adj_log_decay * decay_scale * jax.nn.sigmoid(shifted)
    adj_rate = adj_shifted + adj_strength * strengths * (1.0 - strengths)
    grad_ref[0, :, rate_at : rate_at + LANES] = adj_rate.astype(BF16)
    side_sum_ref[0:1, :] += jnp.sum(adj_log_decay * log_decay, axis=0, keepdims=True)
    side_sum_ref[1:2, :] += jnp.sum(adj_shifted, axis=0, keepdims=True)

    adj_conv = jnp.concatenate(q_adjoints + k_adjoints + v_adjoints, axis=1)
    adj_summed = adj_conv * silu_slope(summed, jax.nn.sigmoid(summed))
    joined = jnp.concatenate([adj_summed, after_ref[...]], axis=0)
    after_ref[...] = adj_summed[0:8]
    adj_pre = adj_summed * filter_ref[3:4, :]
    filter_sum_ref[3:4, :] += jnp.sum(adj_summed * taps[3], axis=0, keepdims=True)
    for tap in range(3):
        adj_pre = adj_pre + joined[3 - tap : 3 - tap + rows] * filter_ref[tap : tap + 1, :]
        filter_sum_ref[tap : tap + 1, :] += jnp.sum(adj_summed * taps[tap], axis=0, keepdims=True)
    grad_ref[0, :, :conv_width] = adj_pre.astype(BF16)


def mixer_sizes(projected, heads):
    seqs, tokens, width = projected.shape
    rows = min(CHUNK, tokens)
    conv_width = 2 * heads * DK + heads * DV
    return seqs, tokens, width, rows, tokens // rows, conv_width


def mixer_forward(projected, filters, side, gain, heads):
    seqs, tokens, width, rows, chunks, conv_width = mixer_sizes(projected, heads)
    ratio = rows // 16
    per_row = lambda s, c: (s, c, 0)
    fixed = lambda s, c: (0, 0)
    per_chunk = lambda s, c: (s, c, 0, 0, 0)
    return pl.pallas_call(
        functools.partial(mixer_forward_kernel, heads=heads),
        grid=(seqs, chunks),
        in_specs=[
            pl.BlockSpec((1, rows, width), per_row),
            pl.BlockSpec((1, 16, width), lambda s, c: (s, jnp.maximum(c * ratio - 1, 0), 0)),
            pl.BlockSpec((4, conv_width), fixed),
            pl.BlockSpec((8, LANES), fixed),
            pl.BlockSpec((1, DV), fixed),
        ],
        out_specs=[
            pl.BlockSpec((1, rows, heads * DV), per_row),
            pl.BlockSpec((1, 1, heads, rows, rows), per_chunk),
            pl.BlockSpec((1, rows, heads * DV), per_row),
            pl.BlockSpec((1, 1, heads, DK, DV), per_chunk),
            pl.BlockSpec((1, rows, heads * DV), per_row),
        ],
        out_shape=[
            jax.ShapeDtypeStruct((seqs, tokens, heads * DV), BF16),
            jax.ShapeDtypeStruct((seqs, chunks, heads, rows, rows), BF16),
            jax.ShapeDtypeStruct((seqs, tokens, heads * DV), BF16),
            jax.ShapeDtypeStruct((seqs, chunks, heads, DK, DV), F32),
            jax.ShapeDtypeStruct((seqs, tokens, heads * DV), F32),
        ],
        scratch_shapes=[pltpu.VMEM((heads, DK, DV), F32)],
        compiler_params=pltpu.CompilerParams(vmem_limit_bytes=48 * 1024 * 1024),
        cost_estimate=pl.CostEstimate(
            flops=seqs * chunks * heads * 30 * 2 * rows**3,
            bytes_accessed=12 * 1024 * 1024,
            transcendentals=seqs * tokens * width,
        ),
        name="mixer_forward",
    )(projected, projected, filters, side, gain)


def mixer_backward(projected, filters, side, gain, adjoint, saved, heads):
    seqs, tokens, width, rows, chunks, conv_width = mixer_sizes(projected, heads)
    ratio = rows // 16
    solved, update, start, raw = saved
    per_row = lambda s, c: (s, chunks - 1 - c, 0)
    fixed = lambda s, c: (0, 0)
    per_chunk = lambda s, c: (s, chunks - 1 - c, 0, 0, 0)
    return pl.pallas_call(
        functools.partial(mixer_backward_kernel, heads=heads, chunks=chunks),
        grid=(seqs, chunks),
        in_specs=[
            pl.BlockSpec((1, rows, width), per_row),
            pl.BlockSpec(
                (1, 16, width),
                lambda s, c: (s, jnp.maximum((chunks - 1 - c) * ratio - 1, 0), 0),
            ),
            pl.BlockSpec((4, conv_width), fixed),
            pl.BlockSpec((8, LANES), fixed),
            pl.BlockSpec((1, DV), fixed),
            pl.BlockSpec((1, rows, heads * DV), per_row),
            pl.BlockSpec((1, 1, heads, rows, rows), per_chunk),
            pl.BlockSpec((1, rows, heads * DV), per_row),
            pl.BlockSpec((1, 1, heads, DK, DV), per_chunk),
            pl.BlockSpec((1, rows, heads * DV), per_row),
        ],
        out_specs=[
            pl.BlockSpec((1, rows, width), per_row),
            pl.BlockSpec((4, conv_width), fixed),
            pl.BlockSpec((8, LANES), fixed),
            pl.BlockSpec((1, DV), fixed),
        ],
        out_shape=[
            jax.ShapeDtypeStruct((seqs, tokens, width), BF16),
            jax.ShapeDtypeStruct((4, conv_width), F32),
            jax.ShapeDtypeStruct((8, LANES), F32),
            jax.ShapeDtypeStruct((1, DV), F32),
        ],
        scratch_shapes=[
            pltpu.VMEM((heads, DK, DV), F32),
            pltpu.VMEM((8, conv_width), F32),
        ],
        compiler_params=pltpu.CompilerParams(vmem_limit_bytes=48 * 1024 * 1024),
        cost_estimate=pl.CostEstimate(
            flops=seqs * chunks * heads * 40 * 2 * rows**3,
            bytes_accessed=16 * 1024 * 1024,
            transcendentals=seqs * tokens * width,
        ),
        name="mixer_backward",
    )(projected, projected, filters, side, gain, adjoint, solved, update, start, raw)


def shift_pairs(count, by):
    return [(place, (place + by) % count) for place in range(count)]


def swap_pairs(count, mask):
    return [(place, place ^ mask) for place in range(count)]


def put_block(whole, block, place):
    return lax.dynamic_update_slice(whole, block[None], (place,) + (0,) * block.ndim)


def ring_gather(block, axis):
    count = lax.axis_size(axis)
    me = lax.axis_index(axis)
    whole = put_block(jnp.zeros((count,) + block.shape, block.dtype), block, me)
    right, left = block, block
    far = count // 2 if count % 2 == 0 else 0
    for hop in range(1, (count - 1) // 2 + 1):
        right = lax.ppermute(right, axis, shift_pairs(count, 1))
        left = lax.ppermute(left, axis, shift_pairs(count, -1))
        whole = put_block(whole, right, (me - hop) % count)
        whole = put_block(whole, left, (me + hop) % count)
    if far:
        half = block.shape[0] // 2
        right = lax.ppermute(right[:half], axis, shift_pairs(count, 1))
        left = lax.ppermute(left[half:], axis, shift_pairs(count, -1))
        whole = put_block(whole, right, (me + far) % count)
        whole = lax.dynamic_update_slice(
            whole, left[None], ((me + far) % count, half) + (0,) * (block.ndim - 1)
        )
    return whole


def take_block(whole, place):
    return lax.dynamic_index_in_dim(whole, place, 0, keepdims=False)


def ring_reduce(whole, axis):
    count = lax.axis_size(axis)
    me = lax.axis_index(axis)
    total = take_block(whole, me)
    if count == 1:
        return total
    half = total.shape[0] // 2
    reach = (count - 1) // 2
    right = left = None
    if count % 2 == 0:
        far = take_block(whole, (me + count // 2) % count)
        right = lax.ppermute(far[:half].astype(BF16), axis, shift_pairs(count, 1)).astype(F32)
        left = lax.ppermute(far[half:].astype(BF16), axis, shift_pairs(count, -1)).astype(F32)
    for hop in range(reach, 0, -1):
        ahead = take_block(whole, (me + hop) % count)
        behind = take_block(whole, (me - hop) % count)
        if right is not None and right.shape[0] == half:
            ahead = jnp.concatenate([ahead[:half] + right, ahead[half:]], axis=0)
            behind = jnp.concatenate([behind[:half], behind[half:] + left], axis=0)
        elif right is not None:
            ahead, behind = ahead + right, behind + left
        right = lax.ppermute(ahead.astype(BF16), axis, shift_pairs(count, 1)).astype(F32)
        left = lax.ppermute(behind.astype(BF16), axis, shift_pairs(count, -1)).astype(F32)
    if right.shape[0] == half:
        return total + jnp.concatenate([right, left], axis=0)
    return total + right + left


def exchange(whole, axis):
    count = lax.axis_size(axis)
    me = lax.axis_index(axis)
    result = put_block(jnp.zeros(whole.shape, whole.dtype), take_block(whole, me), me)
    for hop in range(1, count):
        moved = lax.ppermute(
            take_block(whole, (me + hop) % count), axis, shift_pairs(count, hop)
        )
        result = put_block(result, moved, (me - hop) % count)
    return result


def plane_gather(block):
    count = lax.axis_size("dp")
    if count != 8:
        return lax.all_gather(block, "dp", axis=0, tiled=False)
    me = lax.axis_index("dp")
    half = block.shape[0] // 2
    swap = lambda part, mask: lax.ppermute(part, "dp", swap_pairs(8, mask))
    near_two, near_four = swap(block, 2), swap(block, 4)
    far = jnp.concatenate([swap(near_two[:half], 4), swap(near_four[half:], 2)], axis=0)
    whole = jnp.zeros((8,) + block.shape, block.dtype)
    for mask, part in ((0, block), (2, near_two), (4, near_four), (6, far)):
        whole = put_block(whole, part, me ^ mask)
        whole = put_block(whole, swap(part, 1), me ^ mask ^ 1)
    return whole


def plane_reduce(whole):
    count = lax.axis_size("dp")
    if count != 8:
        return lax.psum_scatter(
            whole.astype(BF16), "dp", scatter_dimension=0, tiled=False
        ).astype(F32)
    me = lax.axis_index("dp")
    half = whole.shape[1] // 2
    swap = lambda part, mask: lax.ppermute(part.astype(BF16), "dp", swap_pairs(8, mask)).astype(
        F32
    )
    lane = {
        mask: take_block(whole, me ^ mask) + swap(take_block(whole, me ^ mask ^ 1), 1)
        for mask in (6, 2, 4, 0)
    }
    via_four = swap(lane[6][:half], 4)
    via_two = swap(lane[6][half:], 2)
    to_two = jnp.concatenate([lane[2][:half] + via_four, lane[2][half:]], axis=0)
    to_four = jnp.concatenate([lane[4][:half], lane[4][half:] + via_two], axis=0)
    return lane[0] + swap(to_two, 2) + swap(to_four, 4)


def sum_everywhere(values):
    for axis in ("dp", "seq"):
        count = lax.axis_size(axis)
        if count & (count - 1):
            values = lax.psum(values, axis)
            continue
        mask = 1
        while mask < count:
            values = values + lax.ppermute(values, axis, swap_pairs(count, mask))
            mask *= 2
    return values


def round_up(size, step):
    return (size + step - 1) // step * step


def rms_parts(values):
    scale = lax.rsqrt(jnp.mean(values * values, axis=-1, keepdims=True) + 1e-05)
    return values * scale, scale


def rms_back(unit, scale, gain, adjoint):
    scaled = adjoint * gain
    return scale * (scaled - unit * jnp.mean(scaled * unit, axis=-1, keepdims=True))


def dot(left, right):
    return jnp.dot(left, right, preferred_element_type=F32)


def dot_nt(left, right):
    return jnp.einsum("tc,dc->td", left, right, preferred_element_type=F32)


def dot_tn(left, right):
    return jnp.einsum("tr,tc->rc", left, right, preferred_element_type=F32)


def by_heads(weight, ns):
    return jnp.swapaxes(weight.reshape(weight.shape[0], ns, weight.shape[1] // ns), 0, 1)


def pad_last(values, size):
    if values.shape[-1] == size:
        return values
    return jnp.pad(values, [(0, 0)] * (values.ndim - 1) + [(0, size - values.shape[-1])])


def hidden_out(weight, nd, ns, padded):
    rows, hidden = weight.shape
    block = hidden // (nd * ns)
    parts = jnp.transpose(weight.reshape(rows, nd, ns, block), (2, 0, 1, 3))
    return pad_last(parts.reshape(ns, rows, nd * block), padded)


def hidden_back(parts, nd, hidden):
    ns, rows, _ = parts.shape
    block = hidden // (nd * ns)
    kept = parts[:, :, : nd * block].reshape(ns, rows, nd, block)
    return jnp.transpose(kept, (1, 2, 0, 3)).reshape(rows, hidden)


def shards(
    inputs,
    cotangent,
    query_proj,
    key_proj,
    value_proj,
    gate_proj,
    rate_proj,
    output_proj,
    ffn_gate,
    ffn_up,
    ffn_down,
    mixer_gain,
    ffn_gain,
    query_filter,
    key_filter,
    value_filter,
    decay_log,
    step_bias,
    head_gain,
):
    seqs, piece, width = inputs.shape
    ns, nd = lax.axis_size("seq"), lax.axis_size("dp")
    me = lax.axis_index("seq")
    heads = H // ns
    kq, kv = heads * DK, heads * DV
    own = seqs * piece
    tokens = own * ns
    rows = query_proj.shape[0]
    hidden = ffn_gate.shape[1]
    hidden_own = hidden // ns
    padded = round_up(hidden_own, LANES)

    def to_pieces(values):
        cut = values.reshape((seqs, ns, piece) + values.shape[1:])
        return jnp.swapaxes(cut, 0, 1).reshape((ns, own) + values.shape[1:])

    def from_pieces(values):
        cut = values.reshape((ns, seqs, piece) + values.shape[2:])
        return jnp.swapaxes(cut, 0, 1).reshape((tokens,) + values.shape[2:])

    flat_in = inputs.reshape(own, width)
    flat_cot = cotangent.reshape(own, width)
    mixer_local = jnp.concatenate(
        [by_heads(w, ns) for w in (query_proj, key_proj, value_proj, gate_proj)]
        + [pad_last(by_heads(rate_proj, ns), LANES)],
        axis=2,
    )
    mixer_rows = exchange(mixer_local, "seq").reshape(ns * rows, mixer_local.shape[2])
    mixer_weight = plane_gather(mixer_rows).reshape(width, mixer_local.shape[2])
    all_in = from_pieces(ring_gather(flat_in, "seq"))
    out_rows = ring_gather(output_proj, "seq").reshape(ns * output_proj.shape[0], width)
    out_weight = plane_gather(out_rows).reshape(H * DV, width)
    ffn_local = jnp.concatenate(
        [hidden_out(ffn_gate, nd, ns, padded), hidden_out(ffn_up, nd, ns, padded)], axis=2
    )
    ffn_rows = exchange(ffn_local, "seq").reshape(ns * rows, 2 * padded)
    ffn_weight = plane_gather(ffn_rows).reshape(width, 2 * padded)
    down_weight = plane_gather(ffn_down).reshape(hidden_own, width)
    down_weight = jnp.pad(down_weight, ((0, padded - hidden_own), (0, 0)))
    all_cot = from_pieces(ring_gather(flat_cot, "seq"))

    unit_in, scale_in = rms_parts(all_in.astype(F32))
    normed = (unit_in * mixer_gain).astype(BF16)
    projected = dot(normed, mixer_weight).astype(BF16).reshape(seqs, ns * piece, -1)
    own_cols = lambda table, size: lax.dynamic_slice_in_dim(table, me * size, size, 1)
    filters = jnp.concatenate(
        [own_cols(query_filter, kq), own_cols(key_filter, kq), own_cols(value_filter, kv)], axis=1
    )
    own_decay = jnp.exp(lax.dynamic_slice_in_dim(decay_log, me * heads, heads, 0))
    own_bias = lax.dynamic_slice_in_dim(step_bias, me * heads, heads, 0)
    spread = lambda values: pad_last(
        jnp.stack([jnp.zeros_like(values), values], axis=1).reshape(1, 2 * heads), LANES
    )
    side = jnp.concatenate(
        [spread(own_decay), spread(own_bias), jnp.zeros((6, LANES), F32)], axis=0
    )
    gain_row = head_gain.reshape(1, DV)
    mixed, *saved = mixer_forward(projected, filters, side, gain_row, heads)
    mixed_pieces = exchange(to_pieces(mixed.reshape(tokens, kv)), "seq")
    mixed_low = jnp.swapaxes(mixed_pieces, 0, 1).reshape(own, H * DV)

    middle = flat_in.astype(F32) + dot(mixed_low, out_weight)
    unit_two, scale_two = rms_parts(middle)
    second_all = from_pieces(ring_gather((unit_two * ffn_gain).astype(BF16), "seq"))
    hidden_both = dot(second_all, ffn_weight)
    hidden_gate, hidden_up = hidden_both[:, :padded], hidden_both[:, padded:]
    gate_sig = jax.nn.sigmoid(hidden_gate)
    gate_silu = hidden_gate * gate_sig
    active = (gate_silu * hidden_up).astype(BF16)
    block_sum = ring_reduce(to_pieces(dot(active, down_weight)), "seq")
    block_out = (middle + block_sum).astype(BF16).reshape(inputs.shape)

    adj_act = dot_nt(all_cot, down_weight)
    adj_gate = adj_act * hidden_up * silu_slope(hidden_gate, gate_sig)
    adj_both = jnp.concatenate(
        [adj_gate.astype(BF16), (adj_act * gate_silu).astype(BF16)], axis=1
    )
    adj_second = ring_reduce(to_pieces(dot_nt(adj_both, ffn_weight)), "seq")
    grad_down = dot_tn(active, all_cot)[:hidden_own].reshape(nd, -1, width)
    grad_ffn = dot_tn(second_all, adj_both).reshape(nd, ns * rows, 2 * padded)
    down_out = plane_reduce(grad_down).astype(BF16)
    ffn_parts = exchange(plane_reduce(grad_ffn).astype(BF16).reshape(ns, rows, -1), "seq")
    ffngate_out = hidden_back(ffn_parts[:, :, :padded], nd, hidden)
    ffnup_out = hidden_back(ffn_parts[:, :, padded:], nd, hidden)

    gain_two = jnp.sum(adj_second * unit_two, axis=0)
    adj_middle = flat_cot.astype(F32) + rms_back(unit_two, scale_two, ffn_gain, adj_second)
    attn_low = adj_middle.astype(BF16)
    adj_mixed = dot_nt(attn_low, out_weight).astype(BF16)
    adj_heads = from_pieces(
        exchange(jnp.swapaxes(adj_mixed.reshape(own, ns, kv), 0, 1), "seq")
    ).reshape(seqs, ns * piece, kv)
    grad_out = dot_tn(mixed_low, attn_low).reshape(nd, -1, width)
    grad_out = plane_reduce(grad_out)
    out_out = ring_reduce(grad_out.reshape(ns, -1, width), "seq").astype(BF16)

    adj_projected, filter_sum, side_sum, gain_sum = mixer_backward(
        projected, filters, side, gain_row, adj_heads, saved, heads
    )
    adj_projected = adj_projected.reshape(tokens, -1)
    adj_partial = dot_nt(adj_projected, mixer_weight)
    gain_one = jnp.sum(adj_partial * unit_in, axis=0)
    adj_normed = ring_reduce(to_pieces(adj_partial), "seq")
    grad_mixer = dot_tn(normed, adj_projected).reshape(nd, ns * rows, -1)
    mixer_parts = exchange(plane_reduce(grad_mixer).astype(BF16).reshape(ns, rows, -1), "seq")
    whole_rows = lambda parts: jnp.swapaxes(parts, 0, 1).reshape(rows, -1)
    query_out = whole_rows(mixer_parts[:, :, :kq])
    key_out = whole_rows(mixer_parts[:, :, kq : 2 * kq])
    value_out = whole_rows(mixer_parts[:, :, 2 * kq : 2 * kq + kv])
    gate_out = whole_rows(mixer_parts[:, :, 2 * kq + kv : 2 * kq + 2 * kv])
    rate_at = 2 * kq + 2 * kv
    rate_out = whole_rows(mixer_parts[:, :, rate_at : rate_at + 2 * heads])

    unit_one, scale_one = rms_parts(flat_in.astype(F32))
    grad_inputs = (
        (adj_middle + rms_back(unit_one, scale_one, mixer_gain, adj_normed))
        .astype(BF16)
        .reshape(inputs.shape)
    )

    def place(own_part, table, size):
        return lax.dynamic_update_slice_in_dim(
            jnp.zeros(table.shape, F32), own_part, me * size, table.ndim - 1
        )

    small = (
        gain_one,
        gain_two,
        place(filter_sum[:, :kq], query_filter, kq),
        place(filter_sum[:, kq : 2 * kq], key_filter, kq),
        place(filter_sum[:, 2 * kq :], value_filter, kv),
        place(side_sum[0, 1 : 2 * heads : 2], decay_log, heads),
        place(side_sum[1, 1 : 2 * heads : 2], step_bias, heads),
        gain_sum.reshape(DV),
    )
    packed = jnp.concatenate([pad_last(part.reshape(-1), round_up(part.size, LANES)) for part in small])
    packed = sum_everywhere(packed.reshape(-1, LANES)).astype(BF16).reshape(-1)
    outs = []
    at = 0
    for part in small:
        outs.append(packed[at : at + part.size].reshape(part.shape))
        at += round_up(part.size, LANES)
    return (
        block_out,
        grad_inputs,
        query_out,
        key_out,
        value_out,
        gate_out,
        rate_out,
        out_out,
        ffngate_out,
        ffnup_out,
        down_out,
        *outs,
    )


def solution(mesh):
    tokens = P("dp", "seq", None)
    weight = P(("dp", "seq"), None)
    specs = (tokens,) * 2 + (weight,) * 9 + (P(),) * 8
    return jax.shard_map(shards, mesh=mesh, in_specs=specs, out_specs=specs, check_vma=False)
```

time: 2020 us -> 628 us (0.31)
  matrix products: 633 us -> 52 us
  waiting for transfers between devices: 597 us -> 229 us
  blocking collectives: 223 us -> 0 us
  local copies, waits for them, and re-layouts: 294 us -> 118 us
  other arithmetic: 192 us -> 25.2 us
  starting transfers between devices: 34 us -> 133 us
  Pallas kernels: 0 us -> 59.1 us
    dot_general x1083 -> x12, matrix products: 633 us -> 52 us  [the longest x4 17.6 us: dot_tn(): return jnp.einsum('tr,tc->rc', left, right, preferred_element_type=F32)]
    reduce_scatter x17 -> x0, waiting for transfers between devices: 359 us -> none  [the longest x1 61.4 us: shards(): lax.psum_scatter(flat_rows(grad_down, device_total).astype(jnp.bfloat16),...]
    ppermute x0 -> x119, waiting for transfers between devices: none -> 229 us  [the longest x32 59.5 us: plane_gather(): swap = lambda part, mask: lax.ppermute(part, 'dp', swap_pairs(8, mask))]
    all_gather x8 -> x0, waiting for transfers between devices: 183 us -> none  [the longest x1 61.9 us: shards(): lax.all_gather(gate_proj, ('dp', 'seq'), axis=0, tiled=True)]
    ppermute x0 -> x119, starting transfers between devices: none -> 133 us  [the longest x18 26.5 us: exchange(): lax.ppermute(take_block(whole, (me + hop) % count), axis, shift_pairs(cou...]
    all_to_all x4 -> x0, blocking collectives: 97.8 us -> none  [the longest x1 36.4 us: shards(): lax.all_to_all(mixed.astype(jnp.bfloat16), 'seq', split_axis=1, concat_ax...]
    convert_element_type x28 -> x8, local copies, waits for them, and re-layouts: 83.8 us -> 6.98 us  [the longest x4 6.02 us: plane_reduce(): part.astype(BF16)]
    all_gather x1 -> x0, blocking collectives: 71.4 us -> none  [shards(): lax.all_gather(rate_proj, ('dp', 'seq'), axis=0, tiled=True)]
  transfers between devices with their start and end apart: 33 -> 119, of which waited for: 17 -> 62; matrix products, arithmetic and copies ran while one was open for 20% -> 27% of each run, Pallas kernels for 0% -> 10%
where the time goes in v1:
time: 628 us; the launch traced here: 619 us
  waiting for transfers between devices  229 us (36%)
  starting transfers between devices  133 us (21%)
  local copies, waits for them, and re-layouts  118 us (19%)
  Pallas kernels  59.1 us (9%)
  matrix products  52 us (8%)
  other arithmetic  25.2 us (4%)
    ppermute x32, waiting for transfers between devices, plane_gather(): swap = lambda part, mask: lax.ppermute(part, 'dp', swap_pairs(8, mask))  59.5 us
    ppermute x18, waiting for transfers between devices, exchange(): lax.ppermute(take_block(whole, (me + hop) % count), axis, shift_pairs(cou...  51.5 us
    dynamic_update_slice x68, local copies, waits for them, and re-layouts, put_block(): lax.dynamic_update_slice(whole, block[None], (place,) + (0,) * block.ndim)  40.2 us
    ppermute x32, waiting for transfers between devices, plane_reduce(): lax.ppermute(part.astype(BF16), 'dp', swap_pairs(8, mask)).astype(F32)  36.2 us
    pallas_call x1, Pallas kernels, mixer_forward(): pl.pallas_call(functools.partial(mixer_forward_kernel, heads=heads), grid...  32.9 us
    ppermute x18, starting transfers between devices, exchange(): lax.ppermute(take_block(whole, (me + hop) % count), axis, shift_pairs(cou...  26.5 us
    pallas_call x1, Pallas kernels, mixer_backward(): pl.pallas_call(functools.partial(mixer_backward_kernel, heads=heads, chun...  26.2 us
    ppermute x4, waiting for transfers between devices, ring_reduce(): lax.ppermute(behind.astype(BF16), axis, shift_pairs(count, -1)).astype(F32)  22.6 us
  transfers between devices with their start and end apart: 119, of which 62 were waited for; matrix products, arithmetic and copies ran while one was open for 27% of the time, Pallas kernels for 10%

profile of v1, /device:TPU:0, one launch (start us, length us, event | category | flops | bytes accessed | tf_op | source)
XLA Modules:
  0.0 618.8 jit_solution(6302417267614875848)
XLA Ops:
  5.9 3.8 collective-permute-start.19
  24.4 12.7 %collective-permute-done.34 = bf16[32,1536]{1,0:T(8,128)(2,1)} collective-permute-done((bf16[32,1536]{1,0:T(8,128)(2,1)}, bf16[32,1536]{1,0:T(8,128)(2,1)}, u32[]{:S(2)}, u32[]{:S(2)}) %collective-permute-start.34) | collective-permute-done | bytes 98336 | tf_op jit(solution)/shard_map/ppermute | solution.py:497
  38.6 4.9 collective-permute-done.35
  51.0 5.0 collective-permute-done.4
  57.2 5.1 collective-permute-done.5
  78.6 4.2 collective-permute-start.21
  92.4 4.2 collective-permute-start.58
  99.1 7.6 %collective-permute-done.38 = bf16[128,1536]{1,0:T(8,128)(2,1)S(1)} collective-permute-done((bf16[128,1536]{1,0:T(8,128)(2,1)S(1)}, bf16[128,1536]{1,0:T(8,128)(2,1)S(1)}, u32[]{:S(2)}, u32[]{:S(2)}) %collective-permute-start.38) | collective-permute-done | bytes 393248 | tf_op jit(solution)/shard_map/ppermute | solution.py:510
  109.1 6.8 %collective-permute-done.40 = bf16[128,1536]{1,0:T(8,128)(2,1)S(1)} collective-permute-done((bf16[128,1536]{1,0:T(8,128)(2,1)S(1)}, bf16[128,1536]{1,0:T(8,128)(2,1)S(1)}, u32[]{:S(2)}, u32[]{:S(2)}) %collective-permute-start.40) | collective-permute-done | bytes 393248 | tf_op jit(solution)/shard_map/ppermute | solution.py:510
  124.6 4.2 collective-permute-done.8
  133.5 12.8 %collective-permute-done.42 = bf16[64,1536]{1,0:T(8,128)(2,1)S(1)} collective-permute-done((bf16[64,1536]{1,0:T(8,128)(2,1)S(1)}, bf16[64,1536]{1,0:T(8,128)(2,1)S(1)}, u32[]{:S(2)}, u32[]{:S(2)}) %collective-permute-start.42) | collective-permute-done | bytes 196640 | tf_op jit(solution)/shard_map/ppermute | solution.py:510
  149.1 3.9 collective-permute-start.3
  155.6 5.1 collective-permute-done.12
  161.0 5.5 collective-permute-done.13
  166.5 4.1 collective-permute-start.60
  170.8 6.1 collective-permute-done.59
  183.7 3.7 collective-permute-done.27
  190.0 5.3 fusion.4.current_ref.before_ref
  195.3 32.9 %mixer_forward.1 = (bf16[1,1024,512]{2,1,0:T(8,128)(2,1)S(1)}, bf16[1,4,2,256,256]{4,3,2,1,0:T(8,128)(2,1)S(1)}, bf16[1,1024,512]{2,1,0:T(8,128)(2,1)S(1)}, f32[...) custom-call(bf16[1,1024,1664]{2,1,0:T(8,128)(2,1)} %fusion.4.current_ref.before_ref, ...), custom_call_target="tpu_custom_call" | custom-call | flops 8053063680 | bytes 12582912 | tf_op jit(solution)/shard_map/mixer_forward/pallas_call | solution.py:340
  248.2 4.7 collective-permute-done.16
  257.5 3.9 multiply_reduce_fusion.4
  264.1 3.9 collective-permute-start.30
  272.2 9.3 %collective-permute-done.30 = bf16[256,1024]{1,0:T(8,128)(2,1)S(1)} collective-permute-done((bf16[256,1024]{1,0:T(8,128)(2,1)S(1)}, bf16[256,1024]{1,0:T(8,128)(2,1)S(1)}, u32[]{:S(2)}, u32[]{:S(2)}) %collective-permute-start.30) | collective-permute-done | bytes 524320 | tf_op jit(solution)/shard_map/ppermute | solution.py:445
  282.9 9.8 %collective-permute-done.31 = bf16[256,1024]{1,0:T(8,128)(2,1)S(1)} collective-permute-done((bf16[256,1024]{1,0:T(8,128)(2,1)S(1)}, bf16[256,1024]{1,0:T(8,128)(2,1)S(1)}, u32[]{:S(2)}, u32[]{:S(2)}) %collective-permute-start.31) | collective-permute-done | bytes 524320 | tf_op jit(solution)/shard_map/ppermute | solution.py:446
  292.7 3.7 collective-permute-start.33
  299.0 3.9 collective-permute-done.33
  303.7 3.9 copy.131
  307.6 6.1 fusion.115
  313.7 3.7 multiply_convert_fusion.3
  321.2 5.3 fusion.116
  341.9 4.6 collective-permute-done.55
  346.5 7.1 %collective-permute-done.53 = bf16[128,1024]{1,0:T(8,128)(2,1)S(1)} collective-permute-done((bf16[128,1024]{1,0:T(8,128)(2,1)S(1)}, bf16[128,1024]{1,0:T(8,128)(2,1)S(1)}, u32[]{:S(2)}, u32[]{:S(2)}) %collective-permute-start.53) | collective-permute-done | bytes 262176 | tf_op jit(solution)/shard_map/ppermute | solution.py:475
  373.1 4.4 collective-permute-done.101
  378.4 4.7 collective-permute-done.98
  391.4 19.6 %collective-permute-done.56 = bf16[256,1024]{1,0:T(8,128)(2,1)S(1)} collective-permute-done((bf16[256,1024]{1,0:T(8,128)(2,1)S(1)}, bf16[256,1024]{1,0:T(8,128)(2,1)S(1)}, u32[]{:S(2)}, u32[]{:S(2)}) %collective-permute-start.56) | collective-permute-done | bytes 524320 | tf_op jit(solution)/shard_map/ppermute | solution.py:486
  418.7 5.7 constant_dynamic-slice_fusion
  432.0 5.9 fusion.61
  440.9 3.6 fusion.41
  458.1 26.2 %mixer_backward.1 = (bf16[1,1024,1664]{2,1,0:T(8,128)(2,1)}, f32[4,1024]{1,0:T(4,128)S(1)}, f32[8,128]{1,0:T(8,128)S(1)}, f32[1,256]{1,0:T(1,128)S(1)}) custom-call(bf16[1,1024,1664]{2,1,0:T(8,128)(2,1)} %fusion.4.current_ref.before_ref, bf16[1,1024,1664]{2,1,0:T(8,128)(2,1)} %fusion.4.current_ref.before_ref, f32[4,1024]{1,0:T(4,128)S(1)} %pad_maximum_fusion.18.filter_ref, ...), custom_call_target="tpu_custom_call" | custom-call | flops 10737418240 | bytes 16777216 | tf_op jit(solution)/shard_map/mixer_backward/pallas_call | solution.py:382
  484.3 6.0 multiply_reduce_fusion
  496.4 6.5 %fusion = f32[8,128,1664]{2,1,0:T(8,128)S(1)} fusion(bf16[8,128,1024]{2,1,0:T(8,128)(2,1)} %bitcast.570, bf16[1,1024,1664]{2,1,0:T(8,128)(2,1)} %get-tuple-element.33), kind=kOutput, calls=%fused_computation.6 | convolution fusion | flops 3489660928 | bytes 12320768 | tf_op jit(solution)/shard_map/tr,tc->rc/dot_general | solution.py:578
  508.7 4.7 collective-permute-done.104
  528.7 4.3 collective-permute-start.70
  557.4 4.0 collective-permute-start.71
  566.7 6.0 collective-permute-done.78
  573.2 5.3 collective-permute-done.75
  580.6 4.2 collective-permute-done.69
  588.6 4.4 collective-permute-done.90
  (596 shorter events, 292.5 us)
Async XLA Ops:
  0.7 115.2 %collective-permute-start = (bf16[256,1024]{1,0:T(8,128)(2,1)}, bf16[256,1024]{1,0:T(8,128)(2,1)}, u32[]{:S(2)}, u32[]{:S(2)}) collective-permute-start(bf16[256,1024]{1,0:T(8,128)(2,1)} %bitcast.543), channel_id=1, source_target_pairs={{0,1},{1,2},{2,3},{3,0},{4,5},{5,6},{6,7},{7,4},{8,9},{9,10},{10,1... | collective-permute-start | bytes 1572872 | tf_op jit(solution)/shard_map/ppermute | solution.py:445
  3.8 114.8 %collective-permute-start.1 = (bf16[256,1024]{1,0:T(8,128)(2,1)}, bf16[256,1024]{1,0:T(8,128)(2,1)}, u32[]{:S(2)}, u32[]{:S(2)}) collective-permute-start(bf16[256,1024]{1,0:T(8,128)(2,1)} %bitcast.544), channel_id=1, source_target_pairs={{0,3},{1,0},{2,1},{3,2},{4,7},{5,4},{6,5},{7,6},{8,11},{9,8},{10,9... | collective-permute-start | bytes 1572872 | tf_op jit(solution)/shard_map/ppermute | solution.py:446
  5.9 63.8 %collective-permute-start.18 = (bf16[64,1024]{1,0:T(8,128)(2,1)}, bf16[64,1024]{1,0:T(8,128)(2,1)}, u32[]{:S(2)}, u32[]{:S(2)}) collective-permute-start(bf16[64,1024]{1,0:T(8,128)(2,1)} %param.26), channel_id=1, source_target_pairs={{0,1},{1,2},{2,3},{3,0},{4,5},{5,6},{6,7},{7,4},{8,9},{9,10},{10,1... | collective-permute-start | bytes 393224 | tf_op jit(solution)/shard_map/ppermute | solution.py:445
  5.9 66.0 %collective-permute-start.19 = (bf16[64,1024]{1,0:T(8,128)(2,1)}, bf16[64,1024]{1,0:T(8,128)(2,1)S(1)}, u32[]{:S(2)}, u32[]{:S(2)}) collective-permute-start(bf16[64,1024]{1,0:T(8,128)(2,1)} %param.26), channel_id=1, source_target_pairs={{0,3},{1,0},{2,1},{3,2},{4,7},{5,4},{6,5},{7,6},{8,11},{9,8},{10,9... | collective-permute-start | bytes 393224 | tf_op jit(solution)/shard_map/ppermute | solution.py:446
  14.9 22.2 %collective-permute-start.34 = (bf16[32,1536]{1,0:T(8,128)(2,1)}, bf16[32,1536]{1,0:T(8,128)(2,1)}, u32[]{:S(2)}, u32[]{:S(2)}) collective-permute-start(bf16[32,1536]{1,0:T(8,128)(2,1)} %get-tuple-element.135), channel_id=1, source_target_pairs={{0,1},{1,2},{2,3},{3,0},{4,5},{5,6},{6,7},{7,4},{8,9},{9,10},{10,1... | collective-permute-start | bytes 294920 | tf_op jit(solution)/shard_map/ppermute | solution.py:497
  73.4 23.1 %collective-permute-start.37 = (bf16[128,1536]{1,0:T(8,128)(2,1)S(1)}, bf16[128,1536]{1,0:T(8,128)(2,1)S(1)}, u32[]{:S(2)}, u32[]{:S(2)}) collective-permute-start(bf16[128,1536]{1,0:T(8,128)(2,1)S(1)} %bitcast.583), channel_id=1, source_target_pairs={{0,4},{4,0},{8,12},{12,8},{16,20},{20,16},{24,28},{28,24},{1,5},{5... | collective-permute-start | bytes 1179656 | tf_op jit(solution)/shard_map/ppermute | solution.py:510
  89.1 30.9 %collective-permute-start.57 = (bf16[256,1024]{1,0:T(8,128)(2,1)S(1)}, bf16[256,1024]{1,0:T(8,128)(2,1)S(1)}, u32[]{:S(2)}, u32[]{:S(2)}) collective-permute-start(bf16[256,1024]{1,0:T(8,128)(2,1)S(1)} %bitcast.575), channel_id=1, source_target_pairs={{0,1},{1,2},{2,3},{3,0},{4,5},{5,6},{6,7},{7,4},{8,9},{9,10},{10,1... | collective-permute-start | bytes 1572872 | tf_op jit(solution)/shard_map/ppermute | solution.py:445
  92.4 29.9 %collective-permute-start.58 = (bf16[256,1024]{1,0:T(8,128)(2,1)S(1)}, bf16[256,1024]{1,0:T(8,128)(2,1)S(1)}, u32[]{:S(2)}, u32[]{:S(2)}) collective-permute-start(bf16[256,1024]{1,0:T(8,128)(2,1)S(1)} %bitcast.576), channel_id=1, source_target_pairs={{0,3},{1,0},{2,1},{3,2},{4,7},{5,4},{6,5},{7,6},{8,11},{9,8},{10,9... | collective-permute-start | bytes 1572872 | tf_op jit(solution)/shard_map/ppermute | solution.py:446
  120.0 34.0 %collective-permute-start.22 = (bf16[256,1024]{1,0:T(8,128)(2,1)S(1)}, bf16[256,1024]{1,0:T(8,128)(2,1)S(1)}, u32[]{:S(2)}, u32[]{:S(2)}) collective-permute-start(bf16[256,1024]{1,0:T(8,128)(2,1)S(1)} %bitcast.572), channel_id=1, source_target_pairs={{0,4},{4,0},{8,12},{12,8},{16,20},{20,16},{24,28},{28,24},{1,5},{5... | collective-permute-start | bytes 1572872 | tf_op jit(solution)/shard_map/ppermute | solution.py:510
  122.3 25.9 %collective-permute-start.23 = (bf16[256,1024]{1,0:T(8,128)(2,1)S(1)}, bf16[256,1024]{1,0:T(8,128)(2,1)}, u32[]{:S(2)}, u32[]{:S(2)}) collective-permute-start(bf16[256,1024]{1,0:T(8,128)(2,1)S(1)} %bitcast.573), channel_id=1, source_target_pairs={{0,8},{4,12},{8,0},{12,4},{16,24},{20,28},{24,16},{28,20},{1,9},{5... | collective-permute-start | bytes 1572872 | tf_op jit(solution)/shard_map/ppermute | solution.py:510
  124.0 25.1 %collective-permute-start.25 = (bf16[256,1024]{1,0:T(8,128)(2,1)S(1)}, bf16[256,1024]{1,0:T(8,128)(2,1)}, u32[]{:S(2)}, u32[]{:S(2)}) collective-permute-start(bf16[256,1024]{1,0:T(8,128)(2,1)S(1)} %bitcast.574), channel_id=1, source_target_pairs={{0,16},{4,20},{8,24},{12,28},{16,0},{20,4},{24,8},{28,12},{1,17},{... | collective-permute-start | bytes 1572872 | tf_op jit(solution)/shard_map/ppermute | solution.py:510
  146.3 32.4 %collective-permute-start.39 = (bf16[128,1536]{1,0:T(8,128)(2,1)S(1)}, bf16[128,1536]{1,0:T(8,128)(2,1)S(1)}, u32[]{:S(2)}, u32[]{:S(2)}) collective-permute-start(bf16[128,1536]{1,0:T(8,128)(2,1)S(1)} %collective-permute-done.38), channel_id=1, source_target_pairs={{0,4},{4,0},{8,12},{12,8},{16,20},{20,16},{24,28},{28,24},{1,5},{5... | collective-permute-start | bytes 1179656 | tf_op jit(solution)/shard_map/ppermute | solution.py:510
  146.9 33.8 %collective-permute-start.41 = (bf16[128,1536]{1,0:T(8,128)(2,1)S(1)}, bf16[128,1536]{1,0:T(8,128)(2,1)S(1)}, u32[]{:S(2)}, u32[]{:S(2)}) collective-permute-start(bf16[128,1536]{1,0:T(8,128)(2,1)S(1)} %collective-permute-done.40), channel_id=1, source_target_pairs={{0,4},{4,0},{8,12},{12,8},{16,20},{20,16},{24,28},{28,24},{1,5},{5... | collective-permute-start | bytes 1179656 | tf_op jit(solution)/shard_map/ppermute | solution.py:510
  148.2 18.4 %collective-permute-start.2 = (bf16[128,1024]{1,0:T(8,128)(2,1)S(1)}, bf16[128,1024]{1,0:T(8,128)(2,1)S(1)}, u32[]{:S(2)}, u32[]{:S(2)}) collective-permute-start(bf16[128,1024]{1,0:T(8,128)(2,1)S(1)} %slice.472), channel_id=1, source_target_pairs={{0,1},{1,2},{2,3},{3,0},{4,5},{5,6},{6,7},{7,4},{8,9},{9,10},{10,1... | collective-permute-start | bytes 786440 | tf_op jit(solution)/shard_map/ppermute | solution.py:451
  149.1 21.5 %collective-permute-start.3 = (bf16[128,1024]{1,0:T(8,128)(2,1)S(1)}, bf16[128,1024]{1,0:T(8,128)(2,1)S(1)}, u32[]{:S(2)}, u32[]{:S(2)}) collective-permute-start(bf16[128,1024]{1,0:T(8,128)(2,1)S(1)} %slice.473), channel_id=1, source_target_pairs={{0,3},{1,0},{2,1},{3,2},{4,7},{5,4},{6,5},{7,6},{8,11},{9,8},{10,9... | collective-permute-start | bytes 786440 | tf_op jit(solution)/shard_map/ppermute | solution.py:452
  178.0 92.4 %collective-permute-start.44 = (bf16[128,1536]{1,0:T(8,128)(2,1)}, bf16[128,1536]{1,0:T(8,128)(2,1)}, u32[]{:S(2)}, u32[]{:S(2)}) collective-permute-start(bf16[128,1536]{1,0:T(8,128)(2,1)} %constant_dynamic-update-slice_fusion.11), channel_id=1, source_target_pairs={{0,4},{4,0},{8,12},{12,8},{16,20},{20,16},{24,28},{28,24},{1,5},{5... | collective-permute-start | bytes 1179656 | tf_op jit(solution)/shard_map/ppermute | solution.py:510
  183.0 51.8 %collective-permute-start.24 = (bf16[256,1024]{1,0:T(8,128)(2,1)}, bf16[256,1024]{1,0:T(8,128)(2,1)}, u32[]{:S(2)}, u32[]{:S(2)}) collective-permute-start(bf16[256,1024]{1,0:T(8,128)(2,1)} %collective-permute-done.23), channel_id=1, source_target_pairs={{0,4},{4,0},{8,12},{12,8},{16,20},{20,16},{24,28},{28,24},{1,5},{5... | collective-permute-start | bytes 1572872 | tf_op jit(solution)/shard_map/ppermute | solution.py:510
  187.4 53.9 %collective-permute-start.26 = (bf16[256,1024]{1,0:T(8,128)(2,1)}, bf16[256,1024]{1,0:T(8,128)(2,1)}, u32[]{:S(2)}, u32[]{:S(2)}) collective-permute-start(bf16[256,1024]{1,0:T(8,128)(2,1)} %collective-permute-done.25), channel_id=1, source_target_pairs={{0,4},{4,0},{8,12},{12,8},{16,20},{20,16},{24,28},{28,24},{1,5},{5... | collective-permute-start | bytes 1572872 | tf_op jit(solution)/shard_map/ppermute | solution.py:510
  189.9 65.3 %collective-permute-start.29 = (bf16[256,1024]{1,0:T(8,128)(2,1)}, bf16[256,1024]{1,0:T(8,128)(2,1)}, u32[]{:S(2)}, u32[]{:S(2)}) collective-permute-start(bf16[256,1024]{1,0:T(8,128)(2,1)} %constant_dynamic-update-slice_fusion.9), channel_id=1, source_target_pairs={{0,4},{4,0},{8,12},{12,8},{16,20},{20,16},{24,28},{28,24},{1,5},{5... | collective-permute-start | bytes 1572872 | tf_op jit(solution)/shard_map/ppermute | solution.py:510
  230.9 16.3 %collective-permute-start.15 = (bf16[256,512]{0,1:T(8,128)(2,1)}, bf16[256,512]{0,1:T(8,128)(2,1)}, u32[]{:S(2)}, u32[]{:S(2)}) collective-permute-start(bf16[256,512]{0,1:T(8,128)(2,1)} %bitcast.30), channel_id=1, source_target_pairs={{0,1},{1,2},{2,3},{3,0},{4,5},{5,6},{6,7},{7,4},{8,9},{9,10},{10,1... | collective-permute-start | bytes 786440 | tf_op jit(solution)/shard_map/ppermute | solution.py:497
  234.7 18.3 %collective-permute-start.16 = (bf16[256,512]{0,1:T(8,128)(2,1)}, bf16[256,512]{0,1:T(8,128)(2,1)S(1)}, u32[]{:S(2)}, u32[]{:S(2)}) collective-permute-start(bf16[256,512]{0,1:T(8,128)(2,1)} %bitcast.596), channel_id=1, source_target_pairs={{0,2},{1,3},{2,0},{3,1},{4,6},{5,7},{6,4},{7,5},{8,10},{9,11},{10,... | collective-permute-start | bytes 786440 | tf_op jit(solution)/shard_map/ppermute | solution.py:497
  264.1 17.4 %collective-permute-start.30 = (bf16[256,1024]{1,0:T(8,128)(2,1)S(1)}, bf16[256,1024]{1,0:T(8,128)(2,1)S(1)}, u32[]{:S(2)}, u32[]{:S(2)}) collective-permute-start(bf16[256,1024]{1,0:T(8,128)(2,1)S(1)} %get-tuple-element.43), channel_id=1, source_target_pairs={{0,1},{1,2},{2,3},{3,0},{4,5},{5,6},{6,7},{7,4},{8,9},{9,10},{10,1... | collective-permute-start | bytes 1572872 | tf_op jit(solution)/shard_map/ppermute | solution.py:445
  268.0 24.6 %collective-permute-start.31 = (bf16[256,1024]{1,0:T(8,128)(2,1)S(1)}, bf16[256,1024]{1,0:T(8,128)(2,1)S(1)}, u32[]{:S(2)}, u32[]{:S(2)}) collective-permute-start(bf16[256,1024]{1,0:T(8,128)(2,1)S(1)} %get-tuple-element.43), channel_id=1, source_target_pairs={{0,3},{1,0},{2,1},{3,2},{4,7},{5,4},{6,5},{7,6},{8,11},{9,8},{10,9... | collective-permute-start | bytes 1572872 | tf_op jit(solution)/shard_map/ppermute | solution.py:446
  281.5 16.8 %collective-permute-start.32 = (bf16[128,1024]{1,0:T(8,128)(2,1)S(1)}, bf16[128,1024]{1,0:T(8,128)(2,1)S(1)}, u32[]{:S(2)}, u32[]{:S(2)}) collective-permute-start(bf16[128,1024]{1,0:T(8,128)(2,1)S(1)} %slice.480), channel_id=1, source_target_pairs={{0,1},{1,2},{2,3},{3,0},{4,5},{5,6},{6,7},{7,4},{8,9},{9,10},{10,1... | collective-permute-start | bytes 786440 | tf_op jit(solution)/shard_map/ppermute | solution.py:451
  338.4 15.2 %collective-permute-start.53 = (bf16[128,1024]{1,0:T(8,128)(2,1)S(1)}, bf16[128,1024]{1,0:T(8,128)(2,1)S(1)}, u32[]{:S(2)}, u32[]{:S(2)}) collective-permute-start(bf16[128,1024]{1,0:T(8,128)(2,1)S(1)} %get-tuple-element.109), channel_id=1, source_target_pairs={{0,1},{1,2},{2,3},{3,0},{4,5},{5,6},{6,7},{7,4},{8,9},{9,10},{10,1... | collective-permute-start | bytes 786440 | tf_op jit(solution)/shard_map/ppermute | solution.py:475
  339.0 23.9 %collective-permute-start.96 = (bf16[128,1536]{1,0:T(8,128)(2,1)S(1)}, bf16[128,1536]{1,0:T(8,128)(2,1)S(1)}, u32[]{:S(2)}, u32[]{:S(2)}) collective-permute-start(bf16[128,1536]{1,0:T(8,128)(2,1)S(1)} %get-tuple-element.63), channel_id=1, source_target_pairs={{0,4},{4,0},{8,12},{12,8},{16,20},{20,16},{24,28},{28,24},{1,5},{5... | collective-permute-start | bytes 1179656 | tf_op jit(solution)/shard_map/ppermute | solution.py:528
  339.3 24.4 %collective-permute-start.100 = (bf16[128,1536]{1,0:T(8,128)(2,1)S(1)}, bf16[128,1536]{1,0:T(8,128)(2,1)S(1)}, u32[]{:S(2)}, u32[]{:S(2)}) collective-permute-start(bf16[128,1536]{1,0:T(8,128)(2,1)S(1)} %get-tuple-element.61), channel_id=1, source_target_pairs={{0,4},{4,0},{8,12},{12,8},{16,20},{20,16},{24,28},{28,24},{1,5},{5... | collective-permute-start | bytes 1179656 | tf_op jit(solution)/shard_map/ppermute | solution.py:528
  341.9 23.3 %collective-permute-start.97 = (bf16[128,1536]{1,0:T(8,128)(2,1)S(1)}, bf16[128,1536]{1,0:T(8,128)(2,1)S(1)}, u32[]{:S(2)}, u32[]{:S(2)}) collective-permute-start(bf16[128,1536]{1,0:T(8,128)(2,1)S(1)} %get-tuple-element.62), channel_id=1, source_target_pairs={{0,4},{4,0},{8,12},{12,8},{16,20},{20,16},{24,28},{28,24},{1,5},{5... | collective-permute-start | bytes 1179656 | tf_op jit(solution)/shard_map/ppermute | solution.py:528
  346.5 98.0 %collective-permute-start.95 = (bf16[128,1536]{1,0:T(8,128)(2,1)}, bf16[128,1536]{1,0:T(8,128)(2,1)}, u32[]{:S(2)}, u32[]{:S(2)}) collective-permute-start(bf16[128,1536]{1,0:T(8,128)(2,1)} %get-tuple-element.60), channel_id=1, source_target_pairs={{0,4},{4,0},{8,12},{12,8},{16,20},{20,16},{24,28},{28,24},{1,5},{5... | collective-permute-start | bytes 1179656 | tf_op jit(solution)/shard_map/ppermute | solution.py:528
  362.9 26.0 %collective-permute-start.64 = (bf16[256,1024]{1,0:T(8,128)(2,1)S(1)}, bf16[256,1024]{1,0:T(8,128)(2,1)S(1)}, u32[]{:S(2)}, u32[]{:S(2)}) collective-permute-start(bf16[256,1024]{1,0:T(8,128)(2,1)S(1)} %pad_maximum_fusion.4), channel_id=1, source_target_pairs={{0,3},{1,0},{2,1},{3,2},{4,7},{5,4},{6,5},{7,6},{8,11},{9,8},{10,9... | collective-permute-start | bytes 1572872 | tf_op jit(solution)/shard_map/ppermute | solution.py:486
  366.1 24.4 %collective-permute-start.62 = (bf16[256,1024]{1,0:T(8,128)(2,1)S(1)}, bf16[256,1024]{1,0:T(8,128)(2,1)S(1)}, u32[]{:S(2)}, u32[]{:S(2)}) collective-permute-start(bf16[256,1024]{1,0:T(8,128)(2,1)S(1)} %pad_maximum_fusion.3), channel_id=1, source_target_pairs={{0,1},{1,2},{2,3},{3,0},{4,5},{5,6},{6,7},{7,4},{8,9},{9,10},{10,1... | collective-permute-start | bytes 1572872 | tf_op jit(solution)/shard_map/ppermute | solution.py:485
  370.4 40.7 %collective-permute-start.56 = (bf16[256,1024]{1,0:T(8,128)(2,1)S(1)}, bf16[256,1024]{1,0:T(8,128)(2,1)S(1)}, u32[]{:S(2)}, u32[]{:S(2)}) collective-permute-start(bf16[256,1024]{1,0:T(8,128)(2,1)S(1)} %pad_maximum_fusion.2), channel_id=1, source_target_pairs={{0,3},{1,0},{2,1},{3,2},{4,7},{5,4},{6,5},{7,6},{8,11},{9,8},{10,9... | collective-permute-start | bytes 1572872 | tf_op jit(solution)/shard_map/ppermute | solution.py:486
  383.2 27.8 %collective-permute-start.54 = (bf16[256,1024]{1,0:T(8,128)(2,1)S(1)}, bf16[256,1024]{1,0:T(8,128)(2,1)S(1)}, u32[]{:S(2)}, u32[]{:S(2)}) collective-permute-start(bf16[256,1024]{1,0:T(8,128)(2,1)S(1)} %pad_maximum_fusion.1), channel_id=1, source_target_pairs={{0,1},{1,2},{2,3},{3,0},{4,5},{5,6},{6,7},{7,4},{8,9},{9,10},{10,1... | collective-permute-start | bytes 1572872 | tf_op jit(solution)/shard_map/ppermute | solution.py:485
  388.9 57.1 %collective-permute-start.102 = (bf16[128,1536]{1,0:T(8,128)(2,1)}, bf16[128,1536]{1,0:T(8,128)(2,1)}, u32[]{:S(2)}, u32[]{:S(2)}) collective-permute-start(bf16[128,1536]{1,0:T(8,128)(2,1)} %pad_maximum_fusion.12), channel_id=1, source_target_pairs={{0,16},{4,20},{8,24},{12,28},{16,0},{20,4},{24,8},{28,12},{1,17},{... | collective-permute-start | bytes 1179656 | tf_op jit(solution)/shard_map/ppermute | solution.py:528
  390.5 55.5 %collective-permute-start.99 = (bf16[128,1536]{1,0:T(8,128)(2,1)}, bf16[128,1536]{1,0:T(8,128)(2,1)}, u32[]{:S(2)}, u32[]{:S(2)}) collective-permute-start(bf16[128,1536]{1,0:T(8,128)(2,1)} %pad_maximum_fusion.11), channel_id=1, source_target_pairs={{0,8},{4,12},{8,0},{12,4},{16,24},{20,28},{24,16},{28,20},{1,9},{5... | collective-permute-start | bytes 1179656 | tf_op jit(solution)/shard_map/ppermute | solution.py:528
  427.1 21.2 %collective-permute-start.65 = (bf16[256,512]{0,1:T(8,128)(2,1)}, bf16[256,512]{0,1:T(8,128)(2,1)}, u32[]{:S(2)}, u32[]{:S(2)}) collective-permute-start(bf16[256,512]{0,1:T(8,128)(2,1)} %bitcast.217), channel_id=1, source_target_pairs={{0,1},{1,2},{2,3},{3,0},{4,5},{5,6},{6,7},{7,4},{8,9},{9,10},{10,1... | collective-permute-start | bytes 786440 | tf_op jit(solution)/shard_map/ppermute | solution.py:497
  429.7 20.4 %collective-permute-start.66 = (bf16[256,512]{0,1:T(8,128)(2,1)}, bf16[256,512]{0,1:T(8,128)(2,1)}, u32[]{:S(2)}, u32[]{:S(2)}) collective-permute-start(bf16[256,512]{0,1:T(8,128)(2,1)} %bitcast.218), channel_id=1, source_target_pairs={{0,2},{1,3},{2,0},{3,1},{4,6},{5,7},{6,4},{7,5},{8,10},{9,11},{10,... | collective-permute-start | bytes 786440 | tf_op jit(solution)/shard_map/ppermute | solution.py:497
  446.0 82.7 %collective-permute-start.84 = (bf16[256,1024]{1,0:T(8,128)(2,1)}, bf16[256,1024]{1,0:T(8,128)(2,1)}, u32[]{:S(2)}, u32[]{:S(2)}) collective-permute-start(bf16[256,1024]{1,0:T(8,128)(2,1)} %get-tuple-element.49), channel_id=1, source_target_pairs={{0,4},{4,0},{8,12},{12,8},{16,20},{20,16},{24,28},{28,24},{1,5},{5... | collective-permute-start | bytes 1572872 | tf_op jit(solution)/shard_map/ppermute | solution.py:528
  446.0 87.0 %collective-permute-start.88 = (bf16[256,1024]{1,0:T(8,128)(2,1)}, bf16[256,1024]{1,0:T(8,128)(2,1)}, u32[]{:S(2)}, u32[]{:S(2)}) collective-permute-start(bf16[256,1024]{1,0:T(8,128)(2,1)} %get-tuple-element.47), channel_id=1, source_target_pairs={{0,4},{4,0},{8,12},{12,8},{16,20},{20,16},{24,28},{28,24},{1,5},{5... | collective-permute-start | bytes 1572872 | tf_op jit(solution)/shard_map/ppermute | solution.py:528
  448.3 84.7 %collective-permute-start.85 = (bf16[256,1024]{1,0:T(8,128)(2,1)}, bf16[256,1024]{1,0:T(8,128)(2,1)}, u32[]{:S(2)}, u32[]{:S(2)}) collective-permute-start(bf16[256,1024]{1,0:T(8,128)(2,1)} %get-tuple-element.48), channel_id=1, source_target_pairs={{0,4},{4,0},{8,12},{12,8},{16,20},{20,16},{24,28},{28,24},{1,5},{5... | collective-permute-start | bytes 1572872 | tf_op jit(solution)/shard_map/ppermute | solution.py:528
  450.1 137.0 %collective-permute-start.83 = (bf16[256,1024]{1,0:T(8,128)(2,1)}, bf16[256,1024]{1,0:T(8,128)(2,1)}, u32[]{:S(2)}, u32[]{:S(2)}) collective-permute-start(bf16[256,1024]{1,0:T(8,128)(2,1)} %get-tuple-element.46), channel_id=1, source_target_pairs={{0,4},{4,0},{8,12},{12,8},{16,20},{20,16},{24,28},{28,24},{1,5},{5... | collective-permute-start | bytes 1572872 | tf_op jit(solution)/shard_map/ppermute | solution.py:528
  453.9 52.4 %collective-permute-start.103 = (bf16[32,1536]{1,0:T(8,128)(2,1)S(1)}, bf16[32,1536]{1,0:T(8,128)(2,1)}, u32[]{:S(2)}, u32[]{:S(2)}) collective-permute-start(bf16[32,1536]{1,0:T(8,128)(2,1)S(1)} %get-tuple-element.129), channel_id=1, source_target_pairs={{0,1},{1,2},{2,3},{3,0},{4,5},{5,6},{6,7},{7,4},{8,9},{9,10},{10,1... | collective-permute-start | bytes 294920 | tf_op jit(solution)/shard_map/ppermute | solution.py:497
  533.0 22.4 %collective-permute-start.73 = (bf16[128,1664]{1,0:T(8,128)(2,1)}, bf16[128,1664]{1,0:T(8,128)(2,1)}, u32[]{:S(2)}, u32[]{:S(2)}) collective-permute-start(bf16[128,1664]{1,0:T(8,128)(2,1)} %get-tuple-element.56), channel_id=1, source_target_pairs={{0,4},{4,0},{8,12},{12,8},{16,20},{20,16},{24,28},{28,24},{1,5},{5... | collective-permute-start | bytes 1277960 | tf_op jit(solution)/shard_map/ppermute | solution.py:528
  533.0 22.9 %collective-permute-start.77 = (bf16[128,1664]{1,0:T(8,128)(2,1)}, bf16[128,1664]{1,0:T(8,128)(2,1)}, u32[]{:S(2)}, u32[]{:S(2)}) collective-permute-start(bf16[128,1664]{1,0:T(8,128)(2,1)} %get-tuple-element.54), channel_id=1, source_target_pairs={{0,4},{4,0},{8,12},{12,8},{16,20},{20,16},{24,28},{28,24},{1,5},{5... | collective-permute-start | bytes 1277960 | tf_op jit(solution)/shard_map/ppermute | solution.py:528
  540.3 17.0 %collective-permute-start.74 = (bf16[128,1664]{1,0:T(8,128)(2,1)}, bf16[128,1664]{1,0:T(8,128)(2,1)}, u32[]{:S(2)}, u32[]{:S(2)}) collective-permute-start(bf16[128,1664]{1,0:T(8,128)(2,1)} %get-tuple-element.55), channel_id=1, source_target_pairs={{0,4},{4,0},{8,12},{12,8},{16,20},{20,16},{24,28},{28,24},{1,5},{5... | collective-permute-start | bytes 1277960 | tf_op jit(solution)/shard_map/ppermute | solution.py:528
  551.9 46.8 %collective-permute-start.72 = (bf16[128,1664]{1,0:T(8,128)(2,1)}, bf16[128,1664]{1,0:T(8,128)(2,1)}, u32[]{:S(2)}, u32[]{:S(2)}) collective-permute-start(bf16[128,1664]{1,0:T(8,128)(2,1)} %get-tuple-element.53), channel_id=1, source_target_pairs={{0,4},{4,0},{8,12},{12,8},{16,20},{20,16},{24,28},{28,24},{1,5},{5... | collective-permute-start | bytes 1277960 | tf_op jit(solution)/shard_map/ppermute | solution.py:528
  557.4 21.8 %collective-permute-start.71 = (bf16[256,1024]{1,0:T(8,128)(2,1)}, bf16[256,1024]{1,0:T(8,128)(2,1)S(1)}, u32[]{:S(2)}, u32[]{:S(2)}) collective-permute-start(bf16[256,1024]{1,0:T(8,128)(2,1)} %pad_maximum_fusion.6), channel_id=1, source_target_pairs={{0,3},{1,0},{2,1},{3,2},{4,7},{5,4},{6,5},{7,6},{8,11},{9,8},{10,9... | collective-permute-start | bytes 1572872 | tf_op jit(solution)/shard_map/ppermute | solution.py:486
  564.4 20.5 %collective-permute-start.69 = (bf16[256,1024]{1,0:T(8,128)(2,1)S(1)}, bf16[256,1024]{1,0:T(8,128)(2,1)S(1)}, u32[]{:S(2)}, u32[]{:S(2)}) collective-permute-start(bf16[256,1024]{1,0:T(8,128)(2,1)S(1)} %copy-done.35), channel_id=1, source_target_pairs={{0,1},{1,2},{2,3},{3,0},{4,5},{5,6},{6,7},{7,4},{8,9},{9,10},{10,1... | collective-permute-start | bytes 1572872 | tf_op jit(solution)/shard_map/ppermute | solution.py:485
  (122 other events, 1318.7 us)

commit v2 on v1

--- a/solution.py
+++ b/solution.py
@@ -122,7 +122,7 @@
 
 
 def mixer_forward_kernel(
-    current_ref, before_ref, filter_ref, side_ref, gain_ref,
+    order_ref, current_ref, before_ref, filter_ref, side_ref, gain_ref,
     mixed_ref, solved_ref, update_ref, start_ref, raw_ref, memory_ref, *, heads
 ):
     chunk = pl.program_id(1)
@@ -135,13 +135,13 @@
     gate_at = conv_width
     rate_at = conv_width + heads * DV
     taps = conv_taps(
-        current_ref[0, :, :conv_width], before_ref[0, :, :conv_width], chunk == 0
+        current_ref[:, :conv_width], before_ref[:, :conv_width], chunk == 0
     )
     rows = taps[0].shape[0]
     summed = taps[0] * filter_ref[0:1, :]
     for tap in range(1, 4):
         summed = summed + taps[tap] * filter_ref[tap : tap + 1, :]
-    rate = current_ref[0, :, rate_at : rate_at + LANES].astype(F32)
+    rate = current_ref[:, rate_at : rate_at + LANES].astype(F32)
     strengths = jax.nn.sigmoid(rate)
     shifted, log_decay, running = decay_parts(rate, side_ref[0:1, :], side_ref[1:2, :])
     running_rows = running.T
@@ -165,17 +165,17 @@
         start_ref[0, 0, head] = start
         solved_ref[0, 0, head] = solved.astype(BF16)
         at = head * DV
-        update_ref[0, :, at : at + DV] = update.astype(BF16)
-        raw_ref[0, :, at : at + DV] = raw
-        gate = current_ref[0, :, gate_at + at : gate_at + at + DV].astype(F32)
+        update_ref[:, at : at + DV] = update.astype(BF16)
+        raw_ref[:, at : at + DV] = raw
+        gate = current_ref[:, gate_at + at : gate_at + at + DV].astype(F32)
         normal = raw * lax.rsqrt(jnp.mean(raw * raw, axis=1, keepdims=True) + 1e-05)
-        mixed_ref[0, :, at : at + DV] = (
+        mixed_ref[:, at : at + DV] = (
             normal * gain_ref[...] * (gate * jax.nn.sigmoid(gate))
         ).astype(BF16)
 
 
 def mixer_backward_kernel(
-    current_ref, before_ref, filter_ref, side_ref, gain_ref,
+    order_ref, current_ref, before_ref, filter_ref, side_ref, gain_ref,
     adjoint_ref, solved_ref, update_ref, start_ref, raw_ref,
     grad_ref, filter_sum_ref, side_sum_ref, gain_sum_ref, memory_ref, after_ref, *, heads, chunks
 ):
@@ -196,13 +196,13 @@
     gate_at = conv_width
     rate_at = conv_width + heads * DV
     taps = conv_taps(
-        current_ref[0, :, :conv_width], before_ref[0, :, :conv_width], step == chunks - 1
+        current_ref[:, :conv_width], before_ref[:, :conv_width], step == chunks - 1
     )
     rows = taps[0].shape[0]
     summed = taps[0] * filter_ref[0:1, :]
     for tap in range(1, 4):
         summed = summed + taps[tap] * filter_ref[tap : tap + 1, :]
-    rate = current_ref[0, :, rate_at : rate_at + LANES].astype(F32)
+    rate = current_ref[:, rate_at : rate_at + LANES].astype(F32)
     strengths = jax.nn.sigmoid(rate)
     decay_scale = side_ref[0:1, :]
     shifted, log_decay, running = decay_parts(rate, decay_scale, side_ref[1:2, :])
@@ -223,11 +223,11 @@
         strength = strengths[:, 2 * head : 2 * head + 1]
         scaling = jnp.exp(total)
         at = head * DV
-        raw = raw_ref[0, :, at : at + DV]
-        gate = current_ref[0, :, gate_at + at : gate_at + at + DV].astype(F32)
+        raw = raw_ref[:, at : at + DV]
+        gate = current_ref[:, gate_at + at : gate_at + at + DV].astype(F32)
         gate_sig = jax.nn.sigmoid(gate)
         gate_silu = gate * gate_sig
-        adj_mixed = adjoint_ref[0, :, at : at + DV].astype(F32)
+        adj_mixed = adjoint_ref[:, at : at + DV].astype(F32)
         inv = lax.rsqrt(jnp.mean(raw * raw, axis=1, keepdims=True) + 1e-05)
         normal = raw * inv
         upstream = adj_mixed * gain_ref[...] * gate_silu
@@ -235,12 +235,12 @@
             upstream - normal * jnp.mean(upstream * normal, axis=1, keepdims=True)
         )
         adj_gate = adj_mixed * normal * gain_ref[...] * silu_slope(gate, gate_sig)
-        grad_ref[0, :, gate_at + at : gate_at + at + DV] = adj_gate.astype(BF16)
+        grad_ref[:, gate_at + at : gate_at + at + DV] = adj_gate.astype(BF16)
         gain_sum_ref[...] += jnp.sum(adj_mixed * normal * gate_silu, axis=0, keepdims=True)
 
         start = start_ref[0, 0, head]
         solved = solved_ref[0, 0, head]
-        update = update_ref[0, :, at : at + DV]
+        update = update_ref[:, at : at + DV]
         adj_memory = memory_ref[head]
         tail_decay = jnp.exp(last - total)
         last_decay = jnp.exp(last)
@@ -308,7 +308,7 @@
     adj_log_decay = exact_mm(upper, sum_across - sum_down.T) + sum_last
     adj_shifted = -adj_log_decay * decay_scale * jax.nn.sigmoid(shifted)
     adj_rate = adj_shifted + adj_strength * strengths * (1.0 - strengths)
-    grad_ref[0, :, rate_at : rate_at + LANES] = adj_rate.astype(BF16)
+    grad_ref[:, rate_at : rate_at + LANES] = adj_rate.astype(BF16)
     side_sum_ref[0:1, :] += jnp.sum(adj_log_decay * log_decay, axis=0, keepdims=True)
     side_sum_ref[1:2, :] += jnp.sum(adj_shifted, axis=0, keepdims=True)
 
@@ -321,106 +321,88 @@
     for tap in range(3):
         adj_pre = adj_pre + joined[3 - tap : 3 - tap + rows] * filter_ref[tap : tap + 1, :]
         filter_sum_ref[tap : tap + 1, :] += jnp.sum(adj_summed * taps[tap], axis=0, keepdims=True)
-    grad_ref[0, :, :conv_width] = adj_pre.astype(BF16)
-
-
-def mixer_sizes(projected, heads):
-    seqs, tokens, width = projected.shape
-    rows = min(CHUNK, tokens)
-    conv_width = 2 * heads * DK + heads * DV
-    return seqs, tokens, width, rows, tokens // rows, conv_width
-
-
-def mixer_forward(projected, filters, side, gain, heads):
-    seqs, tokens, width, rows, chunks, conv_width = mixer_sizes(projected, heads)
+    grad_ref[:, :conv_width] = adj_pre.astype(BF16)
+
+
+def mixer_call(kernel, order, heads, rows, seqs, chunks, backward, operands, outs, scratch, name):
     ratio = rows // 16
-    per_row = lambda s, c: (s, c, 0)
-    fixed = lambda s, c: (0, 0)
-    per_chunk = lambda s, c: (s, c, 0, 0, 0)
+    natural = lambda c: chunks - 1 - c if backward else c
+    block = lambda s, c, order_ref: order_ref[s * chunks + natural(c)]
+
+    def before(s, c, order_ref):
+        previous = order_ref[s * chunks + jnp.maximum(natural(c) - 1, 0)]
+        return (previous * ratio + ratio - 1, 0)
+
+    def spec(array):
+        if array.ndim == 5:
+            return pl.BlockSpec(
+                (1, 1) + array.shape[2:], lambda s, c, order_ref: (s, natural(c), 0, 0, 0)
+            )
+        if array.shape[0] == rows * seqs * chunks:
+            return pl.BlockSpec(
+                (rows, array.shape[1]), lambda s, c, order_ref: (block(s, c, order_ref), 0)
+            )
+        return pl.BlockSpec(array.shape, lambda s, c, order_ref: (0, 0))
+
+    in_specs = [spec(operand) for operand in operands]
+    in_specs.insert(1, pl.BlockSpec((16, operands[0].shape[1]), before))
     return pl.pallas_call(
-        functools.partial(mixer_forward_kernel, heads=heads),
-        grid=(seqs, chunks),
-        in_specs=[
-            pl.BlockSpec((1, rows, width), per_row),
-            pl.BlockSpec((1, 16, width), lambda s, c: (s, jnp.maximum(c * ratio - 1, 0), 0)),
-            pl.BlockSpec((4, conv_width), fixed),
-            pl.BlockSpec((8, LANES), fixed),
-            pl.BlockSpec((1, DV), fixed),
-        ],
-        out_specs=[
-            pl.BlockSpec((1, rows, heads * DV), per_row),
-            pl.BlockSpec((1, 1, heads, rows, rows), per_chunk),
-            pl.BlockSpec((1, rows, heads * DV), per_row),
-            pl.BlockSpec((1, 1, heads, DK, DV), per_chunk),
-            pl.BlockSpec((1, rows, heads * DV), per_row),
-        ],
-        out_shape=[
-            jax.ShapeDtypeStruct((seqs, tokens, heads * DV), BF16),
-            jax.ShapeDtypeStruct((seqs, chunks, heads, rows, rows), BF16),
-            jax.ShapeDtypeStruct((seqs, tokens, heads * DV), BF16),
-            jax.ShapeDtypeStruct((seqs, chunks, heads, DK, DV), F32),
-            jax.ShapeDtypeStruct((seqs, tokens, heads * DV), F32),
-        ],
-        scratch_shapes=[pltpu.VMEM((heads, DK, DV), F32)],
+        kernel,
+        grid_spec=pltpu.PrefetchScalarGridSpec(
+            num_scalar_prefetch=1,
+            grid=(seqs, chunks),
+            in_specs=in_specs,
+            out_specs=[spec(out) for out in outs],
+            scratch_shapes=scratch,
+        ),
+        out_shape=outs,
         compiler_params=pltpu.CompilerParams(vmem_limit_bytes=48 * 1024 * 1024),
         cost_estimate=pl.CostEstimate(
-            flops=seqs * chunks * heads * 30 * 2 * rows**3,
-            bytes_accessed=12 * 1024 * 1024,
-            transcendentals=seqs * tokens * width,
+            flops=seqs * chunks * heads * 60 * 2 * rows**3,
+            bytes_accessed=24 * 1024 * 1024,
+            transcendentals=rows * seqs * chunks * 1024,
         ),
-        name="mixer_forward",
-    )(projected, projected, filters, side, gain)
-
-
-def mixer_backward(projected, filters, side, gain, adjoint, saved, heads):
-    seqs, tokens, width, rows, chunks, conv_width = mixer_sizes(projected, heads)
-    ratio = rows // 16
-    solved, update, start, raw = saved
-    per_row = lambda s, c: (s, chunks - 1 - c, 0)
-    fixed = lambda s, c: (0, 0)
-    per_chunk = lambda s, c: (s, chunks - 1 - c, 0, 0, 0)
-    return pl.pallas_call(
+        name=name,
+    )(order, operands[0], *operands)
+
+
+def mixer_forward(projected, filters, side, gain, order, heads, seqs, rows):
+    tokens = projected.shape[0]
+    chunks = tokens // (rows * seqs)
+    shape = jax.ShapeDtypeStruct
+    return mixer_call(
+        functools.partial(mixer_forward_kernel, heads=heads),
+        order, heads, rows, seqs, chunks, False,
+        (projected, filters, side, gain),
+        [
+            shape((tokens, heads * DV), BF16),
+            shape((seqs, chunks, heads, rows, rows), BF16),
+            shape((tokens, heads * DV), BF16),
+            shape((seqs, chunks, heads, DK, DV), F32),
+            shape((tokens, heads * DV), F32),
+        ],
+        [pltpu.VMEM((heads, DK, DV), F32)],
+        "mixer_forward",
+    )
+
+
+def mixer_backward(projected, filters, side, gain, adjoint, saved, order, heads, seqs, rows):
+    tokens = projected.shape[0]
+    chunks = tokens // (rows * seqs)
+    shape = jax.ShapeDtypeStruct
+    return mixer_call(
         functools.partial(mixer_backward_kernel, heads=heads, chunks=chunks),
-        grid=(seqs, chunks),
-        in_specs=[
-            pl.BlockSpec((1, rows, width), per_row),
-            pl.BlockSpec(
-                (1, 16, width),
-                lambda s, c: (s, jnp.maximum((chunks - 1 - c) * ratio - 1, 0), 0),
-            ),
-            pl.BlockSpec((4, conv_width), fixed),
-            pl.BlockSpec((8, LANES), fixed),
-            pl.BlockSpec((1, DV), fixed),
-            pl.BlockSpec((1, rows, heads * DV), per_row),
-            pl.BlockSpec((1, 1, heads, rows, rows), per_chunk),
-            pl.BlockSpec((1, rows, heads * DV), per_row),
-            pl.BlockSpec((1, 1, heads, DK, DV), per_chunk),
-            pl.BlockSpec((1, rows, heads * DV), per_row),
+        order, heads, rows, seqs, chunks, True,
+        (projected, filters, side, gain, adjoint, *saved),
+        [
+            shape(projected.shape, BF16),
+            shape(filters.shape, F32),
+            shape((8, LANES), F32),
+            shape((1, DV), F32),
         ],
-        out_specs=[
-            pl.BlockSpec((1, rows, width), per_row),
-            pl.BlockSpec((4, conv_width), fixed),
-            pl.BlockSpec((8, LANES), fixed),
-            pl.BlockSpec((1, DV), fixed),
-        ],
-        out_shape=[
-            jax.ShapeDtypeStruct((seqs, tokens, width), BF16),
-            jax.ShapeDtypeStruct((4, conv_width), F32),
-            jax.ShapeDtypeStruct((8, LANES), F32),
-            jax.ShapeDtypeStruct((1, DV), F32),
-        ],
-        scratch_shapes=[
-            pltpu.VMEM((heads, DK, DV), F32),
-            pltpu.VMEM((8, conv_width), F32),
-        ],
-        compiler_params=pltpu.CompilerParams(vmem_limit_bytes=48 * 1024 * 1024),
-        cost_estimate=pl.CostEstimate(
-            flops=seqs * chunks * heads * 40 * 2 * rows**3,
-            bytes_accessed=16 * 1024 * 1024,
-            transcendentals=seqs * tokens * width,
-        ),
-        name="mixer_backward",
-    )(projected, projected, filters, side, gain, adjoint, solved, update, start, raw)
+        [pltpu.VMEM((heads, DK, DV), F32), pltpu.VMEM((8, filters.shape[1]), F32)],
+        "mixer_backward",
+    )
 
 
 def shift_pairs(count, by):
@@ -437,24 +419,19 @@
 
 def ring_gather(block, axis):
     count = lax.axis_size(axis)
-    me = lax.axis_index(axis)
-    whole = put_block(jnp.zeros((count,) + block.shape, block.dtype), block, me)
+    found = {0: block}
     right, left = block, block
-    far = count // 2 if count % 2 == 0 else 0
     for hop in range(1, (count - 1) // 2 + 1):
         right = lax.ppermute(right, axis, shift_pairs(count, 1))
         left = lax.ppermute(left, axis, shift_pairs(count, -1))
-        whole = put_block(whole, right, (me - hop) % count)
-        whole = put_block(whole, left, (me + hop) % count)
-    if far:
+        found[count - hop] = right
+        found[hop] = left
+    if count % 2 == 0:
         half = block.shape[0] // 2
         right = lax.ppermute(right[:half], axis, shift_pairs(count, 1))
         left = lax.ppermute(left[half:], axis, shift_pairs(count, -1))
-        whole = put_block(whole, right, (me + far) % count)
-        whole = lax.dynamic_update_slice(
-            whole, left[None], ((me + far) % count, half) + (0,) * (block.ndim - 1)
-        )
-    return whole
+        found[count // 2] = jnp.concatenate([right, left], axis=0)
+    return jnp.concatenate([found[hop] for hop in range(count)], axis=0)
 
 
 def take_block(whole, place):
@@ -463,30 +440,38 @@
 
 def ring_reduce(whole, axis):
     count = lax.axis_size(axis)
-    me = lax.axis_index(axis)
-    total = take_block(whole, me)
+    blocks = whole.reshape((count, whole.shape[0] // count) + whole.shape[1:])
+    total = blocks[0]
     if count == 1:
-        return total
+        return total, total
     half = total.shape[0] // 2
-    reach = (count - 1) // 2
+    first = total
+    move = lambda part, by: lax.ppermute(
+        part.astype(BF16), axis, shift_pairs(count, by)
+    ).astype(F32)
     right = left = None
     if count % 2 == 0:
-        far = take_block(whole, (me + count // 2) % count)
-        right = lax.ppermute(far[:half].astype(BF16), axis, shift_pairs(count, 1)).astype(F32)
-        left = lax.ppermute(far[half:].astype(BF16), axis, shift_pairs(count, -1)).astype(F32)
-    for hop in range(reach, 0, -1):
-        ahead = take_block(whole, (me + hop) % count)
-        behind = take_block(whole, (me - hop) % count)
+        far = blocks[count // 2]
+        right, left = move(far[:half], 1), move(far[half:], -1)
+        first = right
+    for hop in range((count - 1) // 2, 0, -1):
+        ahead, behind = blocks[hop], blocks[count - hop]
         if right is not None and right.shape[0] == half:
             ahead = jnp.concatenate([ahead[:half] + right, ahead[half:]], axis=0)
             behind = jnp.concatenate([behind[:half], behind[half:] + left], axis=0)
         elif right is not None:
             ahead, behind = ahead + right, behind + left
-        right = lax.ppermute(ahead.astype(BF16), axis, shift_pairs(count, 1)).astype(F32)
-        left = lax.ppermute(behind.astype(BF16), axis, shift_pairs(count, -1)).astype(F32)
+        right, left = move(ahead, 1), move(behind, -1)
     if right.shape[0] == half:
-        return total + jnp.concatenate([right, left], axis=0)
-    return total + right + left
+        return total + jnp.concatenate([right, left], axis=0), first
+    return total + right + left, first
+
+
+def hand_out(blocks, axis, by):
+    count = lax.axis_size(axis)
+    return [blocks[0]] + [
+        lax.ppermute(blocks[hop], axis, shift_pairs(count, hop * by)) for hop in range(1, count)
+    ]
 
 
 def exchange(whole, axis):
@@ -501,42 +486,8 @@
     return result
 
 
-def plane_gather(block):
-    count = lax.axis_size("dp")
-    if count != 8:
-        return lax.all_gather(block, "dp", axis=0, tiled=False)
-    me = lax.axis_index("dp")
-    half = block.shape[0] // 2
-    swap = lambda part, mask: lax.ppermute(part, "dp", swap_pairs(8, mask))
-    near_two, near_four = swap(block, 2), swap(block, 4)
-    far = jnp.concatenate([swap(near_two[:half], 4), swap(near_four[half:], 2)], axis=0)
-    whole = jnp.zeros((8,) + block.shape, block.dtype)
-    for mask, part in ((0, block), (2, near_two), (4, near_four), (6, far)):
-        whole = put_block(whole, part, me ^ mask)
-        whole = put_block(whole, swap(part, 1), me ^ mask ^ 1)
-    return whole
-
-
-def plane_reduce(whole):
-    count = lax.axis_size("dp")
-    if count != 8:
-        return lax.psum_scatter(
-            whole.astype(BF16), "dp", scatter_dimension=0, tiled=False
-        ).astype(F32)
-    me = lax.axis_index("dp")
-    half = whole.shape[1] // 2
-    swap = lambda part, mask: lax.ppermute(part.astype(BF16), "dp", swap_pairs(8, mask)).astype(
-        F32
-    )
-    lane = {
-        mask: take_block(whole, me ^ mask) + swap(take_block(whole, me ^ mask ^ 1), 1)
-        for mask in (6, 2, 4, 0)
-    }
-    via_four = swap(lane[6][:half], 4)
-    via_two = swap(lane[6][half:], 2)
-    to_two = jnp.concatenate([lane[2][:half] + via_four, lane[2][half:]], axis=0)
-    to_four = jnp.concatenate([lane[4][:half], lane[4][half:] + via_two], axis=0)
-    return lane[0] + swap(to_two, 2) + swap(to_four, 4)
+def after(values, *others):
+    return lax.optimization_barrier((values, *others))[0]
 
 
 def sum_everywhere(values):
@@ -635,14 +586,6 @@
     hidden_own = hidden // ns
     padded = round_up(hidden_own, LANES)
 
-    def to_pieces(values):
-        cut = values.reshape((seqs, ns, piece) + values.shape[1:])
-        return jnp.swapaxes(cut, 0, 1).reshape((ns, own) + values.shape[1:])
-
-    def from_pieces(values):
-        cut = values.reshape((ns, seqs, piece) + values.shape[2:])
-        return jnp.swapaxes(cut, 0, 1).reshape((tokens,) + values.shape[2:])
-
     flat_in = inputs.reshape(own, width)
     flat_cot = cotangent.reshape(own, width)
     mixer_local = jnp.concatenate(
@@ -650,23 +593,39 @@
         + [pad_last(by_heads(rate_proj, ns), LANES)],
         axis=2,
     )
+    all_in = ring_gather(flat_in, "seq")
     mixer_rows = exchange(mixer_local, "seq").reshape(ns * rows, mixer_local.shape[2])
-    mixer_weight = plane_gather(mixer_rows).reshape(width, mixer_local.shape[2])
-    all_in = from_pieces(ring_gather(flat_in, "seq"))
-    out_rows = ring_gather(output_proj, "seq").reshape(ns * output_proj.shape[0], width)
-    out_weight = plane_gather(out_rows).reshape(H * DV, width)
+    mixer_weight = lax.all_gather(mixer_rows, "dp", axis=0, tiled=True)
     ffn_local = jnp.concatenate(
         [hidden_out(ffn_gate, nd, ns, padded), hidden_out(ffn_up, nd, ns, padded)], axis=2
     )
-    ffn_rows = exchange(ffn_local, "seq").reshape(ns * rows, 2 * padded)
-    ffn_weight = plane_gather(ffn_rows).reshape(width, 2 * padded)
-    down_weight = plane_gather(ffn_down).reshape(hidden_own, width)
+    out_local = after(output_proj, all_in)
+    out_here = jnp.zeros((ns,) + output_proj.shape, BF16)
+    for hop, rows_there in enumerate(hand_out([out_local] * ns, "seq", 1)):
+        out_here = put_block(out_here, rows_there, (me - hop) % ns)
+    out_rows = ns * output_proj.shape[0]
+    both = jnp.concatenate([out_here.reshape(out_rows, width), ffn_down], axis=0)
+    both = lax.all_gather(both, "dp", axis=0, tiled=False)
+    out_weight = both[:, :out_rows].reshape(ns, kv, width)
+    turned = jnp.concatenate([take_block(out_weight, (me - hop) % ns) for hop in range(ns)], axis=0)
+    down_weight = both[:, out_rows:].reshape(hidden_own, width)
     down_weight = jnp.pad(down_weight, ((0, padded - hidden_own), (0, 0)))
-    all_cot = from_pieces(ring_gather(flat_cot, "seq"))
-
+    ffn_rows = exchange(after(ffn_local, out_here), "seq").reshape(ns * rows, 2 * padded)
+    ffn_weight = lax.all_gather(ffn_rows, "dp", axis=0, tiled=True)
+
+    chunk_rows = min(CHUNK, piece)
+    per_piece = piece // chunk_rows
+    order = jnp.stack(
+        [
+            (((part - me) % ns) * seqs + row) * per_piece + within
+            for row in range(seqs)
+            for part in range(ns)
+            for within in range(per_piece)
+        ]
+    ).astype(jnp.int32)
     unit_in, scale_in = rms_parts(all_in.astype(F32))
     normed = (unit_in * mixer_gain).astype(BF16)
-    projected = dot(normed, mixer_weight).astype(BF16).reshape(seqs, ns * piece, -1)
+    projected = dot(normed, mixer_weight).astype(BF16)
     own_cols = lambda table, size: lax.dynamic_slice_in_dim(table, me * size, size, 1)
     filters = jnp.concatenate(
         [own_cols(query_filter, kq), own_cols(key_filter, kq), own_cols(value_filter, kv)], axis=1
@@ -680,54 +639,81 @@
         [spread(own_decay), spread(own_bias), jnp.zeros((6, LANES), F32)], axis=0
     )
     gain_row = head_gain.reshape(1, DV)
-    mixed, *saved = mixer_forward(projected, filters, side, gain_row, heads)
-    mixed_pieces = exchange(to_pieces(mixed.reshape(tokens, kv)), "seq")
-    mixed_low = jnp.swapaxes(mixed_pieces, 0, 1).reshape(own, H * DV)
-
-    middle = flat_in.astype(F32) + dot(mixed_low, out_weight)
+    mixed, *saved = mixer_forward(
+        projected, filters, side, gain_row, order, heads, seqs, chunk_rows
+    )
+    all_cot = jnp.concatenate(hand_out([after(flat_cot, projected)] * ns, "seq", -1), axis=0)
+    mixed = after(mixed, all_cot)
+    mixed_parts = hand_out(mixed.reshape(ns, own, kv), "seq", 1)
+    mixed_low = jnp.concatenate(mixed_parts, axis=1)
+
+    middle = flat_in.astype(F32) + dot(mixed_low, turned)
     unit_two, scale_two = rms_parts(middle)
-    second_all = from_pieces(ring_gather((unit_two * ffn_gain).astype(BF16), "seq"))
+    second_all = ring_gather((unit_two * ffn_gain).astype(BF16), "seq")
     hidden_both = dot(second_all, ffn_weight)
     hidden_gate, hidden_up = hidden_both[:, :padded], hidden_both[:, padded:]
     gate_sig = jax.nn.sigmoid(hidden_gate)
     gate_silu = hidden_gate * gate_sig
     active = (gate_silu * hidden_up).astype(BF16)
-    block_sum = ring_reduce(to_pieces(dot(active, down_weight)), "seq")
-    block_out = (middle + block_sum).astype(BF16).reshape(inputs.shape)
-
     adj_act = dot_nt(all_cot, down_weight)
     adj_gate = adj_act * hidden_up * silu_slope(hidden_gate, gate_sig)
     adj_both = jnp.concatenate(
         [adj_gate.astype(BF16), (adj_act * gate_silu).astype(BF16)], axis=1
     )
-    adj_second = ring_reduce(to_pieces(dot_nt(adj_both, ffn_weight)), "seq")
-    grad_down = dot_tn(active, all_cot)[:hidden_own].reshape(nd, -1, width)
-    grad_ffn = dot_tn(second_all, adj_both).reshape(nd, ns * rows, 2 * padded)
-    down_out = plane_reduce(grad_down).astype(BF16)
-    ffn_parts = exchange(plane_reduce(grad_ffn).astype(BF16).reshape(ns, rows, -1), "seq")
-    ffngate_out = hidden_back(ffn_parts[:, :, :padded], nd, hidden)
-    ffnup_out = hidden_back(ffn_parts[:, :, padded:], nd, hidden)
+    adj_partial_two = dot_nt(adj_both, ffn_weight)
+    adj_second, first_in = ring_reduce(adj_partial_two, "seq")
+    scatter = lambda grad: lax.psum_scatter(
+        grad.astype(BF16), "dp", scatter_dimension=0, tiled=True
+    )
+    active_late, adj_both_late = after((active, adj_both), first_in)
+    ffn_sums = scatter(dot_tn(second_all, adj_both_late))
+    grad_down = dot_tn(active_late, all_cot)[:hidden_own].astype(BF16)
 
     gain_two = jnp.sum(adj_second * unit_two, axis=0)
     adj_middle = flat_cot.astype(F32) + rms_back(unit_two, scale_two, ffn_gain, adj_second)
     attn_low = adj_middle.astype(BF16)
-    adj_mixed = dot_nt(attn_low, out_weight).astype(BF16)
-    adj_heads = from_pieces(
-        exchange(jnp.swapaxes(adj_mixed.reshape(own, ns, kv), 0, 1), "seq")
-    ).reshape(seqs, ns * piece, kv)
-    grad_out = dot_tn(mixed_low, attn_low).reshape(nd, -1, width)
-    grad_out = plane_reduce(grad_out)
-    out_out = ring_reduce(grad_out.reshape(ns, -1, width), "seq").astype(BF16)
+    adj_mixed = dot_nt(attn_low, turned).astype(BF16)
+    adj_heads = jnp.concatenate(
+        hand_out([adj_mixed[:, hop * kv : (hop + 1) * kv] for hop in range(ns)], "seq", -1), axis=0
+    )
+    active_late = after(active, adj_mixed)
+    block_parts = dot(active_late, down_weight).reshape(ns, own, width)
+    mixed_stack = jnp.stack(mixed_parts)
+    mixed_natural = jnp.concatenate(
+        [take_block(mixed_stack, (me - part) % ns) for part in range(ns)], axis=1
+    )
+    grad_out = dot_tn(mixed_natural, after(attn_low, adj_mixed)).astype(BF16)
+    both_grads = jnp.concatenate(
+        [grad_out.reshape(nd, out_rows, width), grad_down.reshape(nd, -1, width)], axis=1
+    ).reshape(-1, width)
+    both_sums = scatter(both_grads)
+    adj_heads = after(adj_heads, both_grads)
+    block_low = after(block_parts[1:].astype(BF16), adj_heads)
+    block_in = hand_out(
+        [block_parts[0]] + [block_low[hop] for hop in range(ns - 1)], "seq", 1
+    )
+    block_sum = sum(part.astype(F32) for part in block_in[1:]) + block_in[0]
+    block_out = (middle + block_sum).astype(BF16).reshape(inputs.shape)
+    down_out = both_sums[out_rows:]
+    out_sums = both_sums[:out_rows].reshape(ns, -1, width)
+    out_out = take_block(out_sums, me).astype(F32)
+    out_blocks = [take_block(out_sums, (me + hop) % ns) for hop in range(ns)]
+    for part in hand_out(out_blocks, "seq", 1)[1:]:
+        out_out = out_out + part.astype(F32)
+    out_out = out_out.astype(BF16)
+    ffn_parts = exchange(ffn_sums.reshape(ns, rows, -1), "seq")
+    ffngate_out = hidden_back(ffn_parts[:, :, :padded], nd, hidden)
+    ffnup_out = hidden_back(ffn_parts[:, :, padded:], nd, hidden)
 
     adj_projected, filter_sum, side_sum, gain_sum = mixer_backward(
-        projected, filters, side, gain_row, adj_heads, saved, heads
-    )
-    adj_projected = adj_projected.reshape(tokens, -1)
+        projected, filters, side, gain_row, adj_heads, saved, order, heads, seqs, chunk_rows
+    )
+    adj_projected = after(adj_projected, block_in[1], block_in[-1])
     adj_partial = dot_nt(adj_projected, mixer_weight)
     gain_one = jnp.sum(adj_partial * unit_in, axis=0)
-    adj_normed = ring_reduce(to_pieces(adj_partial), "seq")
-    grad_mixer = dot_tn(normed, adj_projected).reshape(nd, ns * rows, -1)
-    mixer_parts = exchange(plane_reduce(grad_mixer).astype(BF16).reshape(ns, rows, -1), "seq")
+    adj_normed, first_in = ring_reduce(adj_partial, "seq")
+    grad_mixer = dot_tn(normed, after(adj_projected, first_in)).astype(BF16)
+    mixer_parts = exchange(scatter(grad_mixer).reshape(ns, rows, -1), "seq")
     whole_rows = lambda parts: jnp.swapaxes(parts, 0, 1).reshape(rows, -1)
     query_out = whole_rows(mixer_parts[:, :, :kq])
     key_out = whole_rows(mixer_parts[:, :, kq : 2 * kq])

time: 628 us -> 493 us (0.79)
  local copies, waits for them, and re-layouts: 118 us -> 52.2 us
  waiting for transfers between devices: 229 us -> 185 us
  starting transfers between devices: 133 us -> 90.7 us
  between operations: 3.03 us -> 15.9 us
    dynamic_update_slice x68 -> x17, local copies, waits for them, and re-layouts: 40.2 us -> 1.16 us  [put_block(): lax.dynamic_update_slice(whole, block[None], (place,) + (0,) * block.ndim)]
    ppermute x80 -> x26, waiting for transfers between devices: 140 us -> 101 us  [the longest x18 73.5 us: hand_out(): lax.ppermute(blocks[hop], axis, shift_pairs(count, hop * by))]
    ppermute x18 -> x12, waiting for transfers between devices: 51.5 us -> 20 us  [exchange(): lax.ppermute(take_block(whole, (me + hop) % count), axis, shift_pairs(cou...]
    ppermute x80 -> x26, starting transfers between devices: 62.7 us -> 40.2 us  [the longest x18 23.4 us: hand_out(): lax.ppermute(blocks[hop], axis, shift_pairs(count, hop * by))]
    ppermute x4 -> x2, waiting for transfers between devices: 9.27 us -> 24.1 us  [ring_gather(): right = lax.ppermute(right, axis, shift_pairs(count, 1))]
    another operation x19 -> x8, local copies, waits for them, and re-layouts: 14 us -> 0.13 us
    add x6 -> x0, other arithmetic: 9.98 us -> none  [the longest x4 5.56 us: plane_reduce(): take_block(whole, me ^ mask) + swap(take_block(whole, me ^ mask ^ 1), 1)]
    ppermute x4 -> x2, starting transfers between devices: 10.7 us -> 1.12 us  [ring_gather(): left = lax.ppermute(left, axis, shift_pairs(count, -1))]
  transfers between devices with their start and end apart: 119 -> 57, of which waited for: 62 -> 35; matrix products, arithmetic and copies ran while one was open for 27% -> 22% of each run, Pallas kernels for 10% -> 12%
where the time goes in v2:
time: 493 us; the launch traced here: 486 us
  waiting for transfers between devices  185 us (38%)
  starting transfers between devices  90.7 us (18%)
  Pallas kernels  60.2 us (12%)
  matrix products  56.8 us (12%)
  local copies, waits for them, and re-layouts  52.2 us (11%)
  other arithmetic  25.1 us (5%)
  between operations  15.9 us (3%)
    ppermute x18, waiting for transfers between devices, hand_out(): lax.ppermute(blocks[hop], axis, shift_pairs(count, hop * by))  73.5 us
    pallas_call x2, Pallas kernels, mixer_call(): pl.pallas_call(kernel, grid_spec=pltpu.PrefetchScalarGridSpec(num_scalar_...  60.2 us
    ppermute x8, waiting for transfers between devices, ring_reduce(): lax.ppermute(part.astype(BF16), axis, shift_pairs(count, by)).astype(F32)  27.8 us
    ppermute x12, starting transfers between devices, exchange(): lax.ppermute(take_block(whole, (me + hop) % count), axis, shift_pairs(cou...  24.7 us
    ppermute x2, waiting for transfers between devices, ring_gather(): right = lax.ppermute(right, axis, shift_pairs(count, 1))  24.1 us
    ppermute x18, starting transfers between devices, hand_out(): lax.ppermute(blocks[hop], axis, shift_pairs(count, hop * by))  23.4 us
    dot_general x4, matrix products, dot_nt(): return jnp.einsum('tc,dc->td', left, right, preferred_element_type=F32)  21.5 us
    ppermute x12, waiting for transfers between devices, exchange(): lax.ppermute(take_block(whole, (me + hop) % count), axis, shift_pairs(cou...  20 us
  transfers between devices with their start and end apart: 57, of which 35 were waited for; matrix products, arithmetic and copies ran while one was open for 22% of the time, Pallas kernels for 12%

profile of v2, /device:TPU:0, one launch (start us, length us, event | category | flops | bytes accessed | tf_op | source)
XLA Modules:
  0.0 485.9 jit_solution(7136009475088989234)
XLA Ops:
  13.1 3.1 collective-permute-start.4
  22.1 3.8 collective-permute-done.5
  30.6 12.8 %collective-permute-done.1 = bf16[256,1024]{1,0:T(8,128)(2,1)S(1)} collective-permute-done((bf16[256,1024]{1,0:T(8,128)(2,1)S(1)}, bf16[256,1024]{1,0:T(8,128)(2,1)S(1)}, u32[]{:S(2)}, u32[]{:S(2)}) %collective-permute-start.1) | collective-permute-done | bytes 524320 | tf_op jit(solution)/shard_map/ppermute | solution.py:425
  45.0 9.6 %collective-permute-done = bf16[256,1024]{1,0:T(8,128)(2,1)S(1)} collective-permute-done((bf16[256,1024]{1,0:T(8,128)(2,1)S(1)}, bf16[256,1024]{1,0:T(8,128)(2,1)S(1)}, u32[]{:S(2)}, u32[]{:S(2)}) %collective-permute-start) | collective-permute-done | bytes 524320 | tf_op jit(solution)/shard_map/ppermute | solution.py:426
  55.5 2.8 collective-permute-start.3
  60.3 4.7 collective-permute-done.3
  66.7 2.8 collective-permute-start.14
  70.9 3.7 collective-permute-done.13
  74.6 4.3 collective-permute-done.14
  92.5 2.9 collective-permute-done.21
  96.3 7.6 %convolution_convert_fusion.2.current_ref.before_ref = bf16[1024,1664]{1,0:T(8,128)(2,1)} fusion(bf16[1024,1664]{1,0:T(8,128)(2,1)} %all-gather.5.cloned.1.call-done, bf16[1024,1024]{1,0:T(8,128)(2,1)S(1)} %constant_dynamic-update-slice_fusion, f32[1024]{0:T(1024)S(1)} %copy-done.49, f32[1024]{0:T(1024)S(1)} %add_rsqrt_fusion), kind=kOutput, calls=%fused_computation.11 | convolution fusion | flops 3495559168 | bytes 8921088 | tf_op jit(solution)/shard_map/dot_general | solution.py:521
  103.9 3.2 collective-permute-start.7
  108.1 33.3 %mixer_forward.1 = (bf16[1024,512]{1,0:T(8,128)(2,1)S(1)}, bf16[1,4,2,256,256]{4,3,2,1,0:T(8,128)(2,1)S(1)}, bf16[1024,512]{1,0:T(8,128)(2,1)S(1)}, f32[1,4,2,128,256]{4,3,2,1,0:T(8,128)S(1)}, f32[1024,512]{1,0:T(8,128)}) custom-call(s32[4]{0:T(128)S(1)} %pad_add_fusion.order_ref, bf16[1024,1664]{1,0:T(8,128)(2,1)} %convolution_convert_fusion.2.current_ref.before_ref, ...), custom_call_target="tpu_custom_call" | custom-call | flops 16106127360 | bytes 25165824 | tf_op jit(solution)/shard_map/mixer_forward/pallas_call | solution.py:349
  141.6 11.9 %collective-permute-done.8 = bf16[256,1024]{1,0:T(8,128)(2,1)S(1)} collective-permute-done((bf16[256,1024]{1,0:T(8,128)(2,1)S(1)}, bf16[256,1024]{1,0:T(8,128)(2,1)S(1)}, u32[]{:S(2)}, u32[]{:S(2)}) %collective-permute-start.8) | collective-permute-done | bytes 524320 | tf_op jit(solution)/shard_map/ppermute | solution.py:473
  155.0 3.3 collective-permute-start.12
  161.5 4.1 collective-permute-done.10
  165.6 9.7 %collective-permute-done.11 = bf16[256,512]{1,0:T(8,128)(2,1)} collective-permute-done((bf16[256,512]{1,0:T(8,128)(2,1)S(1)}, bf16[256,512]{1,0:T(8,128)(2,1)}, u32[]{:S(2)}, u32[]{:S(2)}) %collective-permute-start.11) | collective-permute-done | bytes 262176 | tf_op jit(solution)/shard_map/ppermute | solution.py:473
  179.1 5.1 %collective-permute-start.17 = (bf16[256,1024]{1,0:T(8,128)(2,1)S(1)}, bf16[256,1024]{1,0:T(8,128)(2,1)S(1)}, u32[]{:S(2)}, u32[]{:S(2)}) collective-permute-start(bf16[256,1024]{1,0:T(8,128)(2,1)S(1)} %get-tuple-element.66), channel_id=1, source_target_pairs={{0,1},{1,2},{2,3},{3,0},{4,5},{5,6},{6,7},{7,4},{8,9},{9,10},{10,1... | collective-permute-start | bytes 1572872 | tf_op jit(solution)/shard_map/ppermute | solution.py:425
  185.4 11.3 %collective-permute-done.17 = bf16[256,1024]{1,0:T(8,128)(2,1)S(1)} collective-permute-done((bf16[256,1024]{1,0:T(8,128)(2,1)S(1)}, bf16[256,1024]{1,0:T(8,128)(2,1)S(1)}, u32[]{:S(2)}, u32[]{:S(2)}) %collective-permute-start.17) | collective-permute-done | bytes 524320 | tf_op jit(solution)/shard_map/ppermute | solution.py:425
  199.2 8.7 %collective-permute-done.16 = bf16[256,1024]{1,0:T(8,128)(2,1)S(1)} collective-permute-done((bf16[256,1024]{1,0:T(8,128)(2,1)S(1)}, bf16[256,1024]{1,0:T(8,128)(2,1)S(1)}, u32[]{:S(2)}, u32[]{:S(2)}) %collective-permute-start.16) | collective-permute-done | bytes 524320 | tf_op jit(solution)/shard_map/ppermute | solution.py:426
  207.9 4.6 collective-permute-start.19
  219.3 6.1 %fusion.67 = f32[1024,1536]{1,0:T(8,128)S(1)} fusion(bf16[1024,1024]{1,0:T(8,128)(2,1)} %constant_dynamic-update-slice_fusion.10, bf16[1024,1536]{1,0:T(8,128)(2,1)} %all-gather.7.cloned.1.call-done), kind=kOutput, calls=%fused_computation.217 | convolution fusion | flops 3221225472 | bytes 11534336 | tf_op jit(solution)/shard_map/dot_general | solution.py:521
  225.4 3.7 multiply_convert_fusion.1
  231.7 3.4 fusion.66
  235.8 3.3 collective-permute-start.25
  241.0 5.4 %collective-permute-done.23 = bf16[128,1024]{1,0:T(8,128)(2,1)S(1)} collective-permute-done((bf16[128,1024]{1,0:T(8,128)(2,1)S(1)}, bf16[128,1024]{1,0:T(8,128)(2,1)S(1)}, u32[]{:S(2)}, u32[]{:S(2)}) %collective-permute-start.23) | collective-permute-done | bytes 262176 | tf_op jit(solution)/shard_map/ppermute | solution.py:449
  251.7 2.9 collective-permute-start.26
  254.6 6.6 %convolution_convert_fusion.3 = bf16[1024,1536]{1,0:T(8,128)(2,1)} fusion(bf16[1024,1024]{1,0:T(8,128)(2,1)} %constant_dynamic-update-slice_fusion.10, bf16[1024,1536]{1,0:T(8,128)(2,1)S(1)} %pad_maximum_fusion.2), kind=kOutput, calls=%fused_computation.12 | convolution fusion | flops 3222798336 | bytes 8388608 | tf_op jit(solution)/shard_map/tr,tc->rc/dot_general | solution.py:529
  261.8 5.2 %collective-permute-done.24 = bf16[256,1024]{1,0:T(8,128)(2,1)} collective-permute-done((bf16[256,1024]{1,0:T(8,128)(2,1)}, bf16[256,1024]{1,0:T(8,128)(2,1)}, u32[]{:S(2)}, u32[]{:S(2)}) %collective-permute-start.24) | collective-permute-done | bytes 524320 | tf_op jit(solution)/shard_map/ppermute | solution.py:449
  267.0 8.6 %collective-permute-done.26 = bf16[256,1024]{1,0:T(8,128)(2,1)} collective-permute-done((bf16[256,1024]{1,0:T(8,128)(2,1)}, bf16[256,1024]{1,0:T(8,128)(2,1)}, u32[]{:S(2)}, u32[]{:S(2)}) %collective-permute-start.26) | collective-permute-done | bytes 524320 | tf_op jit(solution)/shard_map/ppermute | solution.py:449
  277.7 3.1 fusion.59
  280.9 6.3 %convolution_convert_fusion.4 = bf16[256,2048]{1,0:T(8,128)(2,1)S(1)} fusion(bf16[256,1024]{1,0:T(8,128)(2,1)S(1)} %get-tuple-element.46, bf16[512,1024]{1,0:T(8,128)(2,1)S(1)} %copy-done.27, bf16[512,1024]{1,0:T(8,128)(2,1)S(1)} %copy-done.29, bf16[512,1024]{1,0:T(8,128)(2,1)S(1)} %copy-done.31, bf16[512,1024]{1,0:T(8,128)(2,1)S(1)} %copy-done.25), kind=kOutput, calls=%fused_computation.21 | convolution fusion | flops 1091043328 | bytes 5767168 | tf_op jit(solution)/shard_map/tc,dc->td/dot_general | solution.py:525
  296.2 3.3 pad_maximum_fusion
  299.5 13.9 %collective-permute-done.28 = bf16[256,512]{1,0:T(8,128)(2,1)} collective-permute-done((bf16[256,512]{1,0:T(8,128)(2,1)}, bf16[256,512]{1,0:T(8,128)(2,1)}, u32[]{:S(2)}, u32[]{:S(2)}) %collective-permute-start.28) | collective-permute-done | bytes 262176 | tf_op jit(solution)/shard_map/ppermute | solution.py:473
  317.0 4.0 collective-permute-start.32
  321.0 26.9 %mixer_backward.1 = (bf16[1024,1664]{1,0:T(8,128)(2,1)}, f32[4,1024]{1,0:T(4,128)S(1)}, f32[8,128]{1,0:T(8,128)S(1)}, f32[1,256]{1,0:T(1,128)S(1)}) custom-call(s32[4]{0:T(128)S(1)} %pad_add_fusion.order_ref, bf16[1024,1664]{1,0:T(8,128)(2,1)} %convolution_convert_fusion.2.current_ref.before_ref, ...), custom_call_target="tpu_custom_call" | custom-call | flops 16106127360 | bytes 25165824 | tf_op jit(solution)/shard_map/mixer_backward/pallas_call | solution.py:349
  348.8 7.6 %convolution_convert_fusion = bf16[1024,1664]{1,0:T(8,128)(2,1)} fusion(bf16[1024,1664]{1,0:T(8,128)(2,1)} %get-tuple-element.56, bf16[1024,1024]{1,0:T(8,128)(2,1)S(1)} %copy-done.13, f32[1024]{0:T(1024)S(1)} %copy-done.49, f32[1024]{0:T(1024)S(1)} %add_rsqrt_fusion), kind=kOutput, calls=%fused_computation.9 | convolution fusion | flops 3495559168 | bytes 8921088 | tf_op jit(solution)/shard_map/tr,tc->rc/dot_general | solution.py:529
  358.1 8.0 %fusion.3 = (f32[1024]{0:T(1024)S(1)}, bf16[1024,1024]{1,0:T(8,128)(2,1)S(1)}, f32[1024,1024]{1,0:T(8,128)S(1)}) fusion(bf16[1024,1024]{1,0:T(8,128)(2,1)} %copy-done.12, f32[1024]{0:T(1024)S(1)} %add_rsqrt_fusion, bf16[1024,1664]{1,0:T(8,128)(2,1)} %get-tuple-element.56, bf16[1024,1664]{1,0:T(8,128)(2,1)} %all-gather.5.cloned.1.call-done), kind=kOutput, calls=%fused_computation.6 | convolution fusion | flops 3494902784 | bytes 15212544 | tf_op jit(solution)/shard_map/tc,dc->td/dot_general | solution.py:525
  369.4 4.0 collective-permute-start.35
  375.0 20.8 %collective-permute-done.31 = bf16[256,1024]{1,0:T(8,128)(2,1)S(1)} collective-permute-done((bf16[256,1024]{1,0:T(8,128)(2,1)S(1)}, bf16[256,1024]{1,0:T(8,128)(2,1)S(1)}, u32[]{:S(2)}, u32[]{:S(2)}) %collective-permute-start.31) | collective-permute-done | bytes 524320 | tf_op jit(solution)/shard_map/ppermute | solution.py:473
  398.7 3.5 collective-permute-start.34
  406.9 11.3 %collective-permute-done.50 = f32[148,128]{1,0:T(8,128)S(1)} collective-permute-done((f32[148,128]{1,0:T(8,128)S(1)}, f32[148,128]{1,0:T(8,128)S(1)}, u32[]{:S(2)}, u32[]{:S(2)}) %collective-permute-start.50) | collective-permute-done | bytes 75808 | tf_op jit(solution)/shard_map/ppermute | solution.py:501
  421.7 5.9 %collective-permute-done.36 = bf16[256,1024]{1,0:T(8,128)(2,1)S(1)} collective-permute-done((bf16[256,1024]{1,0:T(8,128)(2,1)}, bf16[256,1024]{1,0:T(8,128)(2,1)S(1)}, u32[]{:S(2)}, u32[]{:S(2)}) %collective-permute-start.36) | collective-permute-done | bytes 524320 | tf_op jit(solution)/shard_map/ppermute | solution.py:449
  430.4 5.2 %collective-permute-start.43 = (bf16[32,1536]{1,0:T(8,128)(2,1)S(1)}, bf16[32,1536]{1,0:T(8,128)(2,1)S(1)}, u32[]{:S(2)}, u32[]{:S(2)}) collective-permute-start(bf16[32,1536]{1,0:T(8,128)(2,1)S(1)} %get-tuple-element.123), channel_id=1, source_target_pairs={{0,1},{1,2},{2,3},{3,0},{4,5},{5,6},{6,7},{7,4},{8,9},{9,10},{10,1... | collective-permute-start | bytes 294920 | tf_op jit(solution)/shard_map/ppermute | solution.py:482
  438.2 3.3 collective-permute-start.44
  450.5 3.4 collective-permute-start.38
  454.4 3.5 collective-permute-done.38
  473.6 4.5 collective-permute-done.41
  (362 shorter events, 133.0 us)
Async XLA Ops:
  7.2 89.1 %all-gather.5.cloned.1.call-start = ((), (), s32[]{:S(2)}) async-start(), calls=%async_computation.3 | async-start | bytes 3833856 | tf_op jit(solution)/shard_map/all_gather | solution.py:598
  13.1 9.0 %collective-permute-start.4 = (bf16[32,1664]{1,0:T(8,128)(2,1)S(1)}, bf16[32,1664]{1,0:T(8,128)(2,1)S(1)}, u32[]{:S(2)}, u32[]{:S(2)}) collective-permute-start(bf16[32,1664]{1,0:T(8,128)(2,1)S(1)} %bitcast.249), channel_id=1, source_target_pairs={{0,1},{1,2},{2,3},{3,0},{4,5},{5,6},{6,7},{7,4},{8,9},{9,10},{10,1... | collective-permute-start | bytes 319496 | tf_op jit(solution)/shard_map/ppermute | solution.py:482
  16.2 9.7 %collective-permute-start.5 = (bf16[32,1664]{1,0:T(8,128)(2,1)S(1)}, bf16[32,1664]{1,0:T(8,128)(2,1)S(1)}, u32[]{:S(2)}, u32[]{:S(2)}) collective-permute-start(bf16[32,1664]{1,0:T(8,128)(2,1)S(1)} %bitcast.248), channel_id=1, source_target_pairs={{0,2},{1,3},{2,0},{3,1},{4,6},{5,7},{6,4},{7,5},{8,10},{9,11},{10,... | collective-permute-start | bytes 319496 | tf_op jit(solution)/shard_map/ppermute | solution.py:482
  26.7 131.6 %all-gather.9.cloned.1.call-start = ((), (), s32[]{:S(2)}) async-start(), calls=%async_computation.8 | async-start | bytes 6340608 | tf_op jit(solution)/shard_map/all_gather | solution.py:608
  26.8 16.7 %collective-permute-start.1 = (bf16[256,1024]{1,0:T(8,128)(2,1)S(1)}, bf16[256,1024]{1,0:T(8,128)(2,1)S(1)}, u32[]{:S(2)}, u32[]{:S(2)}) collective-permute-start(bf16[256,1024]{1,0:T(8,128)(2,1)S(1)} %bitcast.215), channel_id=1, source_target_pairs={{0,1},{1,2},{2,3},{3,0},{4,5},{5,6},{6,7},{7,4},{8,9},{9,10},{10,1... | collective-permute-start | bytes 1572872 | tf_op jit(solution)/shard_map/ppermute | solution.py:425
  29.5 25.1 %collective-permute-start = (bf16[256,1024]{1,0:T(8,128)(2,1)S(1)}, bf16[256,1024]{1,0:T(8,128)(2,1)S(1)}, u32[]{:S(2)}, u32[]{:S(2)}) collective-permute-start(bf16[256,1024]{1,0:T(8,128)(2,1)S(1)} %bitcast.216), channel_id=1, source_target_pairs={{0,3},{1,0},{2,1},{3,2},{4,7},{5,4},{6,5},{7,6},{8,11},{9,8},{10,9... | collective-permute-start | bytes 1572872 | tf_op jit(solution)/shard_map/ppermute | solution.py:426
  44.2 16.1 %collective-permute-start.2 = (bf16[128,1024]{1,0:T(8,128)(2,1)}, bf16[128,1024]{1,0:T(8,128)(2,1)S(1)}, u32[]{:S(2)}, u32[]{:S(2)}) collective-permute-start(bf16[128,1024]{1,0:T(8,128)(2,1)} %slice.302), channel_id=1, source_target_pairs={{0,1},{1,2},{2,3},{3,0},{4,5},{5,6},{6,7},{7,4},{8,9},{9,10},{10,1... | collective-permute-start | bytes 786440 | tf_op jit(solution)/shard_map/ppermute | solution.py:431
  55.5 9.5 %collective-permute-start.3 = (bf16[128,1024]{1,0:T(8,128)(2,1)}, bf16[128,1024]{1,0:T(8,128)(2,1)}, u32[]{:S(2)}, u32[]{:S(2)}) collective-permute-start(bf16[128,1024]{1,0:T(8,128)(2,1)} %slice.303), channel_id=1, source_target_pairs={{0,3},{1,0},{2,1},{3,2},{4,7},{5,4},{6,5},{7,6},{8,11},{9,8},{10,9... | collective-permute-start | bytes 786440 | tf_op jit(solution)/shard_map/ppermute | solution.py:432
  66.0 8.5 %collective-permute-start.13 = (bf16[64,1024]{1,0:T(8,128)(2,1)}, bf16[64,1024]{1,0:T(8,128)(2,1)S(1)}, u32[]{:S(2)}, u32[]{:S(2)}) collective-permute-start(bf16[64,1024]{1,0:T(8,128)(2,1)} %param.26), channel_id=1, source_target_pairs={{0,1},{1,2},{2,3},{3,0},{4,5},{5,6},{6,7},{7,4},{8,9},{9,10},{10,1... | collective-permute-start | bytes 393224 | tf_op jit(solution)/shard_map/ppermute | solution.py:473
  66.7 12.2 %collective-permute-start.14 = (bf16[64,1024]{1,0:T(8,128)(2,1)}, bf16[64,1024]{1,0:T(8,128)(2,1)S(1)}, u32[]{:S(2)}, u32[]{:S(2)}) collective-permute-start(bf16[64,1024]{1,0:T(8,128)(2,1)} %param.26), channel_id=1, source_target_pairs={{0,2},{1,3},{2,0},{3,1},{4,6},{5,7},{6,4},{7,5},{8,10},{9,11},{10,... | collective-permute-start | bytes 393224 | tf_op jit(solution)/shard_map/ppermute | solution.py:473
  69.5 9.4 %collective-permute-start.15 = (bf16[64,1024]{1,0:T(8,128)(2,1)}, bf16[64,1024]{1,0:T(8,128)(2,1)S(1)}, u32[]{:S(2)}, u32[]{:S(2)}) collective-permute-start(bf16[64,1024]{1,0:T(8,128)(2,1)} %param.26), channel_id=1, source_target_pairs={{0,3},{1,0},{2,1},{3,2},{4,7},{5,4},{6,5},{7,6},{8,11},{9,8},{10,9... | collective-permute-start | bytes 393224 | tf_op jit(solution)/shard_map/ppermute | solution.py:473
  80.8 138.5 %all-gather.7.cloned.1.call-start = ((), (), s32[]{:S(2)}) async-start(), calls=%async_computation.4 | async-start | bytes 3538944 | tf_op jit(solution)/shard_map/all_gather | solution.py:614
  84.9 7.6 %collective-permute-start.20 = (bf16[32,1536]{1,0:T(8,128)(2,1)S(1)}, bf16[32,1536]{1,0:T(8,128)(2,1)S(1)}, u32[]{:S(2)}, u32[]{:S(2)}) collective-permute-start(bf16[32,1536]{1,0:T(8,128)(2,1)S(1)} %get-tuple-element.127), channel_id=1, source_target_pairs={{0,1},{1,2},{2,3},{3,0},{4,5},{5,6},{6,7},{7,4},{8,9},{9,10},{10,1... | collective-permute-start | bytes 294920 | tf_op jit(solution)/shard_map/ppermute | solution.py:482
  87.6 7.8 %collective-permute-start.21 = (bf16[32,1536]{1,0:T(8,128)(2,1)S(1)}, bf16[32,1536]{1,0:T(8,128)(2,1)S(1)}, u32[]{:S(2)}, u32[]{:S(2)}) collective-permute-start(bf16[32,1536]{1,0:T(8,128)(2,1)S(1)} %get-tuple-element.126), channel_id=1, source_target_pairs={{0,2},{1,3},{2,0},{3,1},{4,6},{5,7},{6,4},{7,5},{8,10},{9,11},{10,... | collective-permute-start | bytes 294920 | tf_op jit(solution)/shard_map/ppermute | solution.py:482
  87.8 7.6 %collective-permute-start.22 = (bf16[32,1536]{1,0:T(8,128)(2,1)S(1)}, bf16[32,1536]{1,0:T(8,128)(2,1)S(1)}, u32[]{:S(2)}, u32[]{:S(2)}) collective-permute-start(bf16[32,1536]{1,0:T(8,128)(2,1)S(1)} %get-tuple-element.125), channel_id=1, source_target_pairs={{0,3},{1,0},{2,1},{3,2},{4,7},{5,4},{6,5},{7,6},{8,11},{9,8},{10,9... | collective-permute-start | bytes 294920 | tf_op jit(solution)/shard_map/ppermute | solution.py:482
  96.2 333.1 %reduce-scatter.8.cloned.1.call-start = ((), (), s32[]{:S(2)}) async-start(), calls=%async_computation.7 | async-start | bytes 3538944 | tf_op jit(solution)/shard_map/reduce_scatter | solution.py:665
  103.9 37.6 %collective-permute-start.7 = (bf16[256,1024]{1,0:T(8,128)(2,1)S(1)}, bf16[256,1024]{1,0:T(8,128)(2,1)S(1)}, u32[]{:S(2)}, u32[]{:S(2)}) collective-permute-start(bf16[256,1024]{1,0:T(8,128)(2,1)S(1)} %bitcast.225), channel_id=1, source_target_pairs={{0,3},{1,0},{2,1},{3,2},{4,7},{5,4},{6,5},{7,6},{8,11},{9,8},{10,9... | collective-permute-start | bytes 1572872 | tf_op jit(solution)/shard_map/ppermute | solution.py:473
  107.1 46.3 %collective-permute-start.8 = (bf16[256,1024]{1,0:T(8,128)(2,1)S(1)}, bf16[256,1024]{1,0:T(8,128)(2,1)S(1)}, u32[]{:S(2)}, u32[]{:S(2)}) collective-permute-start(bf16[256,1024]{1,0:T(8,128)(2,1)S(1)} %bitcast.226), channel_id=1, source_target_pairs={{0,2},{1,3},{2,0},{3,1},{4,6},{5,7},{6,4},{7,5},{8,10},{9,11},{10,... | collective-permute-start | bytes 1572872 | tf_op jit(solution)/shard_map/ppermute | solution.py:473
  107.9 45.6 %collective-permute-start.9 = (bf16[256,1024]{1,0:T(8,128)(2,1)S(1)}, bf16[256,1024]{1,0:T(8,128)(2,1)S(1)}, u32[]{:S(2)}, u32[]{:S(2)}) collective-permute-start(bf16[256,1024]{1,0:T(8,128)(2,1)S(1)} %bitcast.227), channel_id=1, source_target_pairs={{0,1},{1,2},{2,3},{3,0},{4,5},{5,6},{6,7},{7,4},{8,9},{9,10},{10,1... | collective-permute-start | bytes 1572872 | tf_op jit(solution)/shard_map/ppermute | solution.py:473
  154.5 11.1 %collective-permute-start.10 = (bf16[256,512]{1,0:T(8,128)(2,1)S(1)}, bf16[256,512]{1,0:T(8,128)(2,1)S(1)}, u32[]{:S(2)}, u32[]{:S(2)}) collective-permute-start(bf16[256,512]{1,0:T(8,128)(2,1)S(1)} %get-tuple-element.98), channel_id=1, source_target_pairs={{0,1},{1,2},{2,3},{3,0},{4,5},{5,6},{6,7},{7,4},{8,9},{9,10},{10,1... | collective-permute-start | bytes 786440 | tf_op jit(solution)/shard_map/ppermute | solution.py:473
  154.5 20.8 %collective-permute-start.11 = (bf16[256,512]{1,0:T(8,128)(2,1)S(1)}, bf16[256,512]{1,0:T(8,128)(2,1)}, u32[]{:S(2)}, u32[]{:S(2)}) collective-permute-start(bf16[256,512]{1,0:T(8,128)(2,1)S(1)} %get-tuple-element.97), channel_id=1, source_target_pairs={{0,2},{1,3},{2,0},{3,1},{4,6},{5,7},{6,4},{7,5},{8,10},{9,11},{10,... | collective-permute-start | bytes 786440 | tf_op jit(solution)/shard_map/ppermute | solution.py:473
  155.0 20.3 %collective-permute-start.12 = (bf16[256,512]{1,0:T(8,128)(2,1)S(1)}, bf16[256,512]{1,0:T(8,128)(2,1)}, u32[]{:S(2)}, u32[]{:S(2)}) collective-permute-start(bf16[256,512]{1,0:T(8,128)(2,1)S(1)} %get-tuple-element.96), channel_id=1, source_target_pairs={{0,3},{1,0},{2,1},{3,2},{4,7},{5,4},{6,5},{7,6},{8,11},{9,8},{10,9... | collective-permute-start | bytes 786440 | tf_op jit(solution)/shard_map/ppermute | solution.py:473
  179.1 17.6 %collective-permute-start.17 = (bf16[256,1024]{1,0:T(8,128)(2,1)S(1)}, bf16[256,1024]{1,0:T(8,128)(2,1)S(1)}, u32[]{:S(2)}, u32[]{:S(2)}) collective-permute-start(bf16[256,1024]{1,0:T(8,128)(2,1)S(1)} %get-tuple-element.66), channel_id=1, source_target_pairs={{0,1},{1,2},{2,3},{3,0},{4,5},{5,6},{6,7},{7,4},{8,9},{9,10},{10,1... | collective-permute-start | bytes 1572872 | tf_op jit(solution)/shard_map/ppermute | solution.py:425
  184.2 23.7 %collective-permute-start.16 = (bf16[256,1024]{1,0:T(8,128)(2,1)S(1)}, bf16[256,1024]{1,0:T(8,128)(2,1)S(1)}, u32[]{:S(2)}, u32[]{:S(2)}) collective-permute-start(bf16[256,1024]{1,0:T(8,128)(2,1)S(1)} %get-tuple-element.66), channel_id=1, source_target_pairs={{0,3},{1,0},{2,1},{3,2},{4,7},{5,4},{6,5},{7,6},{8,11},{9,8},{10,9... | collective-permute-start | bytes 1572872 | tf_op jit(solution)/shard_map/ppermute | solution.py:426
  196.7 20.2 %collective-permute-start.18 = (bf16[128,1024]{1,0:T(8,128)(2,1)S(1)}, bf16[128,1024]{1,0:T(8,128)(2,1)S(1)}, u32[]{:S(2)}, u32[]{:S(2)}) collective-permute-start(bf16[128,1024]{1,0:T(8,128)(2,1)S(1)} %slice.305), channel_id=1, source_target_pairs={{0,1},{1,2},{2,3},{3,0},{4,5},{5,6},{6,7},{7,4},{8,9},{9,10},{10,1... | collective-permute-start | bytes 786440 | tf_op jit(solution)/shard_map/ppermute | solution.py:431
  207.9 9.8 %collective-permute-start.19 = (bf16[128,1024]{1,0:T(8,128)(2,1)S(1)}, bf16[128,1024]{1,0:T(8,128)(2,1)S(1)}, u32[]{:S(2)}, u32[]{:S(2)}) collective-permute-start(bf16[128,1024]{1,0:T(8,128)(2,1)S(1)} %slice.306), channel_id=1, source_target_pairs={{0,3},{1,0},{2,1},{3,2},{4,7},{5,4},{6,5},{7,6},{8,11},{9,8},{10,9... | collective-permute-start | bytes 786440 | tf_op jit(solution)/shard_map/ppermute | solution.py:432
  235.2 11.1 %collective-permute-start.23 = (bf16[128,1024]{1,0:T(8,128)(2,1)S(1)}, bf16[128,1024]{1,0:T(8,128)(2,1)S(1)}, u32[]{:S(2)}, u32[]{:S(2)}) collective-permute-start(bf16[128,1024]{1,0:T(8,128)(2,1)S(1)} %get-tuple-element.84), channel_id=1, source_target_pairs={{0,1},{1,2},{2,3},{3,0},{4,5},{5,6},{6,7},{7,4},{8,9},{9,10},{10,1... | collective-permute-start | bytes 786440 | tf_op jit(solution)/shard_map/ppermute | solution.py:449
  235.8 13.1 %collective-permute-start.25 = (bf16[128,1024]{1,0:T(8,128)(2,1)S(1)}, bf16[128,1024]{1,0:T(8,128)(2,1)S(1)}, u32[]{:S(2)}, u32[]{:S(2)}) collective-permute-start(bf16[128,1024]{1,0:T(8,128)(2,1)S(1)} %get-tuple-element.85), channel_id=1, source_target_pairs={{0,3},{1,0},{2,1},{3,2},{4,7},{5,4},{6,5},{7,6},{8,11},{9,8},{10,9... | collective-permute-start | bytes 786440 | tf_op jit(solution)/shard_map/ppermute | solution.py:449
  250.0 17.0 %collective-permute-start.24 = (bf16[256,1024]{1,0:T(8,128)(2,1)}, bf16[256,1024]{1,0:T(8,128)(2,1)}, u32[]{:S(2)}, u32[]{:S(2)}) collective-permute-start(bf16[256,1024]{1,0:T(8,128)(2,1)} %pad_maximum_fusion.8), channel_id=1, source_target_pairs={{0,1},{1,2},{2,3},{3,0},{4,5},{5,6},{6,7},{7,4},{8,9},{9,10},{10,1... | collective-permute-start | bytes 1572872 | tf_op jit(solution)/shard_map/ppermute | solution.py:449
  251.7 23.9 %collective-permute-start.26 = (bf16[256,1024]{1,0:T(8,128)(2,1)}, bf16[256,1024]{1,0:T(8,128)(2,1)}, u32[]{:S(2)}, u32[]{:S(2)}) collective-permute-start(bf16[256,1024]{1,0:T(8,128)(2,1)} %pad_maximum_fusion.9), channel_id=1, source_target_pairs={{0,3},{1,0},{2,1},{3,2},{4,7},{5,4},{6,5},{7,6},{8,11},{9,8},{10,9... | collective-permute-start | bytes 1572872 | tf_op jit(solution)/shard_map/ppermute | solution.py:449
  261.2 184.9 %reduce-scatter.4.cloned.1.call-start = ((), (), s32[]{:S(2)}) async-start(), calls=%async_computation.5 | async-start | bytes 3833856 | tf_op jit(solution)/shard_map/reduce_scatter | solution.py:665
  288.1 11.5 %collective-permute-start.27 = (bf16[256,512]{1,0:T(8,128)(2,1)}, bf16[256,512]{1,0:T(8,128)(2,1)S(1)}, u32[]{:S(2)}, u32[]{:S(2)}) collective-permute-start(bf16[256,512]{1,0:T(8,128)(2,1)} %get-tuple-element.103), channel_id=1, source_target_pairs={{0,3},{1,0},{2,1},{3,2},{4,7},{5,4},{6,5},{7,6},{8,11},{9,8},{10,9... | collective-permute-start | bytes 786440 | tf_op jit(solution)/shard_map/ppermute | solution.py:473
  289.4 24.0 %collective-permute-start.28 = (bf16[256,512]{1,0:T(8,128)(2,1)}, bf16[256,512]{1,0:T(8,128)(2,1)}, u32[]{:S(2)}, u32[]{:S(2)}) collective-permute-start(bf16[256,512]{1,0:T(8,128)(2,1)} %get-tuple-element.102), channel_id=1, source_target_pairs={{0,2},{1,3},{2,0},{3,1},{4,6},{5,7},{6,4},{7,5},{8,10},{9,11},{10,... | collective-permute-start | bytes 786440 | tf_op jit(solution)/shard_map/ppermute | solution.py:473
  290.1 23.4 %collective-permute-start.29 = (bf16[256,512]{1,0:T(8,128)(2,1)S(1)}, bf16[256,512]{1,0:T(8,128)(2,1)}, u32[]{:S(2)}, u32[]{:S(2)}) collective-permute-start(bf16[256,512]{1,0:T(8,128)(2,1)S(1)} %get-tuple-element.101), channel_id=1, source_target_pairs={{0,1},{1,2},{2,3},{3,0},{4,5},{5,6},{6,7},{7,4},{8,9},{9,10},{10,1... | collective-permute-start | bytes 786440 | tf_op jit(solution)/shard_map/ppermute | solution.py:473
  317.0 30.8 %collective-permute-start.30 = (bf16[256,1024]{1,0:T(8,128)(2,1)S(1)}, bf16[256,1024]{1,0:T(8,128)(2,1)S(1)}, u32[]{:S(2)}, u32[]{:S(2)}) collective-permute-start(bf16[256,1024]{1,0:T(8,128)(2,1)S(1)} %get-tuple-element.88), channel_id=1, source_target_pairs={{0,1},{1,2},{2,3},{3,0},{4,5},{5,6},{6,7},{7,4},{8,9},{9,10},{10,1... | collective-permute-start | bytes 1572872 | tf_op jit(solution)/shard_map/ppermute | solution.py:473
  317.0 30.8 %collective-permute-start.32 = (bf16[256,1024]{1,0:T(8,128)(2,1)S(1)}, bf16[256,1024]{1,0:T(8,128)(2,1)S(1)}, u32[]{:S(2)}, u32[]{:S(2)}) collective-permute-start(bf16[256,1024]{1,0:T(8,128)(2,1)S(1)} %get-tuple-element.89), channel_id=1, source_target_pairs={{0,3},{1,0},{2,1},{3,2},{4,7},{5,4},{6,5},{7,6},{8,11},{9,8},{10,9... | collective-permute-start | bytes 1572872 | tf_op jit(solution)/shard_map/ppermute | solution.py:473
  356.5 107.7 %reduce-scatter.6.cloned.1.call-start = ((), (), s32[]{:S(2)}) async-start(), calls=%async_computation.6 | async-start | bytes 6340608 | tf_op jit(solution)/shard_map/reduce_scatter | solution.py:665
  366.4 29.4 %collective-permute-start.31 = (bf16[256,1024]{1,0:T(8,128)(2,1)S(1)}, bf16[256,1024]{1,0:T(8,128)(2,1)S(1)}, u32[]{:S(2)}, u32[]{:S(2)}) collective-permute-start(bf16[256,1024]{1,0:T(8,128)(2,1)S(1)} %copy-done.32), channel_id=1, source_target_pairs={{0,2},{1,3},{2,0},{3,1},{4,6},{5,7},{6,4},{7,5},{8,10},{9,11},{10,... | collective-permute-start | bytes 1572872 | tf_op jit(solution)/shard_map/ppermute | solution.py:473
  369.3 29.1 %collective-permute-start.33 = (bf16[128,1024]{1,0:T(8,128)(2,1)S(1)}, bf16[128,1024]{1,0:T(8,128)(2,1)S(1)}, u32[]{:S(2)}, u32[]{:S(2)}) collective-permute-start(bf16[128,1024]{1,0:T(8,128)(2,1)S(1)} %get-tuple-element.80), channel_id=1, source_target_pairs={{0,1},{1,2},{2,3},{3,0},{4,5},{5,6},{6,7},{7,4},{8,9},{9,10},{10,1... | collective-permute-start | bytes 786440 | tf_op jit(solution)/shard_map/ppermute | solution.py:449
  369.4 29.0 %collective-permute-start.35 = (bf16[128,1024]{1,0:T(8,128)(2,1)S(1)}, bf16[128,1024]{1,0:T(8,128)(2,1)S(1)}, u32[]{:S(2)}, u32[]{:S(2)}) collective-permute-start(bf16[128,1024]{1,0:T(8,128)(2,1)S(1)} %get-tuple-element.81), channel_id=1, source_target_pairs={{0,3},{1,0},{2,1},{3,2},{4,7},{5,4},{6,5},{7,6},{8,11},{9,8},{10,9... | collective-permute-start | bytes 786440 | tf_op jit(solution)/shard_map/ppermute | solution.py:449
  373.4 24.8 %collective-permute-start.48 = (f32[148,128]{1,0:T(8,128)S(1)}, f32[148,128]{1,0:T(8,128)S(1)}, u32[]{:S(2)}, u32[]{:S(2)}) collective-permute-start(f32[148,128]{1,0:T(8,128)S(1)} %fusion.84), channel_id=1, source_target_pairs={{0,16},{4,20},{8,24},{12,28},{16,0},{20,4},{24,8},{28,12},{1,17},{... | collective-permute-start | bytes 227336 | tf_op jit(solution)/shard_map/ppermute | solution.py:501
  398.7 23.0 %collective-permute-start.34 = (bf16[256,1024]{1,0:T(8,128)(2,1)S(1)}, bf16[256,1024]{1,0:T(8,128)(2,1)S(1)}, u32[]{:S(2)}, u32[]{:S(2)}) collective-permute-start(bf16[256,1024]{1,0:T(8,128)(2,1)S(1)} %pad_maximum_fusion.10), channel_id=1, source_target_pairs={{0,1},{1,2},{2,3},{3,0},{4,5},{5,6},{6,7},{7,4},{8,9},{9,10},{10,1... | collective-permute-start | bytes 1572872 | tf_op jit(solution)/shard_map/ppermute | solution.py:449
  402.7 15.5 %collective-permute-start.50 = (f32[148,128]{1,0:T(8,128)S(1)}, f32[148,128]{1,0:T(8,128)S(1)}, u32[]{:S(2)}, u32[]{:S(2)}) collective-permute-start(f32[148,128]{1,0:T(8,128)S(1)} %add.355), channel_id=1, source_target_pairs={{0,2},{1,3},{2,0},{3,1},{4,6},{5,7},{6,4},{7,5},{8,10},{9,11},{10,... | collective-permute-start | bytes 227336 | tf_op jit(solution)/shard_map/ppermute | solution.py:501
  405.5 22.1 %collective-permute-start.36 = (bf16[256,1024]{1,0:T(8,128)(2,1)}, bf16[256,1024]{1,0:T(8,128)(2,1)S(1)}, u32[]{:S(2)}, u32[]{:S(2)}) collective-permute-start(bf16[256,1024]{1,0:T(8,128)(2,1)} %pad_maximum_fusion.11), channel_id=1, source_target_pairs={{0,3},{1,0},{2,1},{3,2},{4,7},{5,4},{6,5},{7,6},{8,11},{9,8},{10,9... | collective-permute-start | bytes 1572872 | tf_op jit(solution)/shard_map/ppermute | solution.py:449
  430.4 11.5 %collective-permute-start.43 = (bf16[32,1536]{1,0:T(8,128)(2,1)S(1)}, bf16[32,1536]{1,0:T(8,128)(2,1)S(1)}, u32[]{:S(2)}, u32[]{:S(2)}) collective-permute-start(bf16[32,1536]{1,0:T(8,128)(2,1)S(1)} %get-tuple-element.123), channel_id=1, source_target_pairs={{0,1},{1,2},{2,3},{3,0},{4,5},{5,6},{6,7},{7,4},{8,9},{9,10},{10,1... | collective-permute-start | bytes 294920 | tf_op jit(solution)/shard_map/ppermute | solution.py:482
  465.2 8.3 %collective-permute-start.40 = (bf16[64,1024]{1,0:T(8,128)(2,1)S(1)}, bf16[64,1024]{1,0:T(8,128)(2,1)S(1)}, u32[]{:S(2)}, u32[]{:S(2)}) collective-permute-start(bf16[64,1024]{1,0:T(8,128)(2,1)S(1)} %get-tuple-element.104), channel_id=1, source_target_pairs={{0,1},{1,2},{2,3},{3,0},{4,5},{5,6},{6,7},{7,4},{8,9},{9,10},{10,1... | collective-permute-start | bytes 393224 | tf_op jit(solution)/shard_map/ppermute | solution.py:473
  466.8 11.3 %collective-permute-start.41 = (bf16[64,1024]{1,0:T(8,128)(2,1)S(1)}, bf16[64,1024]{1,0:T(8,128)(2,1)S(1)}, u32[]{:S(2)}, u32[]{:S(2)}) collective-permute-start(bf16[64,1024]{1,0:T(8,128)(2,1)S(1)} %get-tuple-element.106), channel_id=1, source_target_pairs={{0,2},{1,3},{2,0},{3,1},{4,6},{5,7},{6,4},{7,5},{8,10},{9,11},{10,... | collective-permute-start | bytes 393224 | tf_op jit(solution)/shard_map/ppermute | solution.py:473
  469.2 8.8 %collective-permute-start.42 = (bf16[64,1024]{1,0:T(8,128)(2,1)S(1)}, bf16[64,1024]{1,0:T(8,128)(2,1)S(1)}, u32[]{:S(2)}, u32[]{:S(2)}) collective-permute-start(bf16[64,1024]{1,0:T(8,128)(2,1)S(1)} %get-tuple-element.105), channel_id=1, source_target_pairs={{0,3},{1,0},{2,1},{3,2},{4,7},{5,4},{6,5},{7,6},{8,11},{9,8},{10,9... | collective-permute-start | bytes 393224 | tf_op jit(solution)/shard_map/ppermute | solution.py:473
  (65 other events, 877.4 us)
Sparse Core Ops, SparseCore 0:
  26.8 34.8 all-gather.4
  81.0 43.1 all-gather.8
  126.7 32.3 all-gather.6
  261.4 44.4 reduce-scatter.7
  356.6 45.7 reduce-scatter.3
  405.7 58.4 reduce-scatter.5

commit v3 on v2

--- a/solution.py
+++ b/solution.py
@@ -47,33 +47,45 @@
     return mm(ones, first) + mm(ones, second) + mm(ones, third)
 
 
-def small_inverse(coupling):
-    size = coupling.shape[0]
-    rows = iota(coupling.shape, 0)
-    cols = iota(coupling.shape, 1)
-    solved = jnp.where((rows // 2 == cols // 2), -coupling, 0.0)
+def small_inverses(couplings):
+    size = couplings[0].shape[0]
+    rows = iota((size, size), 0)
+    cols = iota((size, size), 1)
+    solved = [jnp.where(rows // 2 == cols // 2, -coupling, 0.0) for coupling in couplings]
     width = 2
     while width < size:
         band = (rows // (2 * width) == cols // (2 * width)) & (rows // width != cols // width)
-        part = jnp.where(band, coupling, 0.0)
-        step = part + mm(part, solved)
-        solved = solved - step - mm(solved, step)
+        parts = [jnp.where(band, coupling, 0.0) for coupling in couplings]
+        steps = [part + mm(part, done) for part, done in zip(parts, solved)]
+        solved = [done - step - mm(done, step) for done, step in zip(solved, steps)]
         width = 2 * width
     return solved
 
 
-def lower_inverse(coupling):
-    size = coupling.shape[0]
+def lower_inverses(couplings):
+    size = couplings[0].shape[0]
     if size <= LANES:
-        return small_inverse(coupling)
+        return small_inverses(couplings)
     half = size // 2
-    head = lower_inverse(coupling[:half, :half])
-    tail = lower_inverse(coupling[half:, half:])
-    part = coupling[half:, :half]
-    step = part + mm(part, head)
-    corner = -step - mm(tail, step)
-    top = jnp.concatenate([head, jnp.zeros((half, half), F32)], axis=1)
-    return jnp.concatenate([top, jnp.concatenate([corner, tail], axis=1)], axis=0)
+    solved = lower_inverses(
+        [coupling[:half, :half] for coupling in couplings]
+        + [coupling[half:, half:] for coupling in couplings]
+    )
+    heads, tails = solved[: len(couplings)], solved[len(couplings) :]
+    parts = [coupling[half:, :half] for coupling in couplings]
+    steps = [part + mm(part, head) for part, head in zip(parts, heads)]
+    corners = [-step - mm(tail, step) for step, tail in zip(steps, tails)]
+    blank = jnp.zeros((half, half), F32)
+    return [
+        jnp.concatenate(
+            [
+                jnp.concatenate([head, blank], axis=1),
+                jnp.concatenate([corner, tail], axis=1),
+            ],
+            axis=0,
+        )
+        for head, corner, tail in zip(heads, corners, tails)
+    ]
 
 
 def silu_slope(values, gate):
@@ -146,15 +158,19 @@
     shifted, log_decay, running = decay_parts(rate, side_ref[0:1, :], side_ref[1:2, :])
     running_rows = running.T
     strict = iota((rows, rows), 0) > iota((rows, rows), 1)
+    parts = [head_parts(summed, running, running_rows, head, heads) for head in range(heads)]
+    inners = [mm_nt(part[5], part[5]) for part in parts]
+    solutions = lower_inverses(
+        [
+            jnp.where(strict, strengths[:, 2 * head : 2 * head + 1] * inner * part[8], 0.0)
+            for head, (inner, part) in enumerate(zip(inners, parts))
+        ]
+    )
     for head in range(heads):
-        _, _, _, _, query, key, value, total, decays, last = head_parts(
-            summed, running, running_rows, head, heads
-        )
+        _, _, _, _, query, key, value, total, decays, last = parts[head]
         strength = strengths[:, 2 * head : 2 * head + 1]
         scaling = jnp.exp(total)
-        inner = mm_nt(key, key)
-        coupling = jnp.where(strict, strength * inner * decays, 0.0)
-        solved = lower_inverse(coupling)
+        solved = solutions[head]
         start = memory_ref[head]
         target = strength * (value - scaling * mm(key, start))
         update = target + mm(solved, target)
@@ -417,13 +433,24 @@
     return lax.dynamic_update_slice(whole, block[None], (place,) + (0,) * block.ndim)
 
 
-def ring_gather(block, axis):
+def near_pieces(block, axis):
+    count = lax.axis_size(axis)
+    return (
+        lax.ppermute(block, axis, shift_pairs(count, 1)),
+        lax.ppermute(block, axis, shift_pairs(count, -1)),
+    )
+
+
+def ring_gather(block, axis, near=None):
     count = lax.axis_size(axis)
     found = {0: block}
     right, left = block, block
     for hop in range(1, (count - 1) // 2 + 1):
-        right = lax.ppermute(right, axis, shift_pairs(count, 1))
-        left = lax.ppermute(left, axis, shift_pairs(count, -1))
+        if hop == 1:
+            right, left = near or near_pieces(block, axis)
+        else:
+            right = lax.ppermute(right, axis, shift_pairs(count, 1))
+            left = lax.ppermute(left, axis, shift_pairs(count, -1))
         found[count - hop] = right
         found[hop] = left
     if count % 2 == 0:
@@ -438,9 +465,10 @@
     return lax.dynamic_index_in_dim(whole, place, 0, keepdims=False)
 
 
-def ring_reduce(whole, axis):
+def ring_reduce(wholes, axis):
     count = lax.axis_size(axis)
-    blocks = whole.reshape((count, whole.shape[0] // count) + whole.shape[1:])
+    cut = [whole.reshape(count, whole.shape[0] // count, whole.shape[1]) for whole in wholes]
+    blocks = [jnp.concatenate([part[hop] for part in cut], axis=0) for hop in range(count)]
     total = blocks[0]
     if count == 1:
         return total, total
@@ -593,24 +621,28 @@
         + [pad_last(by_heads(rate_proj, ns), LANES)],
         axis=2,
     )
-    all_in = ring_gather(flat_in, "seq")
-    mixer_rows = exchange(mixer_local, "seq").reshape(ns * rows, mixer_local.shape[2])
-    mixer_weight = lax.all_gather(mixer_rows, "dp", axis=0, tiled=True)
+    mixer_width = mixer_local.shape[2]
     ffn_local = jnp.concatenate(
         [hidden_out(ffn_gate, nd, ns, padded), hidden_out(ffn_up, nd, ns, padded)], axis=2
     )
-    out_local = after(output_proj, all_in)
-    out_here = jnp.zeros((ns,) + output_proj.shape, BF16)
-    for hop, rows_there in enumerate(hand_out([out_local] * ns, "seq", 1)):
-        out_here = put_block(out_here, rows_there, (me - hop) % ns)
+    out_local = jnp.broadcast_to(output_proj.reshape(1, rows, -1), (ns, rows, output_proj.size // rows))
+    near = near_pieces(flat_in, "seq")
+    mixer_rows = exchange(mixer_local, "seq").reshape(ns * rows, mixer_width)
+    mixer_rows, near = lax.optimization_barrier((mixer_rows, near))
+    mixer_weight = lax.all_gather(mixer_rows, "dp", axis=0, tiled=True)
+    all_in = ring_gather(flat_in, "seq", near)
+    shared = exchange(after(jnp.concatenate([ffn_local, out_local], axis=2), near), "seq")
     out_rows = ns * output_proj.shape[0]
-    both = jnp.concatenate([out_here.reshape(out_rows, width), ffn_down], axis=0)
+    out_here = shared[:, :, 2 * padded :].reshape(out_rows, width)
+    down_rows = ffn_down.shape[0]
+    spare = jnp.zeros((-(out_rows + down_rows) % 16, width), BF16)
+    both = jnp.concatenate([out_here, ffn_down, spare], axis=0)
     both = lax.all_gather(both, "dp", axis=0, tiled=False)
     out_weight = both[:, :out_rows].reshape(ns, kv, width)
     turned = jnp.concatenate([take_block(out_weight, (me - hop) % ns) for hop in range(ns)], axis=0)
-    down_weight = both[:, out_rows:].reshape(hidden_own, width)
+    down_weight = both[:, out_rows : out_rows + down_rows].reshape(hidden_own, width)
     down_weight = jnp.pad(down_weight, ((0, padded - hidden_own), (0, 0)))
-    ffn_rows = exchange(after(ffn_local, out_here), "seq").reshape(ns * rows, 2 * padded)
+    ffn_rows = shared[:, :, : 2 * padded].reshape(ns * rows, 2 * padded)
     ffn_weight = lax.all_gather(ffn_rows, "dp", axis=0, tiled=True)
 
     chunk_rows = min(CHUNK, piece)
@@ -642,8 +674,9 @@
     mixed, *saved = mixer_forward(
         projected, filters, side, gain_row, order, heads, seqs, chunk_rows
     )
-    all_cot = jnp.concatenate(hand_out([after(flat_cot, projected)] * ns, "seq", -1), axis=0)
-    mixed = after(mixed, all_cot)
+    cot_near = near_pieces(after(flat_cot, projected), "seq")
+    mixed, cot_near = lax.optimization_barrier((mixed, cot_near))
+    all_cot = ring_gather(flat_cot, "seq", cot_near)
     mixed_parts = hand_out(mixed.reshape(ns, own, kv), "seq", 1)
     mixed_low = jnp.concatenate(mixed_parts, axis=1)
 
@@ -661,59 +694,60 @@
         [adj_gate.astype(BF16), (adj_act * gate_silu).astype(BF16)], axis=1
     )
     adj_partial_two = dot_nt(adj_both, ffn_weight)
-    adj_second, first_in = ring_reduce(adj_partial_two, "seq")
+    adj_second, first_in = ring_reduce([adj_partial_two], "seq")
     scatter = lambda grad: lax.psum_scatter(
         grad.astype(BF16), "dp", scatter_dimension=0, tiled=True
     )
     active_late, adj_both_late = after((active, adj_both), first_in)
-    ffn_sums = scatter(dot_tn(second_all, adj_both_late))
+    grad_ffn = dot_tn(second_all, adj_both_late).astype(BF16)
+    ffn_sums = scatter(grad_ffn)
+    adj_second = after(adj_second, grad_ffn)
     grad_down = dot_tn(active_late, all_cot)[:hidden_own].astype(BF16)
 
     gain_two = jnp.sum(adj_second * unit_two, axis=0)
     adj_middle = flat_cot.astype(F32) + rms_back(unit_two, scale_two, ffn_gain, adj_second)
     attn_low = adj_middle.astype(BF16)
-    adj_mixed = dot_nt(attn_low, turned).astype(BF16)
-    adj_heads = jnp.concatenate(
-        hand_out([adj_mixed[:, hop * kv : (hop + 1) * kv] for hop in range(ns)], "seq", -1), axis=0
-    )
-    active_late = after(active, adj_mixed)
-    block_parts = dot(active_late, down_weight).reshape(ns, own, width)
-    mixed_stack = jnp.stack(mixed_parts)
-    mixed_natural = jnp.concatenate(
-        [take_block(mixed_stack, (me - part) % ns) for part in range(ns)], axis=1
-    )
-    grad_out = dot_tn(mixed_natural, after(attn_low, adj_mixed)).astype(BF16)
+    attn_near = near_pieces(attn_low, "seq")
+    active_late = after(active, attn_low)
+    block_parts = dot(active_late, down_weight)
+    attn_all = ring_gather(attn_low, "seq", attn_near)
+    adj_heads = dot_nt(attn_all, take_block(out_weight, me)).astype(BF16)
+    grad_out = dot_tn(mixed, attn_all).astype(BF16)
+    head_rows = kv // nd
+    spare = jnp.zeros((nd, -(head_rows + down_rows) % 16, width), BF16)
     both_grads = jnp.concatenate(
-        [grad_out.reshape(nd, out_rows, width), grad_down.reshape(nd, -1, width)], axis=1
+        [
+            grad_out.reshape(nd, head_rows, width),
+            grad_down.reshape(nd, down_rows, width),
+            spare,
+        ],
+        axis=1,
     ).reshape(-1, width)
     both_sums = scatter(both_grads)
-    adj_heads = after(adj_heads, both_grads)
-    block_low = after(block_parts[1:].astype(BF16), adj_heads)
-    block_in = hand_out(
-        [block_parts[0]] + [block_low[hop] for hop in range(ns - 1)], "seq", 1
-    )
-    block_sum = sum(part.astype(F32) for part in block_in[1:]) + block_in[0]
+    adj_heads = after(adj_heads, both_grads, ffn_sums)
+    down_out = both_sums[head_rows : head_rows + down_rows]
+    owners = [
+        (place * ns + part, part * nd + place) for place in range(nd) for part in range(ns)
+    ]
+    out_out = lax.ppermute(both_sums[:head_rows], ("dp", "seq"), owners)
+
+    adj_projected, filter_sum, side_sum, gain_sum = mixer_backward(
+        projected, filters, side, gain_row, adj_heads, saved, order, heads, seqs, chunk_rows
+    )
+    grad_mixer = dot_tn(normed, adj_projected).astype(BF16)
+    mixer_sums = scatter(after(grad_mixer, both_sums))
+    adj_partial = dot_nt(after(adj_projected, grad_mixer), mixer_weight)
+    gain_one = jnp.sum(adj_partial * unit_in, axis=0)
+    reduced, _ = ring_reduce([adj_partial, block_parts], "seq")
+    adj_normed, block_sum = reduced[:own], reduced[own:]
     block_out = (middle + block_sum).astype(BF16).reshape(inputs.shape)
-    down_out = both_sums[out_rows:]
-    out_sums = both_sums[:out_rows].reshape(ns, -1, width)
-    out_out = take_block(out_sums, me).astype(F32)
-    out_blocks = [take_block(out_sums, (me + hop) % ns) for hop in range(ns)]
-    for part in hand_out(out_blocks, "seq", 1)[1:]:
-        out_out = out_out + part.astype(F32)
-    out_out = out_out.astype(BF16)
-    ffn_parts = exchange(ffn_sums.reshape(ns, rows, -1), "seq")
+    shared = jnp.concatenate(
+        [mixer_sums.reshape(ns, rows, -1), ffn_sums.reshape(ns, rows, -1)], axis=2
+    )
+    shared = exchange(shared, "seq")
+    mixer_parts, ffn_parts = shared[:, :, :-2 * padded], shared[:, :, -2 * padded:]
     ffngate_out = hidden_back(ffn_parts[:, :, :padded], nd, hidden)
     ffnup_out = hidden_back(ffn_parts[:, :, padded:], nd, hidden)
-
-    adj_projected, filter_sum, side_sum, gain_sum = mixer_backward(
-        projected, filters, side, gain_row, adj_heads, saved, order, heads, seqs, chunk_rows
-    )
-    adj_projected = after(adj_projected, block_in[1], block_in[-1])
-    adj_partial = dot_nt(adj_projected, mixer_weight)
-    gain_one = jnp.sum(adj_partial * unit_in, axis=0)
-    adj_normed, first_in = ring_reduce(adj_partial, "seq")
-    grad_mixer = dot_tn(normed, after(adj_projected, first_in)).astype(BF16)
-    mixer_parts = exchange(scatter(grad_mixer).reshape(ns, rows, -1), "seq")
     whole_rows = lambda parts: jnp.swapaxes(parts, 0, 1).reshape(rows, -1)
     query_out = whole_rows(mixer_parts[:, :, :kq])
     key_out = whole_rows(mixer_parts[:, :, kq : 2 * kq])

time: 493 us -> 487 us (0.988)
  the two profiles are of different devices: /device:TPU:0 before, /device:TPU:11 now
where the time goes in v3:
time: 487 us; the launch traced here: 478 us
  waiting for transfers between devices  225 us (46%)
  matrix products  63.7 us (13%)
  local copies, waits for them, and re-layouts  57.3 us (12%)
  starting transfers between devices  47.4 us (10%)
  Pallas kernels  44.9 us (9%)
  other arithmetic  23.4 us (5%)
  between operations  15.8 us (3%)
    ppermute x9, waiting for transfers between devices, exchange(): lax.ppermute(take_block(whole, (me + hop) % count), axis, shift_pairs(cou...  57.9 us
    pallas_call x2, Pallas kernels, mixer_call(): pl.pallas_call(kernel, grid_spec=pltpu.PrefetchScalarGridSpec(num_scalar_...  44.9 us
    ppermute x8, waiting for transfers between devices, ring_reduce(): lax.ppermute(part.astype(BF16), axis, shift_pairs(count, by)).astype(F32)  36.2 us
    ppermute x5, waiting for transfers between devices, sum_everywhere(): values = values + lax.ppermute(values, axis, swap_pairs(count, mask))  34.1 us
    dot_general x4, matrix products, dot_nt(): return jnp.einsum('tc,dc->td', left, right, preferred_element_type=F32)  23.9 us
    dot_general x4, matrix products, dot(): return jnp.dot(left, right, preferred_element_type=F32)  20.8 us
    unnamed x108, local copies, waits for them, and re-layouts  20.7 us
    ppermute x4, waiting for transfers between devices, near_pieces(): lax.ppermute(block, axis, shift_pairs(count, 1))  19.1 us
  transfers between devices with their start and end apart: 48, of which 26 were waited for; matrix products, arithmetic and copies ran while one was open for 23% of the time, Pallas kernels for 9%

profile of v3, /device:TPU:11, one launch (start us, length us, event | category | flops | bytes accessed | tf_op | source)
XLA Modules:
  0.0 477.7 jit_solution(10335292891166463784)
XLA Ops:
  15.9 2.9 collective-permute-start.1
  19.1 14.8 %collective-permute-done = bf16[32,1664]{1,0:T(8,128)(2,1)S(1)} collective-permute-done((bf16[32,1664]{1,0:T(8,128)(2,1)S(1)}, bf16[32,1664]{1,0:T(8,128)(2,1)S(1)}, u32[]{:S(2)}, u32[]{:S(2)}) %collective-permute-start) | collective-permute-done | bytes 106528 | tf_op jit(solution)/shard_map/ppermute | solution.py:510
  33.9 5.9 %collective-permute-done.1 = bf16[32,1664]{1,0:T(8,128)(2,1)S(1)} collective-permute-done((bf16[32,1664]{1,0:T(8,128)(2,1)S(1)}, bf16[32,1664]{1,0:T(8,128)(2,1)S(1)}, u32[]{:S(2)}, u32[]{:S(2)}) %collective-permute-start.1) | collective-permute-done | bytes 106528 | tf_op jit(solution)/shard_map/ppermute | solution.py:510
  39.8 2.8 collective-permute-done.2
  47.2 5.1 %collective-permute-done.12 = bf16[32,3584]{1,0:T(8,128)(2,1)S(1)} collective-permute-done((bf16[32,3584]{1,0:T(8,128)(2,1)S(1)}, bf16[32,3584]{1,0:T(8,128)(2,1)S(1)}, u32[]{:S(2)}, u32[]{:S(2)}) %collective-permute-start.12) | collective-permute-done | bytes 229408 | tf_op jit(solution)/shard_map/ppermute | solution.py:510
  52.3 12.8 %collective-permute-done.13 = bf16[32,3584]{1,0:T(8,128)(2,1)S(1)} collective-permute-done((bf16[32,3584]{1,0:T(8,128)(2,1)S(1)}, bf16[32,3584]{1,0:T(8,128)(2,1)S(1)}, u32[]{:S(2)}, u32[]{:S(2)}) %collective-permute-start.13) | collective-permute-done | bytes 229408 | tf_op jit(solution)/shard_map/ppermute | solution.py:510
  65.1 2.4 collective-permute-done.14
  67.8 2.0 maximum_maximum_fusion.1
  75.7 4.2 collective-permute-done.5
  80.6 4.9 %collective-permute-done.6 = bf16[128,1024]{1,0:T(8,128)(2,1)S(1)} collective-permute-done((bf16[128,1024]{1,0:T(8,128)(2,1)S(1)}, bf16[128,1024]{1,0:T(8,128)(2,1)S(1)}, u32[]{:S(2)}, u32[]{:S(2)}) %collective-permute-start.6) | collective-permute-done | bytes 262176 | tf_op jit(solution)/shard_map/ppermute | solution.py:459
  87.0 2.4 fusion.4
  89.5 7.5 %convolution_convert_fusion.1.current_ref.before_ref = bf16[1024,1664]{1,0:T(8,128)(2,1)} fusion(bf16[1024,1664]{1,0:T(8,128)(2,1)} %all-gather.5.cloned.1.call-done, bf16[1024,1024]{1,0:T(8,128)(2,1)S(1)} %copy-done.17, f32[1024]{0:T(1024)S(1)} %copy-done.32, f32[1024]{0:T(1024)S(1)} %add_rsqrt_fusion), kind=kOutput, calls=%fused_computation.16 | convolution fusion | flops 3495559168 | bytes 8921088 | tf_op jit(solution)/shard_map/dot_general | solution.py:549
  98.5 18.1 %mixer_forward.1 = (bf16[1024,512]{1,0:T(8,128)(2,1)S(1)}, bf16[1,4,2,256,256]{4,3,2,1,0:T(8,128)(2,1)S(1)}, bf16[1024,512]{1,0:T(8,128)(2,1)S(1)}, f32[1,4,2,128,256]{4,3,2,1,0:T(8,128)S(1)}, f32[1024,512]{1,0:T(8,128)}) custom-call(s32[4]{0:T(128)S(1)} %pad_add_fusion.order_ref, bf16[1024,1664]{1,0:T(8,128)(2,1)} %convolution_convert_fusion.1.current_ref.before_ref, ...), custom_call_target="tpu_custom_call" | custom-call | flops 16106127360 | bytes 25165824 | tf_op jit(solution)/shard_map/mixer_forward/pallas_call | solution.py:365
  117.6 5.0 %collective-permute-done.8 = bf16[256,1024]{1,0:T(8,128)(2,1)} collective-permute-done((bf16[256,1024]{1,0:T(8,128)(2,1)}, bf16[256,1024]{1,0:T(8,128)(2,1)}, u32[]{:S(2)}, u32[]{:S(2)}) %collective-permute-start.8) | collective-permute-done | bytes 524320 | tf_op jit(solution)/shard_map/ppermute | solution.py:440
  126.5 2.6 slice.298
  131.2 10.0 %collective-permute-done.10 = bf16[256,512]{1,0:T(8,128)(2,1)} collective-permute-done((bf16[256,512]{1,0:T(8,128)(2,1)}, bf16[256,512]{1,0:T(8,128)(2,1)}, u32[]{:S(2)}, u32[]{:S(2)}) %collective-permute-start.10) | collective-permute-done | bytes 262176 | tf_op jit(solution)/shard_map/ppermute | solution.py:501
  141.2 6.4 %collective-permute-done.11 = bf16[256,512]{1,0:T(8,128)(2,1)} collective-permute-done((bf16[256,512]{1,0:T(8,128)(2,1)}, bf16[256,512]{1,0:T(8,128)(2,1)}, u32[]{:S(2)}, u32[]{:S(2)}) %collective-permute-start.11) | collective-permute-done | bytes 262176 | tf_op jit(solution)/shard_map/ppermute | solution.py:501
  147.6 2.5 multiply_reduce_fusion.2
  161.9 6.8 %collective-permute-done.15 = bf16[128,1024]{1,0:T(8,128)(2,1)S(1)} collective-permute-done((bf16[128,1024]{1,0:T(8,128)(2,1)S(1)}, bf16[128,1024]{1,0:T(8,128)(2,1)S(1)}, u32[]{:S(2)}, u32[]{:S(2)}) %collective-permute-start.15) | collective-permute-done | bytes 262176 | tf_op jit(solution)/shard_map/ppermute | solution.py:458
  169.5 2.2 collective-permute-start.19
  174.0 13.1 %collective-permute-done.17 = bf16[256,1024]{1,0:T(8,128)(2,1)S(1)} collective-permute-done((bf16[256,1024]{1,0:T(8,128)(2,1)S(1)}, bf16[256,1024]{1,0:T(8,128)(2,1)S(1)}, u32[]{:S(2)}, u32[]{:S(2)}) %collective-permute-start.17) | collective-permute-done | bytes 524320 | tf_op jit(solution)/shard_map/ppermute | solution.py:440
  190.2 2.6 slice.299
  195.9 6.2 %fusion.79 = f32[1024,1536]{0,1:T(8,128)S(1)} fusion(bf16[1024,1024]{1,0:T(8,128)(2,1)} %constant_dynamic-update-slice_fusion.11, bf16[1024,1536]{1,0:T(8,128)(2,1)} %all-gather.7.cloned.1.call-done), kind=kOutput, calls=%fused_computation.211 | convolution fusion | flops 3221225472 | bytes 11534336 | tf_op jit(solution)/shard_map/dot_general | solution.py:549
  202.1 5.7 %multiply_convert_fusion.2 = (bf16[1024,768]{0,1:T(8,128)(2,1)S(1)}, bf16[1024,768]{0,1:T(8,128)(2,1)S(1)}, bf16[1024,768]{0,1:T(8,128)(2,1)}) fusion(f32[1024,1536]{0,1:T(8,128)S(1)} %fusion.79, bf16[1024,1024]{1,0:T(8,128)(2,1)} %constant_dynamic-update-slice_fusion.6, bf16[704,1024]{1,0:T(8,128)(2,1)S(1)} %bitcast.182), kind=kOutput, calls=%fused_computation.21 | convolution fusion | flops 1622409216 | bytes 14548992 | tf_op jit(solution)/shard_map/tc,dc->td/dot_general | solution.py:553
  209.7 5.1 %fusion.77 = (bf16[1024,1024]{1,0:T(8,128)(2,1)S(1)}, f32[1024,1024]{1,0:T(8,128)}) fusion(bf16[1024,1536]{1,0:T(8,128)(2,1)S(1)} %copy-done.35, bf16[1024,768]{0,1:T(8,128)(2,1)S(1)} %get-tuple-element.74, bf16[1024,768]{0,1:T(8,128)(2,1)S(1)} %get-tuple-element.73), kind=kOutput, calls=%fused_computation.209 | convolution fusion | flops 3228565504 | bytes 12582912 | tf_op jit(solution)/shard_map/tc,dc->td/dot_general | solution.py:553
  217.7 6.6 %convolution_convert_fusion.2 = bf16[1024,1536]{1,0:T(8,128)(2,1)} fusion(bf16[1024,1024]{1,0:T(8,128)(2,1)} %constant_dynamic-update-slice_fusion.11, bf16[1024,1536]{0,1:T(8,128)(2,1)S(1)} %pad_maximum_fusion), kind=kOutput, calls=%fused_computation.17 | convolution fusion | flops 3222798336 | bytes 8388608 | tf_op jit(solution)/shard_map/tr,tc->rc/dot_general | solution.py:557
  224.4 7.2 %collective-permute-done.23 = bf16[128,1024]{1,0:T(8,128)(2,1)} collective-permute-done((bf16[128,1024]{1,0:T(8,128)(2,1)S(1)}, bf16[128,1024]{1,0:T(8,128)(2,1)}, u32[]{:S(2)}, u32[]{:S(2)}) %collective-permute-start.23) | collective-permute-done | bytes 262176 | tf_op jit(solution)/shard_map/ppermute | solution.py:477
  234.9 9.8 %collective-permute-done.22 = bf16[256,1024]{1,0:T(8,128)(2,1)S(1)} collective-permute-done((bf16[256,1024]{1,0:T(8,128)(2,1)S(1)}, bf16[256,1024]{1,0:T(8,128)(2,1)S(1)}, u32[]{:S(2)}, u32[]{:S(2)}) %collective-permute-start.22) | collective-permute-done | bytes 524320 | tf_op jit(solution)/shard_map/ppermute | solution.py:477
  244.7 10.9 %collective-permute-done.24 = bf16[256,1024]{1,0:T(8,128)(2,1)S(1)} collective-permute-done((bf16[256,1024]{1,0:T(8,128)(2,1)S(1)}, bf16[256,1024]{1,0:T(8,128)(2,1)S(1)}, u32[]{:S(2)}, u32[]{:S(2)}) %collective-permute-start.24) | collective-permute-done | bytes 524320 | tf_op jit(solution)/shard_map/ppermute | solution.py:477
  260.7 3.4 fusion.80
  264.1 19.1 %collective-permute-done.26 = bf16[256,1024]{1,0:T(8,128)(2,1)S(1)} collective-permute-done((bf16[256,1024]{1,0:T(8,128)(2,1)S(1)}, bf16[256,1024]{1,0:T(8,128)(2,1)S(1)}, u32[]{:S(2)}, u32[]{:S(2)}) %collective-permute-start.26) | collective-permute-done | bytes 524320 | tf_op jit(solution)/shard_map/ppermute | solution.py:439
  284.8 4.5 fusion.78
  289.4 7.5 %collective-permute-done.28 = bf16[128,1024]{1,0:T(8,128)(2,1)S(1)} collective-permute-done((bf16[128,1024]{1,0:T(8,128)(2,1)S(1)}, bf16[128,1024]{1,0:T(8,128)(2,1)S(1)}, u32[]{:S(2)}, u32[]{:S(2)}) %collective-permute-start.28) | collective-permute-done | bytes 262176 | tf_op jit(solution)/shard_map/ppermute | solution.py:459
  298.4 2.6 maximum_maximum_fusion
  301.0 2.5 convolution_convert_fusion.4.adjoint_ref
  306.3 26.8 %mixer_backward.1 = (bf16[1024,1664]{1,0:T(8,128)(2,1)}, f32[4,1024]{1,0:T(4,128)S(1)}, f32[8,128]{1,0:T(8,128)S(1)}, f32[1,256]{1,0:T(1,128)S(1)}) custom-call(s32[4]{0:T(128)S(1)} %pad_add_fusion.order_ref, bf16[1024,1664]{1,0:T(8,128)(2,1)} %convolution_convert_fusion.1.current_ref.before_ref, ...), custom_call_target="tpu_custom_call" | custom-call | flops 16106127360 | bytes 25165824 | tf_op jit(solution)/shard_map/mixer_backward/pallas_call | solution.py:365
  333.0 7.7 %convolution_convert_fusion = bf16[1024,1664]{1,0:T(8,128)(2,1)} fusion(bf16[1024,1664]{1,0:T(8,128)(2,1)} %get-tuple-element.61, bf16[1024,1024]{1,0:T(8,128)(2,1)S(1)} %copy-done.18, f32[1024]{0:T(1024)S(1)} %copy-done.32, f32[1024]{0:T(1024)S(1)} %add_rsqrt_fusion), kind=kOutput, calls=%fused_computation.15 | convolution fusion | flops 3495559168 | bytes 8921088 | tf_op jit(solution)/shard_map/tr,tc->rc/dot_general | solution.py:557
  340.7 10.6 %fusion.3 = (f32[1024]{0:T(1024)S(1)}, bf16[1024,1024]{1,0:T(8,128)(2,1)}, f32[1024,1024]{1,0:T(8,128)}) fusion(bf16[1024,1024]{1,0:T(8,128)(2,1)} %constant_dynamic-update-slice_fusion.1, f32[1024]{0:T(1024)S(1)} %add_rsqrt_fusion, bf16[1024,1664]{1,0:T(8,128)(2,1)} %get-tuple-element.61, bf16[1024,1664]{1,0:T(8,128)(2,1)} %all-gather.5.cloned.1.call-done), kind=kOutput, calls=%fused_computation.5 | convolution fusion | flops 3494902784 | bytes 15212544 | tf_op jit(solution)/shard_map/tc,dc->td/dot_general | solution.py:553
  360.0 8.2 %collective-permute-done.31 = bf16[256,1024]{1,0:T(8,128)(2,1)S(1)} collective-permute-done((bf16[256,1024]{1,0:T(8,128)(2,1)S(1)}, bf16[256,1024]{1,0:T(8,128)(2,1)S(1)}, u32[]{:S(2)}, u32[]{:S(2)}) %collective-permute-start.31) | collective-permute-done | bytes 524320 | tf_op jit(solution)/shard_map/ppermute | solution.py:477
  371.1 11.8 %collective-permute-done.40 = f32[148,128]{1,0:T(8,128)S(1)} collective-permute-done((f32[148,128]{1,0:T(8,128)S(1)}, f32[148,128]{1,0:T(8,128)S(1)}, u32[]{:S(2)}, u32[]{:S(2)}) %collective-permute-start.40) | collective-permute-done | bytes 75808 | tf_op jit(solution)/shard_map/ppermute | solution.py:529
  382.9 2.7 collective-permute-start.41
  387.0 21.0 %collective-permute-done.41 = f32[148,128]{1,0:T(8,128)S(1)} collective-permute-done((f32[148,128]{1,0:T(8,128)S(1)}, f32[148,128]{1,0:T(8,128)S(1)}, u32[]{:S(2)}, u32[]{:S(2)}) %collective-permute-start.41) | collective-permute-done | bytes 75808 | tf_op jit(solution)/shard_map/ppermute | solution.py:529
  411.0 5.5 %collective-permute-start.36 = (bf16[64,1024]{1,0:T(8,128)(2,1)S(1)}, bf16[64,1024]{1,0:T(8,128)(2,1)S(1)}, u32[]{:S(2)}, u32[]{:S(2)}) collective-permute-start(bf16[64,1024]{1,0:T(8,128)(2,1)S(1)} %slice.330), channel_id=1, source_target_pairs={{0,0},{1,8},{2,16},{3,24},{4,1},{5,9},{6,17},{7,25},{8,2},{9,10},{... | collective-permute-start | bytes 393224 | tf_op jit(solution)/shard_map/ppermute | solution.py:732
  417.7 18.4 %collective-permute-done.36 = bf16[64,1024]{1,0:T(8,128)(2,1)S(1)} collective-permute-done((bf16[64,1024]{1,0:T(8,128)(2,1)S(1)}, bf16[64,1024]{1,0:T(8,128)(2,1)S(1)}, u32[]{:S(2)}, u32[]{:S(2)}) %collective-permute-start.36) | collective-permute-done | bytes 131104 | tf_op jit(solution)/shard_map/ppermute | solution.py:732
  436.1 2.1 fusion.14
  441.2 2.5 collective-permute-start.33
  443.8 3.2 fusion.50
  449.2 12.3 %collective-permute-done.34 = bf16[32,3200]{1,0:T(8,128)(2,1)S(1)} collective-permute-done((bf16[32,3200]{1,0:T(8,128)(2,1)S(1)}, bf16[32,3200]{1,0:T(8,128)(2,1)S(1)}, u32[]{:S(2)}, u32[]{:S(2)}) %collective-permute-start.34) | collective-permute-done | bytes 204832 | tf_op jit(solution)/shard_map/ppermute | solution.py:510
  (311 shorter events, 101.0 us)
Async XLA Ops:
  7.2 82.2 %all-gather.5.cloned.1.call-start = ((), (), s32[]{:S(2)}) async-start(), calls=%async_computation.3 | async-start | bytes 3833856 | tf_op jit(solution)/shard_map/all_gather | solution.py:632
  7.3 35.4 %collective-permute-start.3 = (bf16[256,1024]{1,0:T(8,128)(2,1)}, bf16[256,1024]{1,0:T(8,128)(2,1)S(1)}, u32[]{:S(2)}, u32[]{:S(2)}) collective-permute-start(bf16[256,1024]{1,0:T(8,128)(2,1)} %bitcast.174), channel_id=1, source_target_pairs={{0,1},{1,2},{2,3},{3,0},{4,5},{5,6},{6,7},{7,4},{8,9},{9,10},{10,1... | collective-permute-start | bytes 1572872 | tf_op jit(solution)/shard_map/ppermute | solution.py:439
  8.6 34.0 %collective-permute-start.4 = (bf16[256,1024]{1,0:T(8,128)(2,1)}, bf16[256,1024]{1,0:T(8,128)(2,1)S(1)}, u32[]{:S(2)}, u32[]{:S(2)}) collective-permute-start(bf16[256,1024]{1,0:T(8,128)(2,1)} %bitcast.175), channel_id=1, source_target_pairs={{0,3},{1,0},{2,1},{3,2},{4,7},{5,4},{6,5},{7,6},{8,11},{9,8},{10,9... | collective-permute-start | bytes 1572872 | tf_op jit(solution)/shard_map/ppermute | solution.py:440
  14.5 19.4 %collective-permute-start = (bf16[32,1664]{1,0:T(8,128)(2,1)S(1)}, bf16[32,1664]{1,0:T(8,128)(2,1)S(1)}, u32[]{:S(2)}, u32[]{:S(2)}) collective-permute-start(bf16[32,1664]{1,0:T(8,128)(2,1)S(1)} %bitcast.199), channel_id=1, source_target_pairs={{0,1},{1,2},{2,3},{3,0},{4,5},{5,6},{6,7},{7,4},{8,9},{9,10},{10,1... | collective-permute-start | bytes 319496 | tf_op jit(solution)/shard_map/ppermute | solution.py:510
  15.9 23.9 %collective-permute-start.1 = (bf16[32,1664]{1,0:T(8,128)(2,1)S(1)}, bf16[32,1664]{1,0:T(8,128)(2,1)S(1)}, u32[]{:S(2)}, u32[]{:S(2)}) collective-permute-start(bf16[32,1664]{1,0:T(8,128)(2,1)S(1)} %bitcast.198), channel_id=1, source_target_pairs={{0,2},{1,3},{2,0},{3,1},{4,6},{5,7},{6,4},{7,5},{8,10},{9,11},{10,... | collective-permute-start | bytes 319496 | tf_op jit(solution)/shard_map/ppermute | solution.py:510
  18.8 23.7 %collective-permute-start.2 = (bf16[32,1664]{1,0:T(8,128)(2,1)S(1)}, bf16[32,1664]{1,0:T(8,128)(2,1)S(1)}, u32[]{:S(2)}, u32[]{:S(2)}) collective-permute-start(bf16[32,1664]{1,0:T(8,128)(2,1)S(1)} %bitcast.197), channel_id=1, source_target_pairs={{0,3},{1,0},{2,1},{3,2},{4,7},{5,4},{6,5},{7,6},{8,11},{9,8},{10,9... | collective-permute-start | bytes 319496 | tf_op jit(solution)/shard_map/ppermute | solution.py:510
  43.4 83.1 %all-gather.9.cloned.1.call-start = ((), (), s32[]{:S(2)}) async-start(), calls=%async_computation.8 | async-start | bytes 6488064 | tf_op jit(solution)/shard_map/all_gather | solution.py:640
  45.5 6.7 %collective-permute-start.12 = (bf16[32,3584]{1,0:T(8,128)(2,1)S(1)}, bf16[32,3584]{1,0:T(8,128)(2,1)S(1)}, u32[]{:S(2)}, u32[]{:S(2)}) collective-permute-start(bf16[32,3584]{1,0:T(8,128)(2,1)S(1)} %get-tuple-element.104), channel_id=1, source_target_pairs={{0,1},{1,2},{2,3},{3,0},{4,5},{5,6},{6,7},{7,4},{8,9},{9,10},{10,1... | collective-permute-start | bytes 688136 | tf_op jit(solution)/shard_map/ppermute | solution.py:510
  45.7 19.4 %collective-permute-start.13 = (bf16[32,3584]{1,0:T(8,128)(2,1)S(1)}, bf16[32,3584]{1,0:T(8,128)(2,1)S(1)}, u32[]{:S(2)}, u32[]{:S(2)}) collective-permute-start(bf16[32,3584]{1,0:T(8,128)(2,1)S(1)} %get-tuple-element.103), channel_id=1, source_target_pairs={{0,2},{1,3},{2,0},{3,1},{4,6},{5,7},{6,4},{7,5},{8,10},{9,11},{10,... | collective-permute-start | bytes 688136 | tf_op jit(solution)/shard_map/ppermute | solution.py:510
  46.7 20.9 %collective-permute-start.14 = (bf16[32,3584]{1,0:T(8,128)(2,1)S(1)}, bf16[32,3584]{1,0:T(8,128)(2,1)S(1)}, u32[]{:S(2)}, u32[]{:S(2)}) collective-permute-start(bf16[32,3584]{1,0:T(8,128)(2,1)S(1)} %get-tuple-element.102), channel_id=1, source_target_pairs={{0,3},{1,0},{2,1},{3,2},{4,7},{5,4},{6,5},{7,6},{8,11},{9,8},{10,9... | collective-permute-start | bytes 688136 | tf_op jit(solution)/shard_map/ppermute | solution.py:510
  69.9 126.0 %all-gather.7.cloned.1.call-start = ((), (), s32[]{:S(2)}) async-start(), calls=%async_computation.4 | async-start | bytes 3538944 | tf_op jit(solution)/shard_map/all_gather | solution.py:646
  72.3 7.6 %collective-permute-start.5 = (bf16[128,1024]{1,0:T(8,128)(2,1)S(1)}, bf16[128,1024]{1,0:T(8,128)(2,1)S(1)}, u32[]{:S(2)}, u32[]{:S(2)}) collective-permute-start(bf16[128,1024]{1,0:T(8,128)(2,1)S(1)} %slice.236), channel_id=1, source_target_pairs={{0,1},{1,2},{2,3},{3,0},{4,5},{5,6},{6,7},{7,4},{8,9},{9,10},{10,1... | collective-permute-start | bytes 786440 | tf_op jit(solution)/shard_map/ppermute | solution.py:458
  72.5 13.0 %collective-permute-start.6 = (bf16[128,1024]{1,0:T(8,128)(2,1)S(1)}, bf16[128,1024]{1,0:T(8,128)(2,1)S(1)}, u32[]{:S(2)}, u32[]{:S(2)}) collective-permute-start(bf16[128,1024]{1,0:T(8,128)(2,1)S(1)} %slice.237), channel_id=1, source_target_pairs={{0,3},{1,0},{2,1},{3,2},{4,7},{5,4},{6,5},{7,6},{8,11},{9,8},{10,9... | collective-permute-start | bytes 786440 | tf_op jit(solution)/shard_map/ppermute | solution.py:459
  75.6 228.2 %reduce-scatter.4.cloned.1.call-start = ((), (), s32[]{:S(2)}) async-start(), calls=%async_computation.5 | async-start | bytes 3538944 | tf_op jit(solution)/shard_map/reduce_scatter | solution.py:698
  97.1 20.6 %collective-permute-start.7 = (bf16[256,1024]{1,0:T(8,128)(2,1)}, bf16[256,1024]{1,0:T(8,128)(2,1)}, u32[]{:S(2)}, u32[]{:S(2)}) collective-permute-start(bf16[256,1024]{1,0:T(8,128)(2,1)} %bitcast.18), channel_id=1, source_target_pairs={{0,1},{1,2},{2,3},{3,0},{4,5},{5,6},{6,7},{7,4},{8,9},{9,10},{10,1... | collective-permute-start | bytes 1572872 | tf_op jit(solution)/shard_map/ppermute | solution.py:439
  97.1 25.6 %collective-permute-start.8 = (bf16[256,1024]{1,0:T(8,128)(2,1)}, bf16[256,1024]{1,0:T(8,128)(2,1)}, u32[]{:S(2)}, u32[]{:S(2)}) collective-permute-start(bf16[256,1024]{1,0:T(8,128)(2,1)} %bitcast.18), channel_id=1, source_target_pairs={{0,3},{1,0},{2,1},{3,2},{4,7},{5,4},{6,5},{7,6},{8,11},{9,8},{10,9... | collective-permute-start | bytes 1572872 | tf_op jit(solution)/shard_map/ppermute | solution.py:440
  123.5 17.7 %collective-permute-start.10 = (bf16[256,512]{1,0:T(8,128)(2,1)}, bf16[256,512]{1,0:T(8,128)(2,1)}, u32[]{:S(2)}, u32[]{:S(2)}) collective-permute-start(bf16[256,512]{1,0:T(8,128)(2,1)} %get-tuple-element.100), channel_id=1, source_target_pairs={{0,2},{1,3},{2,0},{3,1},{4,6},{5,7},{6,4},{7,5},{8,10},{9,11},{10,... | collective-permute-start | bytes 786440 | tf_op jit(solution)/shard_map/ppermute | solution.py:501
  124.6 23.0 %collective-permute-start.11 = (bf16[256,512]{1,0:T(8,128)(2,1)}, bf16[256,512]{1,0:T(8,128)(2,1)}, u32[]{:S(2)}, u32[]{:S(2)}) collective-permute-start(bf16[256,512]{1,0:T(8,128)(2,1)} %get-tuple-element.99), channel_id=1, source_target_pairs={{0,3},{1,0},{2,1},{3,2},{4,7},{5,4},{6,5},{7,6},{8,11},{9,8},{10,9... | collective-permute-start | bytes 786440 | tf_op jit(solution)/shard_map/ppermute | solution.py:501
  125.7 21.9 %collective-permute-start.9 = (bf16[256,512]{1,0:T(8,128)(2,1)}, bf16[256,512]{1,0:T(8,128)(2,1)}, u32[]{:S(2)}, u32[]{:S(2)}) collective-permute-start(bf16[256,512]{1,0:T(8,128)(2,1)} %get-tuple-element.101), channel_id=1, source_target_pairs={{0,1},{1,2},{2,3},{3,0},{4,5},{5,6},{6,7},{7,4},{8,9},{9,10},{10,1... | collective-permute-start | bytes 786440 | tf_op jit(solution)/shard_map/ppermute | solution.py:501
  151.4 18.1 %collective-permute-start.18 = (bf16[256,1024]{1,0:T(8,128)(2,1)S(1)}, bf16[256,1024]{1,0:T(8,128)(2,1)S(1)}, u32[]{:S(2)}, u32[]{:S(2)}) collective-permute-start(bf16[256,1024]{1,0:T(8,128)(2,1)S(1)} %get-tuple-element.72), channel_id=1, source_target_pairs={{0,1},{1,2},{2,3},{3,0},{4,5},{5,6},{6,7},{7,4},{8,9},{9,10},{10,1... | collective-permute-start | bytes 1572872 | tf_op jit(solution)/shard_map/ppermute | solution.py:439
  153.8 15.0 %collective-permute-start.15 = (bf16[128,1024]{1,0:T(8,128)(2,1)S(1)}, bf16[128,1024]{1,0:T(8,128)(2,1)S(1)}, u32[]{:S(2)}, u32[]{:S(2)}) collective-permute-start(bf16[128,1024]{1,0:T(8,128)(2,1)S(1)} %slice.244), channel_id=1, source_target_pairs={{0,1},{1,2},{2,3},{3,0},{4,5},{5,6},{6,7},{7,4},{8,9},{9,10},{10,1... | collective-permute-start | bytes 786440 | tf_op jit(solution)/shard_map/ppermute | solution.py:458
  154.8 18.4 %collective-permute-start.16 = (bf16[128,1024]{1,0:T(8,128)(2,1)S(1)}, bf16[128,1024]{1,0:T(8,128)(2,1)S(1)}, u32[]{:S(2)}, u32[]{:S(2)}) collective-permute-start(bf16[128,1024]{1,0:T(8,128)(2,1)S(1)} %slice.245), channel_id=1, source_target_pairs={{0,3},{1,0},{2,1},{3,2},{4,7},{5,4},{6,5},{7,6},{8,11},{9,8},{10,9... | collective-permute-start | bytes 786440 | tf_op jit(solution)/shard_map/ppermute | solution.py:459
  156.3 30.8 %collective-permute-start.17 = (bf16[256,1024]{1,0:T(8,128)(2,1)S(1)}, bf16[256,1024]{1,0:T(8,128)(2,1)S(1)}, u32[]{:S(2)}, u32[]{:S(2)}) collective-permute-start(bf16[256,1024]{1,0:T(8,128)(2,1)S(1)} %get-tuple-element.72), channel_id=1, source_target_pairs={{0,3},{1,0},{2,1},{3,2},{4,7},{5,4},{6,5},{7,6},{8,11},{9,8},{10,9... | collective-permute-start | bytes 1572872 | tf_op jit(solution)/shard_map/ppermute | solution.py:440
  169.5 24.2 %collective-permute-start.19 = (bf16[128,1024]{1,0:T(8,128)(2,1)S(1)}, bf16[128,1024]{1,0:T(8,128)(2,1)S(1)}, u32[]{:S(2)}, u32[]{:S(2)}) collective-permute-start(bf16[128,1024]{1,0:T(8,128)(2,1)S(1)} %slice.300), channel_id=1, source_target_pairs={{0,1},{1,2},{2,3},{3,0},{4,5},{5,6},{6,7},{7,4},{8,9},{9,10},{10,1... | collective-permute-start | bytes 786440 | tf_op jit(solution)/shard_map/ppermute | solution.py:458
  187.1 7.2 %collective-permute-start.20 = (bf16[128,1024]{1,0:T(8,128)(2,1)S(1)}, bf16[128,1024]{1,0:T(8,128)(2,1)S(1)}, u32[]{:S(2)}, u32[]{:S(2)}) collective-permute-start(bf16[128,1024]{1,0:T(8,128)(2,1)S(1)} %slice.301), channel_id=1, source_target_pairs={{0,3},{1,0},{2,1},{3,2},{4,7},{5,4},{6,5},{7,6},{8,11},{9,8},{10,9... | collective-permute-start | bytes 786440 | tf_op jit(solution)/shard_map/ppermute | solution.py:459
  215.6 8.8 %collective-permute-start.21 = (bf16[128,1024]{1,0:T(8,128)(2,1)}, bf16[128,1024]{1,0:T(8,128)(2,1)}, u32[]{:S(2)}, u32[]{:S(2)}) collective-permute-start(bf16[128,1024]{1,0:T(8,128)(2,1)} %get-tuple-element.94), channel_id=1, source_target_pairs={{0,1},{1,2},{2,3},{3,0},{4,5},{5,6},{6,7},{7,4},{8,9},{9,10},{10,1... | collective-permute-start | bytes 786440 | tf_op jit(solution)/shard_map/ppermute | solution.py:477
  215.9 15.6 %collective-permute-start.23 = (bf16[128,1024]{1,0:T(8,128)(2,1)S(1)}, bf16[128,1024]{1,0:T(8,128)(2,1)}, u32[]{:S(2)}, u32[]{:S(2)}) collective-permute-start(bf16[128,1024]{1,0:T(8,128)(2,1)S(1)} %get-tuple-element.95), channel_id=1, source_target_pairs={{0,3},{1,0},{2,1},{3,2},{4,7},{5,4},{6,5},{7,6},{8,11},{9,8},{10,9... | collective-permute-start | bytes 786440 | tf_op jit(solution)/shard_map/ppermute | solution.py:477
  224.3 127.1 %reduce-scatter.6.cloned.1.call-start = ((), (), s32[]{:S(2)}) async-start(), calls=%async_computation.6 | async-start | bytes 2949120 | tf_op jit(solution)/shard_map/reduce_scatter | solution.py:698
  233.1 11.6 %collective-permute-start.22 = (bf16[256,1024]{1,0:T(8,128)(2,1)S(1)}, bf16[256,1024]{1,0:T(8,128)(2,1)S(1)}, u32[]{:S(2)}, u32[]{:S(2)}) collective-permute-start(bf16[256,1024]{1,0:T(8,128)(2,1)S(1)} %pad_maximum_fusion.3), channel_id=1, source_target_pairs={{0,1},{1,2},{2,3},{3,0},{4,5},{5,6},{6,7},{7,4},{8,9},{9,10},{10,1... | collective-permute-start | bytes 1572872 | tf_op jit(solution)/shard_map/ppermute | solution.py:477
  233.2 22.4 %collective-permute-start.24 = (bf16[256,1024]{1,0:T(8,128)(2,1)S(1)}, bf16[256,1024]{1,0:T(8,128)(2,1)S(1)}, u32[]{:S(2)}, u32[]{:S(2)}) collective-permute-start(bf16[256,1024]{1,0:T(8,128)(2,1)S(1)} %pad_maximum_fusion.4), channel_id=1, source_target_pairs={{0,3},{1,0},{2,1},{3,2},{4,7},{5,4},{6,5},{7,6},{8,11},{9,8},{10,9... | collective-permute-start | bytes 1572872 | tf_op jit(solution)/shard_map/ppermute | solution.py:477
  259.1 25.4 %collective-permute-start.25 = (bf16[256,1024]{1,0:T(8,128)(2,1)S(1)}, bf16[256,1024]{1,0:T(8,128)(2,1)S(1)}, u32[]{:S(2)}, u32[]{:S(2)}) collective-permute-start(bf16[256,1024]{1,0:T(8,128)(2,1)S(1)} %get-tuple-element.70), channel_id=1, source_target_pairs={{0,3},{1,0},{2,1},{3,2},{4,7},{5,4},{6,5},{7,6},{8,11},{9,8},{10,9... | collective-permute-start | bytes 1572872 | tf_op jit(solution)/shard_map/ppermute | solution.py:440
  260.3 22.9 %collective-permute-start.26 = (bf16[256,1024]{1,0:T(8,128)(2,1)S(1)}, bf16[256,1024]{1,0:T(8,128)(2,1)S(1)}, u32[]{:S(2)}, u32[]{:S(2)}) collective-permute-start(bf16[256,1024]{1,0:T(8,128)(2,1)S(1)} %get-tuple-element.70), channel_id=1, source_target_pairs={{0,1},{1,2},{2,3},{3,0},{4,5},{5,6},{6,7},{7,4},{8,9},{9,10},{10,1... | collective-permute-start | bytes 1572872 | tf_op jit(solution)/shard_map/ppermute | solution.py:439
  283.2 6.2 %collective-permute-start.27 = (bf16[128,1024]{1,0:T(8,128)(2,1)S(1)}, bf16[128,1024]{1,0:T(8,128)(2,1)S(1)}, u32[]{:S(2)}, u32[]{:S(2)}) collective-permute-start(bf16[128,1024]{1,0:T(8,128)(2,1)S(1)} %slice.312), channel_id=1, source_target_pairs={{0,1},{1,2},{2,3},{3,0},{4,5},{5,6},{6,7},{7,4},{8,9},{9,10},{10,1... | collective-permute-start | bytes 786440 | tf_op jit(solution)/shard_map/ppermute | solution.py:458
  284.4 12.5 %collective-permute-start.28 = (bf16[128,1024]{1,0:T(8,128)(2,1)S(1)}, bf16[128,1024]{1,0:T(8,128)(2,1)S(1)}, u32[]{:S(2)}, u32[]{:S(2)}) collective-permute-start(bf16[128,1024]{1,0:T(8,128)(2,1)S(1)} %slice.313), channel_id=1, source_target_pairs={{0,3},{1,0},{2,1},{3,2},{4,7},{5,4},{6,5},{7,6},{8,11},{9,8},{10,9... | collective-permute-start | bytes 786440 | tf_op jit(solution)/shard_map/ppermute | solution.py:459
  303.5 136.3 %reduce-scatter.8.cloned.1.call-start = ((), (), s32[]{:S(2)}) async-start(), calls=%async_computation.7 | async-start | bytes 3833856 | tf_op jit(solution)/shard_map/reduce_scatter | solution.py:698
  351.9 3.5 collective-permute-start.37
  354.7 13.6 %collective-permute-start.31 = (bf16[256,1024]{1,0:T(8,128)(2,1)S(1)}, bf16[256,1024]{1,0:T(8,128)(2,1)S(1)}, u32[]{:S(2)}, u32[]{:S(2)}) collective-permute-start(bf16[256,1024]{1,0:T(8,128)(2,1)S(1)} %get-tuple-element.93), channel_id=1, source_target_pairs={{0,3},{1,0},{2,1},{3,2},{4,7},{5,4},{6,5},{7,6},{8,11},{9,8},{10,9... | collective-permute-start | bytes 1572872 | tf_op jit(solution)/shard_map/ppermute | solution.py:477
  355.4 3.7 collective-permute-start.38
  356.7 28.9 %collective-permute-start.29 = (bf16[256,1024]{1,0:T(8,128)(2,1)S(1)}, bf16[256,1024]{1,0:T(8,128)(2,1)S(1)}, u32[]{:S(2)}, u32[]{:S(2)}) collective-permute-start(bf16[256,1024]{1,0:T(8,128)(2,1)S(1)} %get-tuple-element.90), channel_id=1, source_target_pairs={{0,1},{1,2},{2,3},{3,0},{4,5},{5,6},{6,7},{7,4},{8,9},{9,10},{10,1... | collective-permute-start | bytes 1572872 | tf_op jit(solution)/shard_map/ppermute | solution.py:477
  359.1 9.4 %collective-permute-start.39 = (f32[148,128]{1,0:T(8,128)S(1)}, f32[148,128]{1,0:T(8,128)S(1)}, u32[]{:S(2)}, u32[]{:S(2)}) collective-permute-start(f32[148,128]{1,0:T(8,128)S(1)} %fusion.97), channel_id=1, source_target_pairs={{0,16},{4,20},{8,24},{12,28},{16,0},{20,4},{24,8},{28,12},{1,17},{... | collective-permute-start | bytes 227336 | tf_op jit(solution)/shard_map/ppermute | solution.py:529
  368.5 14.4 %collective-permute-start.40 = (f32[148,128]{1,0:T(8,128)S(1)}, f32[148,128]{1,0:T(8,128)S(1)}, u32[]{:S(2)}, u32[]{:S(2)}) collective-permute-start(f32[148,128]{1,0:T(8,128)S(1)} %add.287), channel_id=1, source_target_pairs={{0,1},{1,0},{2,3},{3,2},{4,5},{5,4},{6,7},{7,6},{8,9},{9,8},{10,11... | collective-permute-start | bytes 227336 | tf_op jit(solution)/shard_map/ppermute | solution.py:529
  370.6 65.5 %collective-permute-start.32 = (bf16[512,1024]{1,0:T(8,128)(2,1)}, bf16[512,1024]{1,0:T(8,128)(2,1)}, u32[]{:S(2)}, u32[]{:S(2)}) collective-permute-start(bf16[512,1024]{1,0:T(8,128)(2,1)} %pad_maximum_fusion.2), channel_id=1, source_target_pairs={{0,3},{1,0},{2,1},{3,2},{4,7},{5,4},{6,5},{7,6},{8,11},{9,8},{10,9... | collective-permute-start | bytes 3145736 | tf_op jit(solution)/shard_map/ppermute | solution.py:477
  382.9 25.0 %collective-permute-start.41 = (f32[148,128]{1,0:T(8,128)S(1)}, f32[148,128]{1,0:T(8,128)S(1)}, u32[]{:S(2)}, u32[]{:S(2)}) collective-permute-start(f32[148,128]{1,0:T(8,128)S(1)} %add.288), channel_id=1, source_target_pairs={{0,2},{1,3},{2,0},{3,1},{4,6},{5,7},{6,4},{7,5},{8,10},{9,11},{10,... | collective-permute-start | bytes 227336 | tf_op jit(solution)/shard_map/ppermute | solution.py:529
  387.0 49.1 %collective-permute-start.30 = (bf16[512,1024]{1,0:T(8,128)(2,1)}, bf16[512,1024]{1,0:T(8,128)(2,1)}, u32[]{:S(2)}, u32[]{:S(2)}) collective-permute-start(bf16[512,1024]{1,0:T(8,128)(2,1)} %pad_maximum_fusion.1), channel_id=1, source_target_pairs={{0,1},{1,2},{2,3},{3,0},{4,5},{5,6},{6,7},{7,4},{8,9},{9,10},{10,1... | collective-permute-start | bytes 3145736 | tf_op jit(solution)/shard_map/ppermute | solution.py:477
  411.0 25.1 %collective-permute-start.36 = (bf16[64,1024]{1,0:T(8,128)(2,1)S(1)}, bf16[64,1024]{1,0:T(8,128)(2,1)S(1)}, u32[]{:S(2)}, u32[]{:S(2)}) collective-permute-start(bf16[64,1024]{1,0:T(8,128)(2,1)S(1)} %slice.330), channel_id=1, source_target_pairs={{0,0},{1,8},{2,16},{3,24},{4,1},{5,9},{6,17},{7,25},{8,2},{9,10},{... | collective-permute-start | bytes 393224 | tf_op jit(solution)/shard_map/ppermute | solution.py:732
  441.2 8.0 %collective-permute-start.33 = (bf16[32,3200]{1,0:T(8,128)(2,1)S(1)}, bf16[32,3200]{1,0:T(8,128)(2,1)S(1)}, u32[]{:S(2)}, u32[]{:S(2)}) collective-permute-start(bf16[32,3200]{1,0:T(8,128)(2,1)S(1)} %get-tuple-element.114), channel_id=1, source_target_pairs={{0,1},{1,2},{2,3},{3,0},{4,5},{5,6},{6,7},{7,4},{8,9},{9,10},{10,1... | collective-permute-start | bytes 614408 | tf_op jit(solution)/shard_map/ppermute | solution.py:510
  446.9 14.6 %collective-permute-start.34 = (bf16[32,3200]{1,0:T(8,128)(2,1)S(1)}, bf16[32,3200]{1,0:T(8,128)(2,1)S(1)}, u32[]{:S(2)}, u32[]{:S(2)}) collective-permute-start(bf16[32,3200]{1,0:T(8,128)(2,1)S(1)} %get-tuple-element.115), channel_id=1, source_target_pairs={{0,2},{1,3},{2,0},{3,1},{4,6},{5,7},{6,4},{7,5},{8,10},{9,11},{10,... | collective-permute-start | bytes 614408 | tf_op jit(solution)/shard_map/ppermute | solution.py:510
  447.8 15.6 %collective-permute-start.35 = (bf16[32,3200]{1,0:T(8,128)(2,1)S(1)}, bf16[32,3200]{1,0:T(8,128)(2,1)S(1)}, u32[]{:S(2)}, u32[]{:S(2)}) collective-permute-start(bf16[32,3200]{1,0:T(8,128)(2,1)S(1)} %get-tuple-element.112), channel_id=1, source_target_pairs={{0,3},{1,0},{2,1},{3,2},{4,7},{5,4},{6,5},{7,6},{8,11},{9,8},{10,9... | collective-permute-start | bytes 614408 | tf_op jit(solution)/shard_map/ppermute | solution.py:510
  (38 other events, 428.7 us)
Sparse Core Ops, SparseCore 0:
  43.5 33.8 all-gather.4
  79.3 43.3 all-gather.8
  125.1 32.3 all-gather.6
  224.4 51.7 reduce-scatter.3
  303.6 44.4 reduce-scatter.5
  351.9 48.0 reduce-scatter.7

commit v4 on v3

--- a/solution.py
+++ b/solution.py
@@ -514,8 +514,8 @@
     return result
 
 
-def after(values, *others):
-    return lax.optimization_barrier((values, *others))[0]
+def together(*values):
+    return lax.optimization_barrier(values)
 
 
 def sum_everywhere(values):
@@ -631,7 +631,8 @@
     mixer_rows, near = lax.optimization_barrier((mixer_rows, near))
     mixer_weight = lax.all_gather(mixer_rows, "dp", axis=0, tiled=True)
     all_in = ring_gather(flat_in, "seq", near)
-    shared = exchange(after(jnp.concatenate([ffn_local, out_local], axis=2), near), "seq")
+    second_local, all_in = together(jnp.concatenate([ffn_local, out_local], axis=2), all_in)
+    shared = exchange(second_local, "seq")
     out_rows = ns * output_proj.shape[0]
     out_here = shared[:, :, 2 * padded :].reshape(out_rows, width)
     down_rows = ffn_down.shape[0]
@@ -674,8 +675,9 @@
     mixed, *saved = mixer_forward(
         projected, filters, side, gain_row, order, heads, seqs, chunk_rows
     )
-    cot_near = near_pieces(after(flat_cot, projected), "seq")
-    mixed, cot_near = lax.optimization_barrier((mixed, cot_near))
+    late_cot, projected = together(flat_cot, projected)
+    cot_near = near_pieces(late_cot, "seq")
+    mixed, cot_near = together(mixed, cot_near)
     all_cot = ring_gather(flat_cot, "seq", cot_near)
     mixed_parts = hand_out(mixed.reshape(ns, own, kv), "seq", 1)
     mixed_low = jnp.concatenate(mixed_parts, axis=1)
@@ -694,22 +696,23 @@
         [adj_gate.astype(BF16), (adj_act * gate_silu).astype(BF16)], axis=1
     )
     adj_partial_two = dot_nt(adj_both, ffn_weight)
-    adj_second, first_in = ring_reduce([adj_partial_two], "seq")
     scatter = lambda grad: lax.psum_scatter(
         grad.astype(BF16), "dp", scatter_dimension=0, tiled=True
     )
-    active_late, adj_both_late = after((active, adj_both), first_in)
+    adj_both_late, adj_partial_two = together(adj_both, adj_partial_two)
     grad_ffn = dot_tn(second_all, adj_both_late).astype(BF16)
+    adj_second, first_in = ring_reduce([adj_partial_two], "seq")
+    grad_ffn, adj_second = together(grad_ffn, adj_second)
     ffn_sums = scatter(grad_ffn)
-    adj_second = after(adj_second, grad_ffn)
-    grad_down = dot_tn(active_late, all_cot)[:hidden_own].astype(BF16)
 
     gain_two = jnp.sum(adj_second * unit_two, axis=0)
     adj_middle = flat_cot.astype(F32) + rms_back(unit_two, scale_two, ffn_gain, adj_second)
     attn_low = adj_middle.astype(BF16)
+    active_late, attn_low = together(active, attn_low)
     attn_near = near_pieces(attn_low, "seq")
-    active_late = after(active, attn_low)
     block_parts = dot(active_late, down_weight)
+    grad_down = dot_tn(active_late, all_cot)[:hidden_own].astype(BF16)
+    attn_near, block_parts, grad_down = together(attn_near, block_parts, grad_down)
     attn_all = ring_gather(attn_low, "seq", attn_near)
     adj_heads = dot_nt(attn_all, take_block(out_weight, me)).astype(BF16)
     grad_out = dot_tn(mixed, attn_all).astype(BF16)
@@ -723,8 +726,8 @@
         ],
         axis=1,
     ).reshape(-1, width)
+    adj_heads, both_grads, ffn_sums = together(adj_heads, both_grads, ffn_sums)
     both_sums = scatter(both_grads)
-    adj_heads = after(adj_heads, both_grads, ffn_sums)
     down_out = both_sums[head_rows : head_rows + down_rows]
     owners = [
         (place * ns + part, part * nd + place) for place in range(nd) for part in range(ns)
@@ -735,11 +738,13 @@
         projected, filters, side, gain_row, adj_heads, saved, order, heads, seqs, chunk_rows
     )
     grad_mixer = dot_tn(normed, adj_projected).astype(BF16)
-    mixer_sums = scatter(after(grad_mixer, both_sums))
-    adj_partial = dot_nt(after(adj_projected, grad_mixer), mixer_weight)
+    adj_projected, grad_mixer = together(adj_projected, grad_mixer)
+    mixer_sums = scatter(grad_mixer)
+    adj_partial = dot_nt(adj_projected, mixer_weight)
     gain_one = jnp.sum(adj_partial * unit_in, axis=0)
     reduced, _ = ring_reduce([adj_partial, block_parts], "seq")
     adj_normed, block_sum = reduced[:own], reduced[own:]
+    gain_one, adj_normed = together(gain_one, adj_normed)
     block_out = (middle + block_sum).astype(BF16).reshape(inputs.shape)
     shared = jnp.concatenate(
         [mixer_sums.reshape(ns, rows, -1), ffn_sums.reshape(ns, rows, -1)], axis=2

time: 487 us -> 506 us (1.039)
  the two profiles are of different devices: /device:TPU:11 before, /device:TPU:0 now
where the time goes in v4:
time: 506 us; the launch traced here: 496 us
  waiting for transfers between devices  214 us (42%)
  starting transfers between devices  77.3 us (15%)
  matrix products  58.9 us (12%)
  local copies, waits for them, and re-layouts  58 us (11%)
  Pallas kernels  44.7 us (9%)
  other arithmetic  26.9 us (5%)
  between operations  15.9 us (3%)
    ppermute x8, waiting for transfers between devices, ring_reduce(): lax.ppermute(part.astype(BF16), axis, shift_pairs(count, by)).astype(F32)  76.3 us
    ppermute x9, waiting for transfers between devices, exchange(): lax.ppermute(take_block(whole, (me + hop) % count), axis, shift_pairs(cou...  49.4 us
    pallas_call x2, Pallas kernels, mixer_call(): pl.pallas_call(kernel, grid_spec=pltpu.PrefetchScalarGridSpec(num_scalar_...  44.7 us
    ppermute x9, starting transfers between devices, exchange(): lax.ppermute(take_block(whole, (me + hop) % count), axis, shift_pairs(cou...  23.2 us
    ppermute x4, waiting for transfers between devices, ring_gather(): right = lax.ppermute(right[:half], axis, shift_pairs(count, 1))  22.5 us
    dot_general x4, matrix products, dot_nt(): return jnp.einsum('tc,dc->td', left, right, preferred_element_type=F32)  21.7 us
    unnamed x117, local copies, waits for them, and re-layouts  19.8 us
    dot_general x4, matrix products, dot_tn(): return jnp.einsum('tr,tc->rc', left, right, preferred_element_type=F32)  19.2 us
  transfers between devices with their start and end apart: 48, of which 29 were waited for; matrix products, arithmetic and copies ran while one was open for 22% of the time, Pallas kernels for 9%

profile of v4, /device:TPU:0, one launch (start us, length us, event | category | flops | bytes accessed | tf_op | source)
XLA Modules:
  0.0 495.9 jit_solution(1992394064657227400)
XLA Ops:
  7.3 3.1 collective-permute-start.3
  22.4 16.6 %collective-permute-done = bf16[32,1664]{1,0:T(8,128)(2,1)S(1)} collective-permute-done((bf16[32,1664]{1,0:T(8,128)(2,1)S(1)}, bf16[32,1664]{1,0:T(8,128)(2,1)S(1)}, u32[]{:S(2)}, u32[]{:S(2)}) %collective-permute-start) | collective-permute-done | bytes 106528 | tf_op jit(solution)/shard_map/ppermute | solution.py:510
  39.0 3.7 collective-permute-done.1
  45.9 2.8 collective-permute-start.5
  50.9 6.0 %collective-permute-done.5 = bf16[128,1024]{1,0:T(8,128)(2,1)S(1)} collective-permute-done((bf16[128,1024]{1,0:T(8,128)(2,1)S(1)}, bf16[128,1024]{1,0:T(8,128)(2,1)S(1)}, u32[]{:S(2)}, u32[]{:S(2)}) %collective-permute-start.5) | collective-permute-done | bytes 262176 | tf_op jit(solution)/shard_map/ppermute | solution.py:458
  57.0 4.5 collective-permute-done.6
  62.4 3.3 collective-permute-start.14
  65.7 6.4 %collective-permute-done.12 = bf16[32,3584]{1,0:T(8,128)(2,1)S(1)} collective-permute-done((bf16[32,3584]{1,0:T(8,128)(2,1)S(1)}, bf16[32,3584]{1,0:T(8,128)(2,1)S(1)}, u32[]{:S(2)}, u32[]{:S(2)}) %collective-permute-start.12) | collective-permute-done | bytes 229408 | tf_op jit(solution)/shard_map/ppermute | solution.py:510
  72.1 12.5 %collective-permute-done.13 = bf16[32,3584]{1,0:T(8,128)(2,1)S(1)} collective-permute-done((bf16[32,3584]{1,0:T(8,128)(2,1)S(1)}, bf16[32,3584]{1,0:T(8,128)(2,1)S(1)}, u32[]{:S(2)}, u32[]{:S(2)}) %collective-permute-start.13) | collective-permute-done | bytes 229408 | tf_op jit(solution)/shard_map/ppermute | solution.py:510
  92.8 7.7 %convolution_convert_fusion.1.current_ref.before_ref = bf16[1024,1664]{1,0:T(8,128)(2,1)} fusion(bf16[1024,1664]{1,0:T(8,128)(2,1)} %all-gather.5.cloned.1.call-done, bf16[1024,1024]{1,0:T(8,128)(2,1)S(1)} %constant_dynamic-update-slice_fusion.1, f32[1024]{0:T(1024)S(1)} %copy-done.36, f32[1024]{0:T(1024)S(1)} %add_rsqrt_fusion), kind=kOutput, calls=%fused_computation.16 | convolution fusion | flops 3495559168 | bytes 8921088 | tf_op jit(solution)/shard_map/dot_general | solution.py:549
  102.5 18.0 %mixer_forward.1 = (bf16[1024,512]{1,0:T(8,128)(2,1)S(1)}, bf16[1,4,2,256,256]{4,3,2,1,0:T(8,128)(2,1)S(1)}, bf16[1024,512]{1,0:T(8,128)(2,1)S(1)}, f32[1,4,2,128,256]{4,3,2,1,0:T(8,128)S(1)}, f32[1024,512]{1,0:T(8,128)}) custom-call(s32[4]{0:T(128)S(1)} %pad_add_fusion.order_ref, bf16[1024,1664]{1,0:T(8,128)(2,1)} %convolution_convert_fusion.1.current_ref.before_ref, ...), custom_call_target="tpu_custom_call" | custom-call | flops 16106127360 | bytes 25165824 | tf_op jit(solution)/shard_map/mixer_forward/pallas_call | solution.py:365
  121.5 3.0 collective-permute-done.8
  131.4 2.6 slice.298
  136.1 14.1 %collective-permute-done.10 = bf16[256,512]{1,0:T(8,128)(2,1)} collective-permute-done((bf16[256,512]{1,0:T(8,128)(2,1)}, bf16[256,512]{1,0:T(8,128)(2,1)}, u32[]{:S(2)}, u32[]{:S(2)}) %collective-permute-start.10) | collective-permute-done | bytes 262176 | tf_op jit(solution)/shard_map/ppermute | solution.py:501
  156.9 2.9 collective-permute-start.20
  165.6 10.7 %collective-permute-done.19 = bf16[128,1024]{1,0:T(8,128)(2,1)S(1)} collective-permute-done((bf16[128,1024]{1,0:T(8,128)(2,1)S(1)}, bf16[128,1024]{1,0:T(8,128)(2,1)S(1)}, u32[]{:S(2)}, u32[]{:S(2)}) %collective-permute-start.19) | collective-permute-done | bytes 262176 | tf_op jit(solution)/shard_map/ppermute | solution.py:458
  177.1 12.2 %collective-permute-start.17 = (bf16[128,1024]{1,0:T(8,128)(2,1)S(1)}, bf16[128,1024]{1,0:T(8,128)(2,1)S(1)}, u32[]{:S(2)}, u32[]{:S(2)}) collective-permute-start(bf16[128,1024]{1,0:T(8,128)(2,1)S(1)} %slice.299), channel_id=1, source_target_pairs={{0,1},{1,2},{2,3},{3,0},{4,5},{5,6},{6,7},{7,4},{8,9},{9,10},{10,1... | collective-permute-start | bytes 786440 | tf_op jit(solution)/shard_map/ppermute | solution.py:458
  190.0 3.1 collective-permute-done.15
  199.3 2.9 collective-permute-done.18
  203.8 6.0 %fusion.73 = f32[1024,1536]{1,0:T(8,128)S(1)} fusion(bf16[1024,1024]{1,0:T(8,128)(2,1)} %constant_dynamic-update-slice_fusion.6, bf16[1024,1536]{1,0:T(8,128)(2,1)} %all-gather.7.cloned.1.call-done), kind=kOutput, calls=%fused_computation.205 | convolution fusion | flops 3221225472 | bytes 11534336 | tf_op jit(solution)/shard_map/dot_general | solution.py:549
  209.9 6.3 %multiply_convert_fusion.1 = (bf16[1024,768]{1,0:T(8,128)(2,1)S(1)}, bf16[1024,768]{1,0:T(8,128)(2,1)S(1)}, bf16[1024,768]{1,0:T(8,128)(2,1)}) fusion(f32[1024,1536]{1,0:T(8,128)S(1)} %fusion.73, bf16[1024,1024]{1,0:T(8,128)(2,1)} %constant_dynamic-update-slice_fusion.11, bf16[704,1024]{1,0:T(8,128)(2,1)S(1)} %bitcast.181), kind=kOutput, calls=%fused_computation.20 | convolution fusion | flops 1622409216 | bytes 14548992 | tf_op jit(solution)/shard_map/tc,dc->td/dot_general | solution.py:553
  218.0 3.4 fusion.64
  222.5 3.2 collective-permute-start.23
  225.8 7.2 %collective-permute-done.21 = bf16[128,1024]{1,0:T(8,128)(2,1)S(1)} collective-permute-done((bf16[128,1024]{1,0:T(8,128)(2,1)S(1)}, bf16[128,1024]{1,0:T(8,128)(2,1)S(1)}, u32[]{:S(2)}, u32[]{:S(2)}) %collective-permute-start.21) | collective-permute-done | bytes 262176 | tf_op jit(solution)/shard_map/ppermute | solution.py:477
  233.0 2.7 collective-permute-done.23
  239.7 6.6 %convolution_convert_fusion.2 = bf16[1024,1536]{1,0:T(8,128)(2,1)} fusion(bf16[1024,1024]{1,0:T(8,128)(2,1)} %constant_dynamic-update-slice_fusion.6, bf16[1024,1536]{1,0:T(8,128)(2,1)S(1)} %pad_maximum_fusion), kind=kOutput, calls=%fused_computation.17 | convolution fusion | flops 3222798336 | bytes 8388608 | tf_op jit(solution)/shard_map/tr,tc->rc/dot_general | solution.py:557
  246.3 5.1 %collective-permute-done.24 = bf16[256,1024]{1,0:T(8,128)(2,1)} collective-permute-done((bf16[256,1024]{1,0:T(8,128)(2,1)}, bf16[256,1024]{1,0:T(8,128)(2,1)}, u32[]{:S(2)}, u32[]{:S(2)}) %collective-permute-start.24) | collective-permute-done | bytes 524320 | tf_op jit(solution)/shard_map/ppermute | solution.py:477
  251.4 10.8 %collective-permute-done.22 = bf16[256,1024]{1,0:T(8,128)(2,1)} collective-permute-done((bf16[256,1024]{1,0:T(8,128)(2,1)}, bf16[256,1024]{1,0:T(8,128)(2,1)}, u32[]{:S(2)}, u32[]{:S(2)}) %collective-permute-start.22) | collective-permute-done | bytes 524320 | tf_op jit(solution)/shard_map/ppermute | solution.py:477
  262.2 2.8 convert_add_fusion.1
  270.9 3.5 fusion.74
  278.3 4.9 collective-permute-done.26
  283.2 11.3 %collective-permute-done.25 = bf16[256,1024]{1,0:T(8,128)(2,1)S(1)} collective-permute-done((bf16[256,1024]{1,0:T(8,128)(2,1)S(1)}, bf16[256,1024]{1,0:T(8,128)(2,1)S(1)}, u32[]{:S(2)}, u32[]{:S(2)}) %collective-permute-start.25) | collective-permute-done | bytes 524320 | tf_op jit(solution)/shard_map/ppermute | solution.py:439
  299.8 5.8 %collective-permute-done.27 = bf16[128,1024]{1,0:T(8,128)(2,1)S(1)} collective-permute-done((bf16[128,1024]{1,0:T(8,128)(2,1)S(1)}, bf16[128,1024]{1,0:T(8,128)(2,1)S(1)}, u32[]{:S(2)}, u32[]{:S(2)}) %collective-permute-start.27) | collective-permute-done | bytes 262176 | tf_op jit(solution)/shard_map/ppermute | solution.py:458
  305.6 3.9 collective-permute-done.28
  318.9 26.7 %mixer_backward.1 = (bf16[1024,1664]{1,0:T(8,128)(2,1)}, f32[4,1024]{1,0:T(4,128)S(1)}, f32[8,128]{1,0:T(8,128)S(1)}, f32[1,256]{1,0:T(1,128)S(1)}) custom-call(s32[4]{0:T(128)S(1)} %pad_add_fusion.order_ref, bf16[1024,1664]{1,0:T(8,128)(2,1)} %convolution_convert_fusion.1.current_ref.before_ref, ...), custom_call_target="tpu_custom_call" | custom-call | flops 16106127360 | bytes 25165824 | tf_op jit(solution)/shard_map/mixer_backward/pallas_call | solution.py:365
  345.6 7.8 %convolution_convert_fusion = bf16[1024,1664]{1,0:T(8,128)(2,1)} fusion(bf16[1024,1664]{1,0:T(8,128)(2,1)} %get-tuple-element.81, bf16[1024,1024]{1,0:T(8,128)(2,1)S(1)} %copy-done.20, f32[1024]{0:T(1024)S(1)} %copy-done.36, f32[1024]{0:T(1024)S(1)} %add_rsqrt_fusion), kind=kOutput, calls=%fused_computation.15 | convolution fusion | flops 3495559168 | bytes 8921088 | tf_op jit(solution)/shard_map/tr,tc->rc/dot_general | solution.py:557
  353.4 9.5 %fusion.3 = (f32[1024]{0:T(1024)S(1)}, bf16[1024,1024]{1,0:T(8,128)(2,1)S(1)}, f32[1024,1024]{1,0:T(8,128)}) fusion(bf16[1024,1024]{1,0:T(8,128)(2,1)S(1)} %copy-done.21, f32[1024]{0:T(1024)S(1)} %add_rsqrt_fusion, bf16[1024,1664]{1,0:T(8,128)(2,1)} %get-tuple-element.81, bf16[1024,1664]{1,0:T(8,128)(2,1)} %all-gather.5.cloned.1.call-done), kind=kOutput, calls=%fused_computation.5 | convolution fusion | flops 3494902784 | bytes 15212544 | tf_op jit(solution)/shard_map/tc,dc->td/dot_general | solution.py:553
  365.8 3.4 collective-permute-start.32
  369.2 11.6 %collective-permute-done.29 = bf16[256,1024]{1,0:T(8,128)(2,1)} collective-permute-done((bf16[256,1024]{1,0:T(8,128)(2,1)}, bf16[256,1024]{1,0:T(8,128)(2,1)}, u32[]{:S(2)}, u32[]{:S(2)}) %collective-permute-start.29) | collective-permute-done | bytes 524320 | tf_op jit(solution)/shard_map/ppermute | solution.py:477
  384.3 18.0 %collective-permute-done.32 = bf16[512,1024]{1,0:T(8,128)(2,1)} collective-permute-done((bf16[512,1024]{1,0:T(8,128)(2,1)S(1)}, bf16[512,1024]{1,0:T(8,128)(2,1)}, u32[]{:S(2)}, u32[]{:S(2)}) %collective-permute-start.32) | collective-permute-done | bytes 1048608 | tf_op jit(solution)/shard_map/ppermute | solution.py:477
  402.3 21.0 %collective-permute-done.30 = bf16[512,1024]{1,0:T(8,128)(2,1)} collective-permute-done((bf16[512,1024]{1,0:T(8,128)(2,1)}, bf16[512,1024]{1,0:T(8,128)(2,1)}, u32[]{:S(2)}, u32[]{:S(2)}) %collective-permute-start.30) | collective-permute-done | bytes 1048608 | tf_op jit(solution)/shard_map/ppermute | solution.py:477
  429.5 4.7 collective-permute-done.38
  438.8 4.4 collective-permute-done.40
  445.8 3.1 collective-permute-done.41
  454.7 3.6 collective-permute-start.33
  459.6 4.8 collective-permute-start.35
  464.3 6.9 %collective-permute-start.34 = (bf16[32,3200]{1,0:T(8,128)(2,1)S(1)}, bf16[32,3200]{1,0:T(8,128)(2,1)S(1)}, u32[]{:S(2)}, u32[]{:S(2)}) collective-permute-start(bf16[32,3200]{1,0:T(8,128)(2,1)S(1)} %get-tuple-element.137), channel_id=1, source_target_pairs={{0,2},{1,3},{2,0},{3,1},{4,6},{5,7},{6,4},{7,5},{8,10},{9,11},{10,... | collective-permute-start | bytes 614408 | tf_op jit(solution)/shard_map/ppermute | solution.py:510
  471.3 10.2 %collective-permute-done.34 = bf16[32,3200]{1,0:T(8,128)(2,1)S(1)} collective-permute-done((bf16[32,3200]{1,0:T(8,128)(2,1)S(1)}, bf16[32,3200]{1,0:T(8,128)(2,1)S(1)}, u32[]{:S(2)}, u32[]{:S(2)}) %collective-permute-start.34) | collective-permute-done | bytes 204832 | tf_op jit(solution)/shard_map/ppermute | solution.py:510
  (323 shorter events, 124.7 us)
Async XLA Ops:
  7.2 85.5 %all-gather.5.cloned.1.call-start = ((), (), s32[]{:S(2)}) async-start(), calls=%async_computation.3 | async-start | bytes 3833856 | tf_op jit(solution)/shard_map/all_gather | solution.py:632
  7.3 35.5 %collective-permute-start.3 = (bf16[256,1024]{1,0:T(8,128)(2,1)}, bf16[256,1024]{1,0:T(8,128)(2,1)S(1)}, u32[]{:S(2)}, u32[]{:S(2)}) collective-permute-start(bf16[256,1024]{1,0:T(8,128)(2,1)} %bitcast.173), channel_id=1, source_target_pairs={{0,1},{1,2},{2,3},{3,0},{4,5},{5,6},{6,7},{7,4},{8,9},{9,10},{10,1... | collective-permute-start | bytes 1572872 | tf_op jit(solution)/shard_map/ppermute | solution.py:439
  10.3 32.4 %collective-permute-start.4 = (bf16[256,1024]{1,0:T(8,128)(2,1)}, bf16[256,1024]{1,0:T(8,128)(2,1)S(1)}, u32[]{:S(2)}, u32[]{:S(2)}) collective-permute-start(bf16[256,1024]{1,0:T(8,128)(2,1)} %bitcast.174), channel_id=1, source_target_pairs={{0,3},{1,0},{2,1},{3,2},{4,7},{5,4},{6,5},{7,6},{8,11},{9,8},{10,9... | collective-permute-start | bytes 1572872 | tf_op jit(solution)/shard_map/ppermute | solution.py:440
  18.2 20.8 %collective-permute-start = (bf16[32,1664]{1,0:T(8,128)(2,1)S(1)}, bf16[32,1664]{1,0:T(8,128)(2,1)S(1)}, u32[]{:S(2)}, u32[]{:S(2)}) collective-permute-start(bf16[32,1664]{1,0:T(8,128)(2,1)S(1)} %bitcast.198), channel_id=1, source_target_pairs={{0,1},{1,2},{2,3},{3,0},{4,5},{5,6},{6,7},{7,4},{8,9},{9,10},{10,1... | collective-permute-start | bytes 319496 | tf_op jit(solution)/shard_map/ppermute | solution.py:510
  18.3 24.4 %collective-permute-start.1 = (bf16[32,1664]{1,0:T(8,128)(2,1)S(1)}, bf16[32,1664]{1,0:T(8,128)(2,1)S(1)}, u32[]{:S(2)}, u32[]{:S(2)}) collective-permute-start(bf16[32,1664]{1,0:T(8,128)(2,1)S(1)} %bitcast.197), channel_id=1, source_target_pairs={{0,2},{1,3},{2,0},{3,1},{4,6},{5,7},{6,4},{7,5},{8,10},{9,11},{10,... | collective-permute-start | bytes 319496 | tf_op jit(solution)/shard_map/ppermute | solution.py:510
  20.8 21.8 %collective-permute-start.2 = (bf16[32,1664]{1,0:T(8,128)(2,1)S(1)}, bf16[32,1664]{1,0:T(8,128)(2,1)S(1)}, u32[]{:S(2)}, u32[]{:S(2)}) collective-permute-start(bf16[32,1664]{1,0:T(8,128)(2,1)S(1)} %bitcast.196), channel_id=1, source_target_pairs={{0,3},{1,0},{2,1},{3,2},{4,7},{5,4},{6,5},{7,6},{8,11},{9,8},{10,9... | collective-permute-start | bytes 319496 | tf_op jit(solution)/shard_map/ppermute | solution.py:510
  43.8 87.6 %all-gather.9.cloned.1.call-start = ((), (), s32[]{:S(2)}) async-start(), calls=%async_computation.8 | async-start | bytes 6488064 | tf_op jit(solution)/shard_map/all_gather | solution.py:641
  45.9 11.1 %collective-permute-start.5 = (bf16[128,1024]{1,0:T(8,128)(2,1)S(1)}, bf16[128,1024]{1,0:T(8,128)(2,1)S(1)}, u32[]{:S(2)}, u32[]{:S(2)}) collective-permute-start(bf16[128,1024]{1,0:T(8,128)(2,1)S(1)} %slice.236), channel_id=1, source_target_pairs={{0,1},{1,2},{2,3},{3,0},{4,5},{5,6},{6,7},{7,4},{8,9},{9,10},{10,1... | collective-permute-start | bytes 786440 | tf_op jit(solution)/shard_map/ppermute | solution.py:458
  48.6 12.8 %collective-permute-start.6 = (bf16[128,1024]{1,0:T(8,128)(2,1)S(1)}, bf16[128,1024]{1,0:T(8,128)(2,1)S(1)}, u32[]{:S(2)}, u32[]{:S(2)}) collective-permute-start(bf16[128,1024]{1,0:T(8,128)(2,1)S(1)} %slice.237), channel_id=1, source_target_pairs={{0,3},{1,0},{2,1},{3,2},{4,7},{5,4},{6,5},{7,6},{8,11},{9,8},{10,9... | collective-permute-start | bytes 786440 | tf_op jit(solution)/shard_map/ppermute | solution.py:459
  61.7 10.3 %collective-permute-start.12 = (bf16[32,3584]{1,0:T(8,128)(2,1)S(1)}, bf16[32,3584]{1,0:T(8,128)(2,1)S(1)}, u32[]{:S(2)}, u32[]{:S(2)}) collective-permute-start(bf16[32,3584]{1,0:T(8,128)(2,1)S(1)} %get-tuple-element.126), channel_id=1, source_target_pairs={{0,1},{1,2},{2,3},{3,0},{4,5},{5,6},{6,7},{7,4},{8,9},{9,10},{10,1... | collective-permute-start | bytes 688136 | tf_op jit(solution)/shard_map/ppermute | solution.py:510
  62.4 22.2 %collective-permute-start.14 = (bf16[32,3584]{1,0:T(8,128)(2,1)S(1)}, bf16[32,3584]{1,0:T(8,128)(2,1)S(1)}, u32[]{:S(2)}, u32[]{:S(2)}) collective-permute-start(bf16[32,3584]{1,0:T(8,128)(2,1)S(1)} %get-tuple-element.124), channel_id=1, source_target_pairs={{0,3},{1,0},{2,1},{3,2},{4,7},{5,4},{6,5},{7,6},{8,11},{9,8},{10,9... | collective-permute-start | bytes 688136 | tf_op jit(solution)/shard_map/ppermute | solution.py:510
  65.7 18.9 %collective-permute-start.13 = (bf16[32,3584]{1,0:T(8,128)(2,1)S(1)}, bf16[32,3584]{1,0:T(8,128)(2,1)S(1)}, u32[]{:S(2)}, u32[]{:S(2)}) collective-permute-start(bf16[32,3584]{1,0:T(8,128)(2,1)S(1)} %get-tuple-element.125), channel_id=1, source_target_pairs={{0,2},{1,3},{2,0},{3,1},{4,6},{5,7},{6,4},{7,5},{8,10},{9,11},{10,... | collective-permute-start | bytes 688136 | tf_op jit(solution)/shard_map/ppermute | solution.py:510
  89.7 114.1 %all-gather.7.cloned.1.call-start = ((), (), s32[]{:S(2)}) async-start(), calls=%async_computation.4 | async-start | bytes 3538944 | tf_op jit(solution)/shard_map/all_gather | solution.py:647
  92.6 223.5 %reduce-scatter.4.cloned.1.call-start = ((), (), s32[]{:S(2)}) async-start(), calls=%async_computation.5 | async-start | bytes 3538944 | tf_op jit(solution)/shard_map/reduce_scatter | solution.py:699
  100.4 24.1 %collective-permute-start.8 = (bf16[256,1024]{1,0:T(8,128)(2,1)}, bf16[256,1024]{1,0:T(8,128)(2,1)}, u32[]{:S(2)}, u32[]{:S(2)}) collective-permute-start(bf16[256,1024]{1,0:T(8,128)(2,1)} %bitcast.20), channel_id=1, source_target_pairs={{0,3},{1,0},{2,1},{3,2},{4,7},{5,4},{6,5},{7,6},{8,11},{9,8},{10,9... | collective-permute-start | bytes 1572872 | tf_op jit(solution)/shard_map/ppermute | solution.py:440
  101.1 23.4 %collective-permute-start.7 = (bf16[256,1024]{1,0:T(8,128)(2,1)}, bf16[256,1024]{1,0:T(8,128)(2,1)}, u32[]{:S(2)}, u32[]{:S(2)}) collective-permute-start(bf16[256,1024]{1,0:T(8,128)(2,1)} %bitcast.20), channel_id=1, source_target_pairs={{0,1},{1,2},{2,3},{3,0},{4,5},{5,6},{6,7},{7,4},{8,9},{9,10},{10,1... | collective-permute-start | bytes 1572872 | tf_op jit(solution)/shard_map/ppermute | solution.py:439
  125.4 10.7 %collective-permute-start.11 = (bf16[256,512]{1,0:T(8,128)(2,1)}, bf16[256,512]{1,0:T(8,128)(2,1)}, u32[]{:S(2)}, u32[]{:S(2)}) collective-permute-start(bf16[256,512]{1,0:T(8,128)(2,1)} %get-tuple-element.121), channel_id=1, source_target_pairs={{0,3},{1,0},{2,1},{3,2},{4,7},{5,4},{6,5},{7,6},{8,11},{9,8},{10,9... | collective-permute-start | bytes 786440 | tf_op jit(solution)/shard_map/ppermute | solution.py:501
  126.3 24.0 %collective-permute-start.10 = (bf16[256,512]{1,0:T(8,128)(2,1)}, bf16[256,512]{1,0:T(8,128)(2,1)}, u32[]{:S(2)}, u32[]{:S(2)}) collective-permute-start(bf16[256,512]{1,0:T(8,128)(2,1)} %get-tuple-element.122), channel_id=1, source_target_pairs={{0,2},{1,3},{2,0},{3,1},{4,6},{5,7},{6,4},{7,5},{8,10},{9,11},{10,... | collective-permute-start | bytes 786440 | tf_op jit(solution)/shard_map/ppermute | solution.py:501
  127.8 22.5 %collective-permute-start.9 = (bf16[256,512]{1,0:T(8,128)(2,1)}, bf16[256,512]{1,0:T(8,128)(2,1)}, u32[]{:S(2)}, u32[]{:S(2)}) collective-permute-start(bf16[256,512]{1,0:T(8,128)(2,1)} %get-tuple-element.123), channel_id=1, source_target_pairs={{0,1},{1,2},{2,3},{3,0},{4,5},{5,6},{6,7},{7,4},{8,9},{9,10},{10,1... | collective-permute-start | bytes 786440 | tf_op jit(solution)/shard_map/ppermute | solution.py:501
  154.0 23.1 %collective-permute-start.16 = (bf16[256,1024]{1,0:T(8,128)(2,1)S(1)}, bf16[256,1024]{1,0:T(8,128)(2,1)S(1)}, u32[]{:S(2)}, u32[]{:S(2)}) collective-permute-start(bf16[256,1024]{1,0:T(8,128)(2,1)S(1)} %get-tuple-element.94), channel_id=1, source_target_pairs={{0,1},{1,2},{2,3},{3,0},{4,5},{5,6},{6,7},{7,4},{8,9},{9,10},{10,1... | collective-permute-start | bytes 1572872 | tf_op jit(solution)/shard_map/ppermute | solution.py:439
  155.9 20.4 %collective-permute-start.19 = (bf16[128,1024]{1,0:T(8,128)(2,1)S(1)}, bf16[128,1024]{1,0:T(8,128)(2,1)S(1)}, u32[]{:S(2)}, u32[]{:S(2)}) collective-permute-start(bf16[128,1024]{1,0:T(8,128)(2,1)S(1)} %slice.249), channel_id=1, source_target_pairs={{0,1},{1,2},{2,3},{3,0},{4,5},{5,6},{6,7},{7,4},{8,9},{9,10},{10,1... | collective-permute-start | bytes 786440 | tf_op jit(solution)/shard_map/ppermute | solution.py:458
  156.9 32.3 %collective-permute-start.20 = (bf16[128,1024]{1,0:T(8,128)(2,1)S(1)}, bf16[128,1024]{1,0:T(8,128)(2,1)S(1)}, u32[]{:S(2)}, u32[]{:S(2)}) collective-permute-start(bf16[128,1024]{1,0:T(8,128)(2,1)S(1)} %slice.250), channel_id=1, source_target_pairs={{0,3},{1,0},{2,1},{3,2},{4,7},{5,4},{6,5},{7,6},{8,11},{9,8},{10,9... | collective-permute-start | bytes 786440 | tf_op jit(solution)/shard_map/ppermute | solution.py:459
  159.9 33.2 %collective-permute-start.15 = (bf16[256,1024]{1,0:T(8,128)(2,1)S(1)}, bf16[256,1024]{1,0:T(8,128)(2,1)S(1)}, u32[]{:S(2)}, u32[]{:S(2)}) collective-permute-start(bf16[256,1024]{1,0:T(8,128)(2,1)S(1)} %get-tuple-element.94), channel_id=1, source_target_pairs={{0,3},{1,0},{2,1},{3,2},{4,7},{5,4},{6,5},{7,6},{8,11},{9,8},{10,9... | collective-permute-start | bytes 1572872 | tf_op jit(solution)/shard_map/ppermute | solution.py:440
  177.1 21.5 %collective-permute-start.17 = (bf16[128,1024]{1,0:T(8,128)(2,1)S(1)}, bf16[128,1024]{1,0:T(8,128)(2,1)S(1)}, u32[]{:S(2)}, u32[]{:S(2)}) collective-permute-start(bf16[128,1024]{1,0:T(8,128)(2,1)S(1)} %slice.299), channel_id=1, source_target_pairs={{0,1},{1,2},{2,3},{3,0},{4,5},{5,6},{6,7},{7,4},{8,9},{9,10},{10,1... | collective-permute-start | bytes 786440 | tf_op jit(solution)/shard_map/ppermute | solution.py:458
  193.1 9.1 %collective-permute-start.18 = (bf16[128,1024]{1,0:T(8,128)(2,1)S(1)}, bf16[128,1024]{1,0:T(8,128)(2,1)S(1)}, u32[]{:S(2)}, u32[]{:S(2)}) collective-permute-start(bf16[128,1024]{1,0:T(8,128)(2,1)S(1)} %slice.300), channel_id=1, source_target_pairs={{0,3},{1,0},{2,1},{3,2},{4,7},{5,4},{6,5},{7,6},{8,11},{9,8},{10,9... | collective-permute-start | bytes 786440 | tf_op jit(solution)/shard_map/ppermute | solution.py:459
  221.9 11.1 %collective-permute-start.21 = (bf16[128,1024]{1,0:T(8,128)(2,1)S(1)}, bf16[128,1024]{1,0:T(8,128)(2,1)S(1)}, u32[]{:S(2)}, u32[]{:S(2)}) collective-permute-start(bf16[128,1024]{1,0:T(8,128)(2,1)S(1)} %get-tuple-element.116), channel_id=1, source_target_pairs={{0,1},{1,2},{2,3},{3,0},{4,5},{5,6},{6,7},{7,4},{8,9},{9,10},{10,1... | collective-permute-start | bytes 786440 | tf_op jit(solution)/shard_map/ppermute | solution.py:477
  222.5 13.1 %collective-permute-start.23 = (bf16[128,1024]{1,0:T(8,128)(2,1)S(1)}, bf16[128,1024]{1,0:T(8,128)(2,1)S(1)}, u32[]{:S(2)}, u32[]{:S(2)}) collective-permute-start(bf16[128,1024]{1,0:T(8,128)(2,1)S(1)} %get-tuple-element.117), channel_id=1, source_target_pairs={{0,3},{1,0},{2,1},{3,2},{4,7},{5,4},{6,5},{7,6},{8,11},{9,8},{10,9... | collective-permute-start | bytes 786440 | tf_op jit(solution)/shard_map/ppermute | solution.py:477
  236.7 14.8 %collective-permute-start.24 = (bf16[256,1024]{1,0:T(8,128)(2,1)}, bf16[256,1024]{1,0:T(8,128)(2,1)}, u32[]{:S(2)}, u32[]{:S(2)}) collective-permute-start(bf16[256,1024]{1,0:T(8,128)(2,1)} %pad_maximum_fusion.4), channel_id=1, source_target_pairs={{0,3},{1,0},{2,1},{3,2},{4,7},{5,4},{6,5},{7,6},{8,11},{9,8},{10,9... | collective-permute-start | bytes 1572872 | tf_op jit(solution)/shard_map/ppermute | solution.py:477
  239.6 22.6 %collective-permute-start.22 = (bf16[256,1024]{1,0:T(8,128)(2,1)}, bf16[256,1024]{1,0:T(8,128)(2,1)}, u32[]{:S(2)}, u32[]{:S(2)}) collective-permute-start(bf16[256,1024]{1,0:T(8,128)(2,1)} %pad_maximum_fusion.3), channel_id=1, source_target_pairs={{0,1},{1,2},{2,3},{3,0},{4,5},{5,6},{6,7},{7,4},{8,9},{9,10},{10,1... | collective-permute-start | bytes 1572872 | tf_op jit(solution)/shard_map/ppermute | solution.py:477
  265.0 186.8 %reduce-scatter.8.cloned.1.call-start = ((), (), s32[]{:S(2)}) async-start(), calls=%async_computation.7 | async-start | bytes 2949120 | tf_op jit(solution)/shard_map/reduce_scatter | solution.py:699
  268.4 14.8 %collective-permute-start.26 = (bf16[256,1024]{1,0:T(8,128)(2,1)S(1)}, bf16[256,1024]{1,0:T(8,128)(2,1)S(1)}, u32[]{:S(2)}, u32[]{:S(2)}) collective-permute-start(bf16[256,1024]{1,0:T(8,128)(2,1)S(1)} %fusion.63), channel_id=1, source_target_pairs={{0,3},{1,0},{2,1},{3,2},{4,7},{5,4},{6,5},{7,6},{8,11},{9,8},{10,9... | collective-permute-start | bytes 1572872 | tf_op jit(solution)/shard_map/ppermute | solution.py:440
  270.9 23.6 %collective-permute-start.25 = (bf16[256,1024]{1,0:T(8,128)(2,1)S(1)}, bf16[256,1024]{1,0:T(8,128)(2,1)S(1)}, u32[]{:S(2)}, u32[]{:S(2)}) collective-permute-start(bf16[256,1024]{1,0:T(8,128)(2,1)S(1)} %fusion.63), channel_id=1, source_target_pairs={{0,1},{1,2},{2,3},{3,0},{4,5},{5,6},{6,7},{7,4},{8,9},{9,10},{10,1... | collective-permute-start | bytes 1572872 | tf_op jit(solution)/shard_map/ppermute | solution.py:439
  294.5 11.1 %collective-permute-start.27 = (bf16[128,1024]{1,0:T(8,128)(2,1)S(1)}, bf16[128,1024]{1,0:T(8,128)(2,1)S(1)}, u32[]{:S(2)}, u32[]{:S(2)}) collective-permute-start(bf16[128,1024]{1,0:T(8,128)(2,1)S(1)} %slice.260), channel_id=1, source_target_pairs={{0,1},{1,2},{2,3},{3,0},{4,5},{5,6},{6,7},{7,4},{8,9},{9,10},{10,1... | collective-permute-start | bytes 786440 | tf_op jit(solution)/shard_map/ppermute | solution.py:458
  296.1 13.5 %collective-permute-start.28 = (bf16[128,1024]{1,0:T(8,128)(2,1)S(1)}, bf16[128,1024]{1,0:T(8,128)(2,1)S(1)}, u32[]{:S(2)}, u32[]{:S(2)}) collective-permute-start(bf16[128,1024]{1,0:T(8,128)(2,1)S(1)} %slice.261), channel_id=1, source_target_pairs={{0,3},{1,0},{2,1},{3,2},{4,7},{5,4},{6,5},{7,6},{8,11},{9,8},{10,9... | collective-permute-start | bytes 786440 | tf_op jit(solution)/shard_map/ppermute | solution.py:459
  299.8 64.5 %collective-permute-start.31 = (bf16[256,1024]{1,0:T(8,128)(2,1)}, bf16[256,1024]{1,0:T(8,128)(2,1)}, u32[]{:S(2)}, u32[]{:S(2)}) collective-permute-start(bf16[256,1024]{1,0:T(8,128)(2,1)} %get-tuple-element.115), channel_id=1, source_target_pairs={{0,3},{1,0},{2,1},{3,2},{4,7},{5,4},{6,5},{7,6},{8,11},{9,8},{10,9... | collective-permute-start | bytes 1572872 | tf_op jit(solution)/shard_map/ppermute | solution.py:477
  316.2 137.3 %reduce-scatter.6.cloned.1.call-start = ((), (), s32[]{:S(2)}) async-start(), calls=%async_computation.6 | async-start | bytes 3833856 | tf_op jit(solution)/shard_map/reduce_scatter | solution.py:699
  363.8 17.0 %collective-permute-start.29 = (bf16[256,1024]{1,0:T(8,128)(2,1)}, bf16[256,1024]{1,0:T(8,128)(2,1)}, u32[]{:S(2)}, u32[]{:S(2)}) collective-permute-start(bf16[256,1024]{1,0:T(8,128)(2,1)} %get-tuple-element.112), channel_id=1, source_target_pairs={{0,1},{1,2},{2,3},{3,0},{4,5},{5,6},{6,7},{7,4},{8,9},{9,10},{10,1... | collective-permute-start | bytes 1572872 | tf_op jit(solution)/shard_map/ppermute | solution.py:477
  365.8 36.5 %collective-permute-start.32 = (bf16[512,1024]{1,0:T(8,128)(2,1)S(1)}, bf16[512,1024]{1,0:T(8,128)(2,1)}, u32[]{:S(2)}, u32[]{:S(2)}) collective-permute-start(bf16[512,1024]{1,0:T(8,128)(2,1)S(1)} %pad_maximum_fusion.2), channel_id=1, source_target_pairs={{0,3},{1,0},{2,1},{3,2},{4,7},{5,4},{6,5},{7,6},{8,11},{9,8},{10,9... | collective-permute-start | bytes 3145736 | tf_op jit(solution)/shard_map/ppermute | solution.py:477
  383.8 39.6 %collective-permute-start.30 = (bf16[512,1024]{1,0:T(8,128)(2,1)}, bf16[512,1024]{1,0:T(8,128)(2,1)}, u32[]{:S(2)}, u32[]{:S(2)}) collective-permute-start(bf16[512,1024]{1,0:T(8,128)(2,1)} %pad_maximum_fusion.1), channel_id=1, source_target_pairs={{0,1},{1,2},{2,3},{3,0},{4,5},{5,6},{6,7},{7,4},{8,9},{9,10},{10,1... | collective-permute-start | bytes 3145736 | tf_op jit(solution)/shard_map/ppermute | solution.py:477
  426.6 1.3 collective-permute-start.37
  428.0 6.3 %collective-permute-start.38 = (f32[148,128]{1,0:T(8,128)S(1)}, f32[148,128]{1,0:T(8,128)S(1)}, u32[]{:S(2)}, u32[]{:S(2)}) collective-permute-start(f32[148,128]{1,0:T(8,128)S(1)} %bitcast_add_fusion), channel_id=1, source_target_pairs={{0,8},{4,12},{8,0},{12,4},{16,24},{20,28},{24,16},{28,20},{1,9},{5... | collective-permute-start | bytes 227336 | tf_op jit(solution)/shard_map/ppermute | solution.py:529
  434.2 4.5 collective-permute-start.39
  438.7 4.5 collective-permute-start.40
  443.2 5.6 %collective-permute-start.41 = (f32[148,128]{1,0:T(8,128)S(1)}, f32[148,128]{1,0:T(8,128)S(1)}, u32[]{:S(2)}, u32[]{:S(2)}) collective-permute-start(f32[148,128]{1,0:T(8,128)S(1)} %add.288), channel_id=1, source_target_pairs={{0,2},{1,3},{2,0},{3,1},{4,6},{5,7},{6,4},{7,5},{8,10},{9,11},{10,... | collective-permute-start | bytes 227336 | tf_op jit(solution)/shard_map/ppermute | solution.py:529
  452.8 6.8 %collective-permute-start.36 = (bf16[64,1024]{1,0:T(8,128)(2,1)S(1)}, bf16[64,1024]{1,0:T(8,128)(2,1)S(1)}, u32[]{:S(2)}, u32[]{:S(2)}) collective-permute-start(bf16[64,1024]{1,0:T(8,128)(2,1)S(1)} %slice.323), channel_id=1, source_target_pairs={{0,0},{1,8},{2,16},{3,24},{4,1},{5,9},{6,17},{7,25},{8,2},{9,10},{... | collective-permute-start | bytes 393224 | tf_op jit(solution)/shard_map/ppermute | solution.py:735
  454.7 16.5 %collective-permute-start.33 = (bf16[32,3200]{1,0:T(8,128)(2,1)S(1)}, bf16[32,3200]{1,0:T(8,128)(2,1)S(1)}, u32[]{:S(2)}, u32[]{:S(2)}) collective-permute-start(bf16[32,3200]{1,0:T(8,128)(2,1)S(1)} %get-tuple-element.136), channel_id=1, source_target_pairs={{0,1},{1,2},{2,3},{3,0},{4,5},{5,6},{6,7},{7,4},{8,9},{9,10},{10,1... | collective-permute-start | bytes 614408 | tf_op jit(solution)/shard_map/ppermute | solution.py:510
  459.6 22.0 %collective-permute-start.35 = (bf16[32,3200]{1,0:T(8,128)(2,1)S(1)}, bf16[32,3200]{1,0:T(8,128)(2,1)S(1)}, u32[]{:S(2)}, u32[]{:S(2)}) collective-permute-start(bf16[32,3200]{1,0:T(8,128)(2,1)S(1)} %get-tuple-element.134), channel_id=1, source_target_pairs={{0,3},{1,0},{2,1},{3,2},{4,7},{5,4},{6,5},{7,6},{8,11},{9,8},{10,9... | collective-permute-start | bytes 614408 | tf_op jit(solution)/shard_map/ppermute | solution.py:510
  464.3 17.2 %collective-permute-start.34 = (bf16[32,3200]{1,0:T(8,128)(2,1)S(1)}, bf16[32,3200]{1,0:T(8,128)(2,1)S(1)}, u32[]{:S(2)}, u32[]{:S(2)}) collective-permute-start(bf16[32,3200]{1,0:T(8,128)(2,1)S(1)} %get-tuple-element.137), channel_id=1, source_target_pairs={{0,2},{1,3},{2,0},{3,1},{4,6},{5,7},{6,4},{7,5},{8,10},{9,11},{10,... | collective-permute-start | bytes 614408 | tf_op jit(solution)/shard_map/ppermute | solution.py:510
  (42 other events, 569.1 us)
Sparse Core Ops, SparseCore 0:
  43.9 34.8 all-gather.4
  89.8 41.5 all-gather.8
  133.9 32.3 all-gather.6
  265.1 47.1 reduce-scatter.3
  316.3 45.2 reduce-scatter.7
  384.0 51.2 reduce-scatter.5

commit v5 on v3

--- a/solution.py
+++ b/solution.py
@@ -740,12 +740,13 @@
     gain_one = jnp.sum(adj_partial * unit_in, axis=0)
     reduced, _ = ring_reduce([adj_partial, block_parts], "seq")
     adj_normed, block_sum = reduced[:own], reduced[own:]
-    block_out = (middle + block_sum).astype(BF16).reshape(inputs.shape)
     shared = jnp.concatenate(
         [mixer_sums.reshape(ns, rows, -1), ffn_sums.reshape(ns, rows, -1)], axis=2
     )
     shared = exchange(shared, "seq")
+    shared, adj_normed, block_sum = lax.optimization_barrier((shared, adj_normed, block_sum))
     mixer_parts, ffn_parts = shared[:, :, :-2 * padded], shared[:, :, -2 * padded:]
+    block_out = (middle + block_sum).astype(BF16).reshape(inputs.shape)
     ffngate_out = hidden_back(ffn_parts[:, :, :padded], nd, hidden)
     ffnup_out = hidden_back(ffn_parts[:, :, padded:], nd, hidden)
     whole_rows = lambda parts: jnp.swapaxes(parts, 0, 1).reshape(rows, -1)

time: 487 us -> 507 us (1.041)
  local copies, waits for them, and re-layouts: 57.3 us -> 65.2 us
  waiting for transfers between devices: 225 us -> 231 us
    ppermute x8, waiting for transfers between devices: 36.2 us -> 44.9 us  [ring_reduce(): lax.ppermute(part.astype(BF16), axis, shift_pairs(count, by)).astype(F32)]
    unnamed x108 -> x110, local copies, waits for them, and re-layouts: 20.7 us -> 21.4 us
  transfers between devices with their start and end apart: 48 -> 48, of which waited for: 26 -> 29; matrix products, arithmetic and copies ran while one was open for 23% -> 21% of each run, Pallas kernels for 9% -> 9%
where the time goes in v5:
time: 507 us; the launch traced here: 497 us
  waiting for transfers between devices  231 us (46%)
  matrix products  65.9 us (13%)
  local copies, waits for them, and re-layouts  65.2 us (13%)
  starting transfers between devices  51 us (10%)
  Pallas kernels  45 us (9%)
  other arithmetic  23.5 us (5%)
  between operations  15.8 us (3%)
    ppermute x9, waiting for transfers between devices, exchange(): lax.ppermute(take_block(whole, (me + hop) % count), axis, shift_pairs(cou...  59.6 us
    pallas_call x2, Pallas kernels, mixer_call(): pl.pallas_call(kernel, grid_spec=pltpu.PrefetchScalarGridSpec(num_scalar_...  45 us
    ppermute x8, waiting for transfers between devices, ring_reduce(): lax.ppermute(part.astype(BF16), axis, shift_pairs(count, by)).astype(F32)  44.9 us
    ppermute x5, waiting for transfers between devices, sum_everywhere(): values = values + lax.ppermute(values, axis, swap_pairs(count, mask))  31.7 us
    dot_general x4, matrix products, dot_nt(): return jnp.einsum('tc,dc->td', left, right, preferred_element_type=F32)  25.3 us
    unnamed x110, local copies, waits for them, and re-layouts  21.4 us
    dot_general x4, matrix products, dot(): return jnp.dot(left, right, preferred_element_type=F32)  20.8 us
    dot_general x4, matrix products, dot_tn(): return jnp.einsum('tr,tc->rc', left, right, preferred_element_type=F32)  19.8 us
  transfers between devices with their start and end apart: 48, of which 29 were waited for; matrix products, arithmetic and copies ran while one was open for 21% of the time, Pallas kernels for 9%

profile of v5, /device:TPU:11, one launch (start us, length us, event | category | flops | bytes accessed | tf_op | source)
XLA Modules:
  0.0 497.4 jit_solution(2766355772314751312)
XLA Ops:
  15.9 2.9 collective-permute-start.1
  19.1 14.8 %collective-permute-done = bf16[32,1664]{1,0:T(8,128)(2,1)S(1)} collective-permute-done((bf16[32,1664]{1,0:T(8,128)(2,1)S(1)}, bf16[32,1664]{1,0:T(8,128)(2,1)S(1)}, u32[]{:S(2)}, u32[]{:S(2)}) %collective-permute-start) | collective-permute-done | bytes 106528 | tf_op jit(solution)/shard_map/ppermute | solution.py:510
  33.9 5.9 %collective-permute-done.1 = bf16[32,1664]{1,0:T(8,128)(2,1)S(1)} collective-permute-done((bf16[32,1664]{1,0:T(8,128)(2,1)S(1)}, bf16[32,1664]{1,0:T(8,128)(2,1)S(1)}, u32[]{:S(2)}, u32[]{:S(2)}) %collective-permute-start.1) | collective-permute-done | bytes 106528 | tf_op jit(solution)/shard_map/ppermute | solution.py:510
  39.8 2.8 collective-permute-done.2
  47.2 5.1 %collective-permute-done.12 = bf16[32,3584]{1,0:T(8,128)(2,1)S(1)} collective-permute-done((bf16[32,3584]{1,0:T(8,128)(2,1)S(1)}, bf16[32,3584]{1,0:T(8,128)(2,1)S(1)}, u32[]{:S(2)}, u32[]{:S(2)}) %collective-permute-start.12) | collective-permute-done | bytes 229408 | tf_op jit(solution)/shard_map/ppermute | solution.py:510
  52.3 12.8 %collective-permute-done.13 = bf16[32,3584]{1,0:T(8,128)(2,1)S(1)} collective-permute-done((bf16[32,3584]{1,0:T(8,128)(2,1)S(1)}, bf16[32,3584]{1,0:T(8,128)(2,1)S(1)}, u32[]{:S(2)}, u32[]{:S(2)}) %collective-permute-start.13) | collective-permute-done | bytes 229408 | tf_op jit(solution)/shard_map/ppermute | solution.py:510
  65.1 2.4 collective-permute-done.14
  75.7 4.2 collective-permute-done.5
  80.5 4.9 collective-permute-done.6
  87.0 2.3 fusion.4
  89.5 7.5 %convolution_convert_fusion.1.current_ref.before_ref = bf16[1024,1664]{1,0:T(8,128)(2,1)} fusion(bf16[1024,1664]{1,0:T(8,128)(2,1)} %all-gather.5.cloned.1.call-done, bf16[1024,1024]{1,0:T(8,128)(2,1)S(1)} %copy-done.15, f32[1024]{0:T(1024)S(1)} %copy-done.31, f32[1024]{0:T(1024)S(1)} %add_rsqrt_fusion), kind=kOutput, calls=%fused_computation.16 | convolution fusion | flops 3495559168 | bytes 8921088 | tf_op jit(solution)/shard_map/dot_general | solution.py:549
  98.4 18.1 %mixer_forward.1 = (bf16[1024,512]{1,0:T(8,128)(2,1)S(1)}, bf16[1,4,2,256,256]{4,3,2,1,0:T(8,128)(2,1)S(1)}, bf16[1024,512]{1,0:T(8,128)(2,1)S(1)}, f32[1,4,2,128,256]{4,3,2,1,0:T(8,128)S(1)}, f32[1024,512]{1,0:T(8,128)}) custom-call(s32[4]{0:T(128)S(1)} %pad_add_fusion.order_ref, bf16[1024,1664]{1,0:T(8,128)(2,1)} %convolution_convert_fusion.1.current_ref.before_ref, ...), custom_call_target="tpu_custom_call" | custom-call | flops 16106127360 | bytes 25165824 | tf_op jit(solution)/shard_map/mixer_forward/pallas_call | solution.py:365
  117.5 5.0 %collective-permute-done.8 = bf16[256,1024]{1,0:T(8,128)(2,1)} collective-permute-done((bf16[256,1024]{1,0:T(8,128)(2,1)}, bf16[256,1024]{1,0:T(8,128)(2,1)}, u32[]{:S(2)}, u32[]{:S(2)}) %collective-permute-start.8) | collective-permute-done | bytes 524320 | tf_op jit(solution)/shard_map/ppermute | solution.py:440
  126.5 2.6 slice.298
  131.1 10.0 %collective-permute-done.10 = bf16[256,512]{1,0:T(8,128)(2,1)} collective-permute-done((bf16[256,512]{1,0:T(8,128)(2,1)}, bf16[256,512]{1,0:T(8,128)(2,1)}, u32[]{:S(2)}, u32[]{:S(2)}) %collective-permute-start.10) | collective-permute-done | bytes 262176 | tf_op jit(solution)/shard_map/ppermute | solution.py:501
  141.1 6.4 %collective-permute-done.11 = bf16[256,512]{1,0:T(8,128)(2,1)} collective-permute-done((bf16[256,512]{1,0:T(8,128)(2,1)}, bf16[256,512]{1,0:T(8,128)(2,1)}, u32[]{:S(2)}, u32[]{:S(2)}) %collective-permute-start.11) | collective-permute-done | bytes 262176 | tf_op jit(solution)/shard_map/ppermute | solution.py:501
  147.6 2.5 multiply_reduce_fusion.2
  161.9 6.8 %collective-permute-done.15 = bf16[128,1024]{1,0:T(8,128)(2,1)S(1)} collective-permute-done((bf16[128,1024]{1,0:T(8,128)(2,1)S(1)}, bf16[128,1024]{1,0:T(8,128)(2,1)S(1)}, u32[]{:S(2)}, u32[]{:S(2)}) %collective-permute-start.15) | collective-permute-done | bytes 262176 | tf_op jit(solution)/shard_map/ppermute | solution.py:458
  173.8 13.2 %collective-permute-done.17 = bf16[256,1024]{1,0:T(8,128)(2,1)S(1)} collective-permute-done((bf16[256,1024]{1,0:T(8,128)(2,1)S(1)}, bf16[256,1024]{1,0:T(8,128)(2,1)S(1)}, u32[]{:S(2)}, u32[]{:S(2)}) %collective-permute-start.17) | collective-permute-done | bytes 524320 | tf_op jit(solution)/shard_map/ppermute | solution.py:440
  190.1 2.6 slice.299
  195.8 6.3 %fusion.79 = f32[1024,1536]{0,1:T(8,128)S(1)} fusion(bf16[1024,1024]{1,0:T(8,128)(2,1)} %constant_dynamic-update-slice_fusion.11, bf16[1024,1536]{1,0:T(8,128)(2,1)} %all-gather.7.cloned.1.call-done), kind=kOutput, calls=%fused_computation.210 | convolution fusion | flops 3221225472 | bytes 11534336 | tf_op jit(solution)/shard_map/dot_general | solution.py:549
  202.1 5.6 %multiply_convert_fusion.2 = (bf16[1024,768]{0,1:T(8,128)(2,1)S(1)}, bf16[1024,768]{0,1:T(8,128)(2,1)S(1)}, bf16[1024,768]{0,1:T(8,128)(2,1)}) fusion(f32[1024,1536]{0,1:T(8,128)S(1)} %fusion.79, bf16[1024,1024]{1,0:T(8,128)(2,1)} %constant_dynamic-update-slice_fusion.6, bf16[704,1024]{1,0:T(8,128)(2,1)S(1)} %bitcast.182), kind=kOutput, calls=%fused_computation.21 | convolution fusion | flops 1622409216 | bytes 14548992 | tf_op jit(solution)/shard_map/tc,dc->td/dot_general | solution.py:553
  209.5 6.6 %convolution_convert_fusion.2 = bf16[1024,1536]{1,0:T(8,128)(2,1)} fusion(bf16[1024,1024]{1,0:T(8,128)(2,1)} %constant_dynamic-update-slice_fusion.11, bf16[1024,1536]{0,1:T(8,128)(2,1)S(1)} %pad_maximum_fusion), kind=kOutput, calls=%fused_computation.17 | convolution fusion | flops 3222798336 | bytes 8388608 | tf_op jit(solution)/shard_map/tr,tc->rc/dot_general | solution.py:557
  216.3 6.1 %fusion.77 = (bf16[1024,1024]{1,0:T(8,128)(2,1)S(1)}, f32[1024,1024]{1,0:T(8,128)S(1)}) fusion(bf16[1024,1536]{1,0:T(8,128)(2,1)} %all-gather.7.cloned.1.call-done, bf16[1024,768]{0,1:T(8,128)(2,1)} %copy-done.19, bf16[1024,768]{0,1:T(8,128)(2,1)} %copy-done.18), kind=kOutput, calls=%fused_computation.208 | convolution fusion | flops 3228565504 | bytes 12582912 | tf_op jit(solution)/shard_map/tc,dc->td/dot_general | solution.py:553
  224.6 3.7 collective-permute-done.21
  228.3 10.2 %collective-permute-done.23 = bf16[128,1024]{1,0:T(8,128)(2,1)S(1)} collective-permute-done((bf16[128,1024]{1,0:T(8,128)(2,1)S(1)}, bf16[128,1024]{1,0:T(8,128)(2,1)S(1)}, u32[]{:S(2)}, u32[]{:S(2)}) %collective-permute-start.23) | collective-permute-done | bytes 262176 | tf_op jit(solution)/shard_map/ppermute | solution.py:477
  240.5 9.3 %collective-permute-done.22 = bf16[256,1024]{1,0:T(8,128)(2,1)S(1)} collective-permute-done((bf16[256,1024]{1,0:T(8,128)(2,1)S(1)}, bf16[256,1024]{1,0:T(8,128)(2,1)S(1)}, u32[]{:S(2)}, u32[]{:S(2)}) %collective-permute-start.22) | collective-permute-done | bytes 524320 | tf_op jit(solution)/shard_map/ppermute | solution.py:477
  249.8 12.4 %collective-permute-done.24 = bf16[256,1024]{1,0:T(8,128)(2,1)S(1)} collective-permute-done((bf16[256,1024]{1,0:T(8,128)(2,1)S(1)}, bf16[256,1024]{1,0:T(8,128)(2,1)S(1)}, u32[]{:S(2)}, u32[]{:S(2)}) %collective-permute-start.24) | collective-permute-done | bytes 524320 | tf_op jit(solution)/shard_map/ppermute | solution.py:477
  266.6 3.4 fusion.80
  270.0 18.6 %collective-permute-done.26 = bf16[256,1024]{1,0:T(8,128)(2,1)S(1)} collective-permute-done((bf16[256,1024]{1,0:T(8,128)(2,1)S(1)}, bf16[256,1024]{1,0:T(8,128)(2,1)S(1)}, u32[]{:S(2)}, u32[]{:S(2)}) %collective-permute-start.26) | collective-permute-done | bytes 524320 | tf_op jit(solution)/shard_map/ppermute | solution.py:439
  291.0 4.5 fusion.78
  297.7 3.2 collective-permute-done.28
  303.0 2.5 maximum_maximum_fusion
  305.8 3.1 convolution_convert_fusion.4.adjoint_ref
  311.4 27.0 %mixer_backward.1 = (bf16[1024,1664]{1,0:T(8,128)(2,1)}, f32[4,1024]{1,0:T(4,128)S(1)}, f32[8,128]{1,0:T(8,128)S(1)}, f32[1,256]{1,0:T(1,128)S(1)}) custom-call(s32[4]{0:T(128)S(1)} %pad_add_fusion.order_ref, bf16[1024,1664]{1,0:T(8,128)(2,1)} %convolution_convert_fusion.1.current_ref.before_ref, ...), custom_call_target="tpu_custom_call" | custom-call | flops 16106127360 | bytes 25165824 | tf_op jit(solution)/shard_map/mixer_backward/pallas_call | solution.py:365
  338.6 8.6 %convolution_convert_fusion = bf16[1024,1664]{1,0:T(8,128)(2,1)} fusion(bf16[1024,1664]{1,0:T(8,128)(2,1)} %get-tuple-element.65, bf16[1024,1024]{1,0:T(8,128)(2,1)} %constant_dynamic-update-slice_fusion.1, f32[1024]{0:T(1024)S(1)} %copy-done.31, f32[1024]{0:T(1024)S(1)} %add_rsqrt_fusion), kind=kOutput, calls=%fused_computation.15 | convolution fusion | flops 3495559168 | bytes 8921088 | tf_op jit(solution)/shard_map/tr,tc->rc/dot_general | solution.py:557
  347.2 10.4 %fusion.3 = (f32[1024]{0:T(1024)S(1)}, bf16[1024,1024]{1,0:T(8,128)(2,1)}, f32[1024,1024]{1,0:T(8,128)}) fusion(bf16[1024,1024]{1,0:T(8,128)(2,1)} %constant_dynamic-update-slice_fusion.1, f32[1024]{0:T(1024)S(1)} %add_rsqrt_fusion, bf16[1024,1664]{1,0:T(8,128)(2,1)} %get-tuple-element.65, bf16[1024,1664]{1,0:T(8,128)(2,1)} %all-gather.5.cloned.1.call-done), kind=kOutput, calls=%fused_computation.5 | convolution fusion | flops 3494902784 | bytes 15212544 | tf_op jit(solution)/shard_map/tc,dc->td/dot_general | solution.py:553
  367.1 9.3 %collective-permute-done.34 = bf16[256,1024]{1,0:T(8,128)(2,1)S(1)} collective-permute-done((bf16[256,1024]{1,0:T(8,128)(2,1)S(1)}, bf16[256,1024]{1,0:T(8,128)(2,1)S(1)}, u32[]{:S(2)}, u32[]{:S(2)}) %collective-permute-start.34) | collective-permute-done | bytes 524320 | tf_op jit(solution)/shard_map/ppermute | solution.py:477
  379.3 10.9 %collective-permute-done.40 = f32[148,128]{1,0:T(8,128)S(1)} collective-permute-done((f32[148,128]{1,0:T(8,128)S(1)}, f32[148,128]{1,0:T(8,128)S(1)}, u32[]{:S(2)}, u32[]{:S(2)}) %collective-permute-start.40) | collective-permute-done | bytes 75808 | tf_op jit(solution)/shard_map/ppermute | solution.py:529
  390.1 2.8 collective-permute-start.41
  394.5 20.7 %collective-permute-done.41 = f32[148,128]{1,0:T(8,128)S(1)} collective-permute-done((f32[148,128]{1,0:T(8,128)S(1)}, f32[148,128]{1,0:T(8,128)S(1)}, u32[]{:S(2)}, u32[]{:S(2)}) %collective-permute-start.41) | collective-permute-done | bytes 75808 | tf_op jit(solution)/shard_map/ppermute | solution.py:529
  418.2 5.5 %collective-permute-start.36 = (bf16[64,1024]{1,0:T(8,128)(2,1)S(1)}, bf16[64,1024]{1,0:T(8,128)(2,1)}, u32[]{:S(2)}, u32[]{:S(2)}) collective-permute-start(bf16[64,1024]{1,0:T(8,128)(2,1)S(1)} %slice.325), channel_id=1, source_target_pairs={{0,0},{1,8},{2,16},{3,24},{4,1},{5,9},{6,17},{7,25},{8,2},{9,10},{... | collective-permute-start | bytes 393224 | tf_op jit(solution)/shard_map/ppermute | solution.py:732
  424.9 18.4 %collective-permute-done.36 = bf16[64,1024]{1,0:T(8,128)(2,1)} collective-permute-done((bf16[64,1024]{1,0:T(8,128)(2,1)S(1)}, bf16[64,1024]{1,0:T(8,128)(2,1)}, u32[]{:S(2)}, u32[]{:S(2)}) %collective-permute-start.36) | collective-permute-done | bytes 131104 | tf_op jit(solution)/shard_map/ppermute | solution.py:732
  443.3 3.3 fusion.14
  448.1 2.8 collective-permute-start.29
  454.6 9.4 %collective-permute-done.29 = bf16[32,3200]{1,0:T(8,128)(2,1)S(1)} collective-permute-done((bf16[32,3200]{1,0:T(8,128)(2,1)S(1)}, bf16[32,3200]{1,0:T(8,128)(2,1)S(1)}, u32[]{:S(2)}, u32[]{:S(2)}) %collective-permute-start.29) | collective-permute-done | bytes 204832 | tf_op jit(solution)/shard_map/ppermute | solution.py:510
  464.0 4.5 collective-permute-done.30
  485.5 3.0 fusion.49
  (314 shorter events, 116.7 us)
Async XLA Ops:
  7.2 82.1 %all-gather.5.cloned.1.call-start = ((), (), s32[]{:S(2)}) async-start(), calls=%async_computation.3 | async-start | bytes 3833856 | tf_op jit(solution)/shard_map/all_gather | solution.py:632
  7.3 35.4 %collective-permute-start.3 = (bf16[256,1024]{1,0:T(8,128)(2,1)}, bf16[256,1024]{1,0:T(8,128)(2,1)S(1)}, u32[]{:S(2)}, u32[]{:S(2)}) collective-permute-start(bf16[256,1024]{1,0:T(8,128)(2,1)} %bitcast.174), channel_id=1, source_target_pairs={{0,1},{1,2},{2,3},{3,0},{4,5},{5,6},{6,7},{7,4},{8,9},{9,10},{10,1... | collective-permute-start | bytes 1572872 | tf_op jit(solution)/shard_map/ppermute | solution.py:439
  8.6 34.0 %collective-permute-start.4 = (bf16[256,1024]{1,0:T(8,128)(2,1)}, bf16[256,1024]{1,0:T(8,128)(2,1)S(1)}, u32[]{:S(2)}, u32[]{:S(2)}) collective-permute-start(bf16[256,1024]{1,0:T(8,128)(2,1)} %bitcast.175), channel_id=1, source_target_pairs={{0,3},{1,0},{2,1},{3,2},{4,7},{5,4},{6,5},{7,6},{8,11},{9,8},{10,9... | collective-permute-start | bytes 1572872 | tf_op jit(solution)/shard_map/ppermute | solution.py:440
  14.5 19.4 %collective-permute-start = (bf16[32,1664]{1,0:T(8,128)(2,1)S(1)}, bf16[32,1664]{1,0:T(8,128)(2,1)S(1)}, u32[]{:S(2)}, u32[]{:S(2)}) collective-permute-start(bf16[32,1664]{1,0:T(8,128)(2,1)S(1)} %bitcast.199), channel_id=1, source_target_pairs={{0,1},{1,2},{2,3},{3,0},{4,5},{5,6},{6,7},{7,4},{8,9},{9,10},{10,1... | collective-permute-start | bytes 319496 | tf_op jit(solution)/shard_map/ppermute | solution.py:510
  15.9 23.9 %collective-permute-start.1 = (bf16[32,1664]{1,0:T(8,128)(2,1)S(1)}, bf16[32,1664]{1,0:T(8,128)(2,1)S(1)}, u32[]{:S(2)}, u32[]{:S(2)}) collective-permute-start(bf16[32,1664]{1,0:T(8,128)(2,1)S(1)} %bitcast.198), channel_id=1, source_target_pairs={{0,2},{1,3},{2,0},{3,1},{4,6},{5,7},{6,4},{7,5},{8,10},{9,11},{10,... | collective-permute-start | bytes 319496 | tf_op jit(solution)/shard_map/ppermute | solution.py:510
  18.8 23.7 %collective-permute-start.2 = (bf16[32,1664]{1,0:T(8,128)(2,1)S(1)}, bf16[32,1664]{1,0:T(8,128)(2,1)S(1)}, u32[]{:S(2)}, u32[]{:S(2)}) collective-permute-start(bf16[32,1664]{1,0:T(8,128)(2,1)S(1)} %bitcast.197), channel_id=1, source_target_pairs={{0,3},{1,0},{2,1},{3,2},{4,7},{5,4},{6,5},{7,6},{8,11},{9,8},{10,9... | collective-permute-start | bytes 319496 | tf_op jit(solution)/shard_map/ppermute | solution.py:510
  43.4 83.1 %all-gather.9.cloned.1.call-start = ((), (), s32[]{:S(2)}) async-start(), calls=%async_computation.8 | async-start | bytes 6488064 | tf_op jit(solution)/shard_map/all_gather | solution.py:640
  45.5 6.7 %collective-permute-start.12 = (bf16[32,3584]{1,0:T(8,128)(2,1)S(1)}, bf16[32,3584]{1,0:T(8,128)(2,1)S(1)}, u32[]{:S(2)}, u32[]{:S(2)}) collective-permute-start(bf16[32,3584]{1,0:T(8,128)(2,1)S(1)} %get-tuple-element.112), channel_id=1, source_target_pairs={{0,1},{1,2},{2,3},{3,0},{4,5},{5,6},{6,7},{7,4},{8,9},{9,10},{10,1... | collective-permute-start | bytes 688136 | tf_op jit(solution)/shard_map/ppermute | solution.py:510
  45.7 19.4 %collective-permute-start.13 = (bf16[32,3584]{1,0:T(8,128)(2,1)S(1)}, bf16[32,3584]{1,0:T(8,128)(2,1)S(1)}, u32[]{:S(2)}, u32[]{:S(2)}) collective-permute-start(bf16[32,3584]{1,0:T(8,128)(2,1)S(1)} %get-tuple-element.111), channel_id=1, source_target_pairs={{0,2},{1,3},{2,0},{3,1},{4,6},{5,7},{6,4},{7,5},{8,10},{9,11},{10,... | collective-permute-start | bytes 688136 | tf_op jit(solution)/shard_map/ppermute | solution.py:510
  46.7 20.9 %collective-permute-start.14 = (bf16[32,3584]{1,0:T(8,128)(2,1)S(1)}, bf16[32,3584]{1,0:T(8,128)(2,1)S(1)}, u32[]{:S(2)}, u32[]{:S(2)}) collective-permute-start(bf16[32,3584]{1,0:T(8,128)(2,1)S(1)} %get-tuple-element.110), channel_id=1, source_target_pairs={{0,3},{1,0},{2,1},{3,2},{4,7},{5,4},{6,5},{7,6},{8,11},{9,8},{10,9... | collective-permute-start | bytes 688136 | tf_op jit(solution)/shard_map/ppermute | solution.py:510
  69.9 125.9 %all-gather.7.cloned.1.call-start = ((), (), s32[]{:S(2)}) async-start(), calls=%async_computation.4 | async-start | bytes 3538944 | tf_op jit(solution)/shard_map/all_gather | solution.py:646
  72.3 7.6 %collective-permute-start.5 = (bf16[128,1024]{1,0:T(8,128)(2,1)S(1)}, bf16[128,1024]{1,0:T(8,128)(2,1)S(1)}, u32[]{:S(2)}, u32[]{:S(2)}) collective-permute-start(bf16[128,1024]{1,0:T(8,128)(2,1)S(1)} %slice.236), channel_id=1, source_target_pairs={{0,1},{1,2},{2,3},{3,0},{4,5},{5,6},{6,7},{7,4},{8,9},{9,10},{10,1... | collective-permute-start | bytes 786440 | tf_op jit(solution)/shard_map/ppermute | solution.py:458
  72.4 13.0 %collective-permute-start.6 = (bf16[128,1024]{1,0:T(8,128)(2,1)S(1)}, bf16[128,1024]{1,0:T(8,128)(2,1)S(1)}, u32[]{:S(2)}, u32[]{:S(2)}) collective-permute-start(bf16[128,1024]{1,0:T(8,128)(2,1)S(1)} %slice.237), channel_id=1, source_target_pairs={{0,3},{1,0},{2,1},{3,2},{4,7},{5,4},{6,5},{7,6},{8,11},{9,8},{10,9... | collective-permute-start | bytes 786440 | tf_op jit(solution)/shard_map/ppermute | solution.py:459
  75.6 233.4 %reduce-scatter.4.cloned.1.call-start = ((), (), s32[]{:S(2)}) async-start(), calls=%async_computation.5 | async-start | bytes 3538944 | tf_op jit(solution)/shard_map/reduce_scatter | solution.py:698
  97.0 20.5 %collective-permute-start.7 = (bf16[256,1024]{1,0:T(8,128)(2,1)}, bf16[256,1024]{1,0:T(8,128)(2,1)}, u32[]{:S(2)}, u32[]{:S(2)}) collective-permute-start(bf16[256,1024]{1,0:T(8,128)(2,1)} %bitcast.18), channel_id=1, source_target_pairs={{0,1},{1,2},{2,3},{3,0},{4,5},{5,6},{6,7},{7,4},{8,9},{9,10},{10,1... | collective-permute-start | bytes 1572872 | tf_op jit(solution)/shard_map/ppermute | solution.py:439
  97.0 25.5 %collective-permute-start.8 = (bf16[256,1024]{1,0:T(8,128)(2,1)}, bf16[256,1024]{1,0:T(8,128)(2,1)}, u32[]{:S(2)}, u32[]{:S(2)}) collective-permute-start(bf16[256,1024]{1,0:T(8,128)(2,1)} %bitcast.18), channel_id=1, source_target_pairs={{0,3},{1,0},{2,1},{3,2},{4,7},{5,4},{6,5},{7,6},{8,11},{9,8},{10,9... | collective-permute-start | bytes 1572872 | tf_op jit(solution)/shard_map/ppermute | solution.py:440
  123.4 17.7 %collective-permute-start.10 = (bf16[256,512]{1,0:T(8,128)(2,1)}, bf16[256,512]{1,0:T(8,128)(2,1)}, u32[]{:S(2)}, u32[]{:S(2)}) collective-permute-start(bf16[256,512]{1,0:T(8,128)(2,1)} %get-tuple-element.108), channel_id=1, source_target_pairs={{0,2},{1,3},{2,0},{3,1},{4,6},{5,7},{6,4},{7,5},{8,10},{9,11},{10,... | collective-permute-start | bytes 786440 | tf_op jit(solution)/shard_map/ppermute | solution.py:501
  124.5 23.1 %collective-permute-start.11 = (bf16[256,512]{1,0:T(8,128)(2,1)}, bf16[256,512]{1,0:T(8,128)(2,1)}, u32[]{:S(2)}, u32[]{:S(2)}) collective-permute-start(bf16[256,512]{1,0:T(8,128)(2,1)} %get-tuple-element.107), channel_id=1, source_target_pairs={{0,3},{1,0},{2,1},{3,2},{4,7},{5,4},{6,5},{7,6},{8,11},{9,8},{10,9... | collective-permute-start | bytes 786440 | tf_op jit(solution)/shard_map/ppermute | solution.py:501
  125.6 21.9 %collective-permute-start.9 = (bf16[256,512]{1,0:T(8,128)(2,1)}, bf16[256,512]{1,0:T(8,128)(2,1)}, u32[]{:S(2)}, u32[]{:S(2)}) collective-permute-start(bf16[256,512]{1,0:T(8,128)(2,1)} %get-tuple-element.109), channel_id=1, source_target_pairs={{0,1},{1,2},{2,3},{3,0},{4,5},{5,6},{6,7},{7,4},{8,9},{9,10},{10,1... | collective-permute-start | bytes 786440 | tf_op jit(solution)/shard_map/ppermute | solution.py:501
  151.3 18.2 %collective-permute-start.18 = (bf16[256,1024]{1,0:T(8,128)(2,1)S(1)}, bf16[256,1024]{1,0:T(8,128)(2,1)S(1)}, u32[]{:S(2)}, u32[]{:S(2)}) collective-permute-start(bf16[256,1024]{1,0:T(8,128)(2,1)S(1)} %get-tuple-element.78), channel_id=1, source_target_pairs={{0,1},{1,2},{2,3},{3,0},{4,5},{5,6},{6,7},{7,4},{8,9},{9,10},{10,1... | collective-permute-start | bytes 1572872 | tf_op jit(solution)/shard_map/ppermute | solution.py:439
  153.6 15.1 %collective-permute-start.15 = (bf16[128,1024]{1,0:T(8,128)(2,1)S(1)}, bf16[128,1024]{1,0:T(8,128)(2,1)S(1)}, u32[]{:S(2)}, u32[]{:S(2)}) collective-permute-start(bf16[128,1024]{1,0:T(8,128)(2,1)S(1)} %slice.244), channel_id=1, source_target_pairs={{0,1},{1,2},{2,3},{3,0},{4,5},{5,6},{6,7},{7,4},{8,9},{9,10},{10,1... | collective-permute-start | bytes 786440 | tf_op jit(solution)/shard_map/ppermute | solution.py:458
  154.7 18.4 %collective-permute-start.16 = (bf16[128,1024]{1,0:T(8,128)(2,1)S(1)}, bf16[128,1024]{1,0:T(8,128)(2,1)S(1)}, u32[]{:S(2)}, u32[]{:S(2)}) collective-permute-start(bf16[128,1024]{1,0:T(8,128)(2,1)S(1)} %slice.245), channel_id=1, source_target_pairs={{0,3},{1,0},{2,1},{3,2},{4,7},{5,4},{6,5},{7,6},{8,11},{9,8},{10,9... | collective-permute-start | bytes 786440 | tf_op jit(solution)/shard_map/ppermute | solution.py:459
  156.2 30.8 %collective-permute-start.17 = (bf16[256,1024]{1,0:T(8,128)(2,1)S(1)}, bf16[256,1024]{1,0:T(8,128)(2,1)S(1)}, u32[]{:S(2)}, u32[]{:S(2)}) collective-permute-start(bf16[256,1024]{1,0:T(8,128)(2,1)S(1)} %get-tuple-element.78), channel_id=1, source_target_pairs={{0,3},{1,0},{2,1},{3,2},{4,7},{5,4},{6,5},{7,6},{8,11},{9,8},{10,9... | collective-permute-start | bytes 1572872 | tf_op jit(solution)/shard_map/ppermute | solution.py:440
  169.5 24.0 %collective-permute-start.19 = (bf16[128,1024]{1,0:T(8,128)(2,1)S(1)}, bf16[128,1024]{1,0:T(8,128)(2,1)S(1)}, u32[]{:S(2)}, u32[]{:S(2)}) collective-permute-start(bf16[128,1024]{1,0:T(8,128)(2,1)S(1)} %slice.300), channel_id=1, source_target_pairs={{0,1},{1,2},{2,3},{3,0},{4,5},{5,6},{6,7},{7,4},{8,9},{9,10},{10,1... | collective-permute-start | bytes 786440 | tf_op jit(solution)/shard_map/ppermute | solution.py:458
  187.0 7.2 %collective-permute-start.20 = (bf16[128,1024]{1,0:T(8,128)(2,1)S(1)}, bf16[128,1024]{1,0:T(8,128)(2,1)S(1)}, u32[]{:S(2)}, u32[]{:S(2)}) collective-permute-start(bf16[128,1024]{1,0:T(8,128)(2,1)S(1)} %slice.301), channel_id=1, source_target_pairs={{0,3},{1,0},{2,1},{3,2},{4,7},{5,4},{6,5},{7,6},{8,11},{9,8},{10,9... | collective-permute-start | bytes 786440 | tf_op jit(solution)/shard_map/ppermute | solution.py:459
  216.1 141.5 %reduce-scatter.6.cloned.1.call-start = ((), (), s32[]{:S(2)}) async-start(), calls=%async_computation.6 | async-start | bytes 2949120 | tf_op jit(solution)/shard_map/reduce_scatter | solution.py:698
  222.5 5.7 %collective-permute-start.21 = (bf16[128,1024]{1,0:T(8,128)(2,1)S(1)}, bf16[128,1024]{1,0:T(8,128)(2,1)S(1)}, u32[]{:S(2)}, u32[]{:S(2)}) collective-permute-start(bf16[128,1024]{1,0:T(8,128)(2,1)S(1)} %get-tuple-element.100), channel_id=1, source_target_pairs={{0,1},{1,2},{2,3},{3,0},{4,5},{5,6},{6,7},{7,4},{8,9},{9,10},{10,1... | collective-permute-start | bytes 786440 | tf_op jit(solution)/shard_map/ppermute | solution.py:477
  222.9 15.6 %collective-permute-start.23 = (bf16[128,1024]{1,0:T(8,128)(2,1)S(1)}, bf16[128,1024]{1,0:T(8,128)(2,1)S(1)}, u32[]{:S(2)}, u32[]{:S(2)}) collective-permute-start(bf16[128,1024]{1,0:T(8,128)(2,1)S(1)} %get-tuple-element.101), channel_id=1, source_target_pairs={{0,3},{1,0},{2,1},{3,2},{4,7},{5,4},{6,5},{7,6},{8,11},{9,8},{10,9... | collective-permute-start | bytes 786440 | tf_op jit(solution)/shard_map/ppermute | solution.py:477
  238.7 11.1 %collective-permute-start.22 = (bf16[256,1024]{1,0:T(8,128)(2,1)S(1)}, bf16[256,1024]{1,0:T(8,128)(2,1)S(1)}, u32[]{:S(2)}, u32[]{:S(2)}) collective-permute-start(bf16[256,1024]{1,0:T(8,128)(2,1)S(1)} %pad_maximum_fusion.3), channel_id=1, source_target_pairs={{0,1},{1,2},{2,3},{3,0},{4,5},{5,6},{6,7},{7,4},{8,9},{9,10},{10,1... | collective-permute-start | bytes 1572872 | tf_op jit(solution)/shard_map/ppermute | solution.py:477
  238.8 23.4 %collective-permute-start.24 = (bf16[256,1024]{1,0:T(8,128)(2,1)S(1)}, bf16[256,1024]{1,0:T(8,128)(2,1)S(1)}, u32[]{:S(2)}, u32[]{:S(2)}) collective-permute-start(bf16[256,1024]{1,0:T(8,128)(2,1)S(1)} %pad_maximum_fusion.4), channel_id=1, source_target_pairs={{0,3},{1,0},{2,1},{3,2},{4,7},{5,4},{6,5},{7,6},{8,11},{9,8},{10,9... | collective-permute-start | bytes 1572872 | tf_op jit(solution)/shard_map/ppermute | solution.py:477
  264.4 26.4 %collective-permute-start.25 = (bf16[256,1024]{1,0:T(8,128)(2,1)S(1)}, bf16[256,1024]{1,0:T(8,128)(2,1)S(1)}, u32[]{:S(2)}, u32[]{:S(2)}) collective-permute-start(bf16[256,1024]{1,0:T(8,128)(2,1)S(1)} %get-tuple-element.76), channel_id=1, source_target_pairs={{0,3},{1,0},{2,1},{3,2},{4,7},{5,4},{6,5},{7,6},{8,11},{9,8},{10,9... | collective-permute-start | bytes 1572872 | tf_op jit(solution)/shard_map/ppermute | solution.py:440
  265.8 22.8 %collective-permute-start.26 = (bf16[256,1024]{1,0:T(8,128)(2,1)S(1)}, bf16[256,1024]{1,0:T(8,128)(2,1)S(1)}, u32[]{:S(2)}, u32[]{:S(2)}) collective-permute-start(bf16[256,1024]{1,0:T(8,128)(2,1)S(1)} %get-tuple-element.76), channel_id=1, source_target_pairs={{0,1},{1,2},{2,3},{3,0},{4,5},{5,6},{6,7},{7,4},{8,9},{9,10},{10,1... | collective-permute-start | bytes 1572872 | tf_op jit(solution)/shard_map/ppermute | solution.py:439
  288.6 9.0 %collective-permute-start.27 = (bf16[128,1024]{1,0:T(8,128)(2,1)S(1)}, bf16[128,1024]{1,0:T(8,128)(2,1)S(1)}, u32[]{:S(2)}, u32[]{:S(2)}) collective-permute-start(bf16[128,1024]{1,0:T(8,128)(2,1)S(1)} %slice.312), channel_id=1, source_target_pairs={{0,1},{1,2},{2,3},{3,0},{4,5},{5,6},{6,7},{7,4},{8,9},{9,10},{10,1... | collective-permute-start | bytes 786440 | tf_op jit(solution)/shard_map/ppermute | solution.py:458
  290.9 9.9 %collective-permute-start.28 = (bf16[128,1024]{1,0:T(8,128)(2,1)S(1)}, bf16[128,1024]{1,0:T(8,128)(2,1)S(1)}, u32[]{:S(2)}, u32[]{:S(2)}) collective-permute-start(bf16[128,1024]{1,0:T(8,128)(2,1)S(1)} %slice.313), channel_id=1, source_target_pairs={{0,3},{1,0},{2,1},{3,2},{4,7},{5,4},{6,5},{7,6},{8,11},{9,8},{10,9... | collective-permute-start | bytes 786440 | tf_op jit(solution)/shard_map/ppermute | solution.py:459
  305.5 141.1 %reduce-scatter.8.cloned.1.call-start = ((), (), s32[]{:S(2)}) async-start(), calls=%async_computation.7 | async-start | bytes 3833856 | tf_op jit(solution)/shard_map/reduce_scatter | solution.py:698
  357.9 4.0 collective-permute-start.37
  361.6 14.7 %collective-permute-start.34 = (bf16[256,1024]{1,0:T(8,128)(2,1)S(1)}, bf16[256,1024]{1,0:T(8,128)(2,1)S(1)}, u32[]{:S(2)}, u32[]{:S(2)}) collective-permute-start(bf16[256,1024]{1,0:T(8,128)(2,1)S(1)} %get-tuple-element.99), channel_id=1, source_target_pairs={{0,3},{1,0},{2,1},{3,2},{4,7},{5,4},{6,5},{7,6},{8,11},{9,8},{10,9... | collective-permute-start | bytes 1572872 | tf_op jit(solution)/shard_map/ppermute | solution.py:477
  362.0 3.7 collective-permute-start.38
  364.5 28.4 %collective-permute-start.32 = (bf16[256,1024]{1,0:T(8,128)(2,1)S(1)}, bf16[256,1024]{1,0:T(8,128)(2,1)S(1)}, u32[]{:S(2)}, u32[]{:S(2)}) collective-permute-start(bf16[256,1024]{1,0:T(8,128)(2,1)S(1)} %get-tuple-element.96), channel_id=1, source_target_pairs={{0,1},{1,2},{2,3},{3,0},{4,5},{5,6},{6,7},{7,4},{8,9},{9,10},{10,1... | collective-permute-start | bytes 1572872 | tf_op jit(solution)/shard_map/ppermute | solution.py:477
  365.7 10.9 %collective-permute-start.39 = (f32[148,128]{1,0:T(8,128)S(1)}, f32[148,128]{1,0:T(8,128)S(1)}, u32[]{:S(2)}, u32[]{:S(2)}) collective-permute-start(f32[148,128]{1,0:T(8,128)S(1)} %fusion.97), channel_id=1, source_target_pairs={{0,16},{4,20},{8,24},{12,28},{16,0},{20,4},{24,8},{28,12},{1,17},{... | collective-permute-start | bytes 227336 | tf_op jit(solution)/shard_map/ppermute | solution.py:529
  376.7 13.4 %collective-permute-start.40 = (f32[148,128]{1,0:T(8,128)S(1)}, f32[148,128]{1,0:T(8,128)S(1)}, u32[]{:S(2)}, u32[]{:S(2)}) collective-permute-start(f32[148,128]{1,0:T(8,128)S(1)} %add.287), channel_id=1, source_target_pairs={{0,1},{1,0},{2,3},{3,2},{4,5},{5,4},{6,7},{7,6},{8,9},{9,8},{10,11... | collective-permute-start | bytes 227336 | tf_op jit(solution)/shard_map/ppermute | solution.py:529
  377.8 65.5 %collective-permute-start.35 = (bf16[512,1024]{1,0:T(8,128)(2,1)}, bf16[512,1024]{1,0:T(8,128)(2,1)}, u32[]{:S(2)}, u32[]{:S(2)}) collective-permute-start(bf16[512,1024]{1,0:T(8,128)(2,1)} %pad_maximum_fusion.2), channel_id=1, source_target_pairs={{0,3},{1,0},{2,1},{3,2},{4,7},{5,4},{6,5},{7,6},{8,11},{9,8},{10,9... | collective-permute-start | bytes 3145736 | tf_op jit(solution)/shard_map/ppermute | solution.py:477
  390.1 25.0 %collective-permute-start.41 = (f32[148,128]{1,0:T(8,128)S(1)}, f32[148,128]{1,0:T(8,128)S(1)}, u32[]{:S(2)}, u32[]{:S(2)}) collective-permute-start(f32[148,128]{1,0:T(8,128)S(1)} %add.288), channel_id=1, source_target_pairs={{0,2},{1,3},{2,0},{3,1},{4,6},{5,7},{6,4},{7,5},{8,10},{9,11},{10,... | collective-permute-start | bytes 227336 | tf_op jit(solution)/shard_map/ppermute | solution.py:529
  394.2 49.1 %collective-permute-start.33 = (bf16[512,1024]{1,0:T(8,128)(2,1)}, bf16[512,1024]{1,0:T(8,128)(2,1)}, u32[]{:S(2)}, u32[]{:S(2)}) collective-permute-start(bf16[512,1024]{1,0:T(8,128)(2,1)} %pad_maximum_fusion.1), channel_id=1, source_target_pairs={{0,1},{1,2},{2,3},{3,0},{4,5},{5,6},{6,7},{7,4},{8,9},{9,10},{10,1... | collective-permute-start | bytes 3145736 | tf_op jit(solution)/shard_map/ppermute | solution.py:477
  418.2 25.1 %collective-permute-start.36 = (bf16[64,1024]{1,0:T(8,128)(2,1)S(1)}, bf16[64,1024]{1,0:T(8,128)(2,1)}, u32[]{:S(2)}, u32[]{:S(2)}) collective-permute-start(bf16[64,1024]{1,0:T(8,128)(2,1)S(1)} %slice.325), channel_id=1, source_target_pairs={{0,0},{1,8},{2,16},{3,24},{4,1},{5,9},{6,17},{7,25},{8,2},{9,10},{... | collective-permute-start | bytes 393224 | tf_op jit(solution)/shard_map/ppermute | solution.py:732
  448.1 15.8 %collective-permute-start.29 = (bf16[32,3200]{1,0:T(8,128)(2,1)S(1)}, bf16[32,3200]{1,0:T(8,128)(2,1)S(1)}, u32[]{:S(2)}, u32[]{:S(2)}) collective-permute-start(bf16[32,3200]{1,0:T(8,128)(2,1)S(1)} %get-tuple-element.122), channel_id=1, source_target_pairs={{0,1},{1,2},{2,3},{3,0},{4,5},{5,6},{6,7},{7,4},{8,9},{9,10},{10,1... | collective-permute-start | bytes 614408 | tf_op jit(solution)/shard_map/ppermute | solution.py:510
  452.1 16.4 %collective-permute-start.30 = (bf16[32,3200]{1,0:T(8,128)(2,1)S(1)}, bf16[32,3200]{1,0:T(8,128)(2,1)S(1)}, u32[]{:S(2)}, u32[]{:S(2)}) collective-permute-start(bf16[32,3200]{1,0:T(8,128)(2,1)S(1)} %get-tuple-element.123), channel_id=1, source_target_pairs={{0,2},{1,3},{2,0},{3,1},{4,6},{5,7},{6,4},{7,5},{8,10},{9,11},{10,... | collective-permute-start | bytes 614408 | tf_op jit(solution)/shard_map/ppermute | solution.py:510
  453.2 17.2 %collective-permute-start.31 = (bf16[32,3200]{1,0:T(8,128)(2,1)S(1)}, bf16[32,3200]{1,0:T(8,128)(2,1)S(1)}, u32[]{:S(2)}, u32[]{:S(2)}) collective-permute-start(bf16[32,3200]{1,0:T(8,128)(2,1)S(1)} %get-tuple-element.120), channel_id=1, source_target_pairs={{0,3},{1,0},{2,1},{3,2},{4,7},{5,4},{6,5},{7,6},{8,11},{9,8},{10,9... | collective-permute-start | bytes 614408 | tf_op jit(solution)/shard_map/ppermute | solution.py:510
  (39 other events, 427.9 us)
Sparse Core Ops, SparseCore 0:
  43.5 33.8 all-gather.4
  79.3 43.3 all-gather.8
  125.1 32.3 all-gather.6
  216.2 51.5 reduce-scatter.3
  305.7 45.8 reduce-scatter.5
  357.7 49.6 reduce-scatter.7
